TPU v7x, 256 devices: a whole 4x4x8 slice. The times are simulated.
256 devices in a mesh: dp: 4 (over x), expert: 64 (over z, y, core).
Axes of the slice: x: 4, y: 4, z: 8, core: 2. Of those that a mesh axis runs over, the one named last changes fastest.
Arguments:
- expert_ids: int32 [12288, 8], P(('dp', 'expert')), may hold values from 0 to 63, all different within a row; in each aligned block of 48 rows (0 to 47, 48 to 95, ...) at most 9 rows name the same one
- route_probs: float32 [12288, 8], P(('dp', 'expert')), may hold values from 0.02 to 0.5
- expert_hidden: bfloat16 [4, 64, 64, 9, 768], P('dp', 'expert'), may hold values from -6 to 6
- down_weight: bfloat16 [64, 768, 4096], P('expert', None, 'dp'), may hold values from -0.21875 to 0.21875
- out_grad: bfloat16 [12288, 4096], P(('dp', 'expert')), may hold values from -0.75 to 0.75
Outputs:
- layer_out: bfloat16 [12288, 4096], P(('dp', 'expert'))
- prob_grad: float32 [12288, 8], P(('dp', 'expert'))
- hidden_grad: bfloat16 [4, 64, 64, 9, 768], P('dp', 'expert')
- weight_grad: float32 [64, 768, 4096], P('expert', None, 'dp')
Inputs may be any that keep to these rules, and one draw needn't show every extreme that they name: `expert_ids`: each row names 8 different experts. Among the rows of one device no expert is named by more than 9 rows, and in every draw some device names some expert exactly 9 times.
All inputs are finite; a program needn't handle non-finite values.
Results may differ from a plain program's by a relative error of at most 0.0085.
Values may be sent and summed in bfloat16 or wider, within the bound.
A program may use at most 128 MiB of HBM per device.

v0:
```python
import jax
import jax.numpy as jnp
from jax import lax
from jax.sharding import PartitionSpec as P


def rounded_partial(values):
    narrow = lax.optimization_barrier(values.astype(jnp.bfloat16))
    return narrow.astype(jnp.float32)


def shards(expert_ids, route_probs, expert_hidden, down_weight, out_grad):
    tok_count, top_count = expert_ids.shape
    expert_count = lax.axis_size("expert")
    capacity = expert_hidden.shape[3]
    hidden_width = down_weight.shape[1]
    model_width = out_grad.shape[1]
    slot_count = expert_count * capacity
    flat_ids = expert_ids.reshape(-1)
    onehot = (flat_ids[:, None] == jnp.arange(expert_count, dtype=jnp.int32)[None, :]).astype(
        jnp.int32
    )
    earlier = jnp.cumsum(onehot, axis=0) - onehot
    position = jnp.sum(earlier * onehot, axis=1)
    slot_index = flat_ids * capacity + position
    slot_owner = (
        jnp.full((slot_count,), -1, dtype=jnp.int32)
        .at[slot_index]
        .set(jnp.arange(tok_count * top_count, dtype=jnp.int32))
    )
    filled = slot_owner >= 0
    safe_owner = jnp.maximum(slot_owner, 0)
    hidden_rows = expert_hidden.reshape(-1, hidden_width)
    flat_probs = route_probs.reshape(-1)
    slot_prob = jnp.where(filled, flat_probs[safe_owner], jnp.float32(0.0))
    slot_out = jnp.dot(
        hidden_rows,
        lax.all_gather(down_weight, "dp", axis=2, tiled=True)[0],
        preferred_element_type=jnp.float32,
    ).astype(jnp.bfloat16)
    returned = lax.all_to_all(
        slot_out.reshape(expert_count, capacity, model_width),
        "expert",
        split_axis=0,
        concat_axis=0,
        tiled=True,
    )
    route_out = returned.reshape(slot_count, model_width)[slot_index].reshape(
        tok_count, top_count, model_width
    )
    layer_out = jnp.einsum(
        "tk,tkd->td", route_probs, route_out, preferred_element_type=jnp.float32
    ).astype(jnp.bfloat16)
    prob_grad = jnp.einsum("td,tkd->tk", out_grad, route_out, preferred_element_type=jnp.float32)
    scaled = (slot_prob[:, None] * out_grad[safe_owner // top_count]).astype(jnp.bfloat16)
    arrived = lax.all_to_all(
        scaled.reshape(expert_count, capacity, model_width),
        "expert",
        split_axis=0,
        concat_axis=0,
        tiled=True,
    )
    arrived = arrived.reshape(-1, model_width)
    partial_value = jnp.einsum(
        "rf,rd->fd", hidden_rows, arrived, preferred_element_type=jnp.float32
    )[None]
    weight_grad = lax.psum_scatter(
        rounded_partial(partial_value).astype(jnp.bfloat16), "dp", scatter_dimension=2, tiled=True
    ).astype(jnp.float32)
    hidden_total = jnp.einsum(
        "rd,fd->rf",
        arrived,
        lax.all_gather(down_weight, "dp", axis=2, tiled=True)[0],
        preferred_element_type=jnp.float32,
    )
    hidden_grad = hidden_total.astype(jnp.bfloat16).reshape(expert_hidden.shape)
    return (layer_out, prob_grad, hidden_grad, weight_grad)


def solution(mesh):
    placed = (
        P(("dp", "expert"), None),
        P(("dp", "expert"), None),
        P("dp", "expert", None, None, None),
        P("expert", None, "dp"),
        P(("dp", "expert"), None),
    )
    return jax.shard_map(
        shards,
        mesh=mesh,
        in_specs=placed,
        out_specs=(
            P(("dp", "expert"), None),
            P(("dp", "expert"), None),
            P("dp", "expert", None, None, None),
            P("expert", None, "dp"),
        ),
        check_vma=False,
    )
```

profile of v0, /device:TPU:18, one launch (start us, length us, event | category | flops | bytes accessed | tf_op | source)
XLA Modules:
  0.0 504.3 jit_solution(4123366977165394074)
XLA Ops:
  7.2 0.8 copy.13
  8.2 0.7 broadcast_multiply_fusion
  8.9 0.9 reduce-window.6
  9.8 0.2 slice_reduce_fusion
  10.4 2.9 scatter_custom_fusion
  13.3 0.8 copy.16
  14.2 4.0 gather_fusion.1
  18.3 5.2 %gather_fusion.2 = bf16[576,4096]{1,0:T(8,128)(2,1)} fusion(bf16[48,4096]{1,0:T(8,128)(2,1)S(1)} %copy-done, s32[1024]{0:T(1024)S(1)} %get-tuple-element.14), kind=kCustom, calls=%fused_computation.2 | custom fusion | bytes 9439488 | tf_op jit(solution)/shard_map/gather | solution.py:55
  23.5 9.4 %reshape.94 = f32[64,9,4096]{2,1,0:T(8,128)} reshape(bf16[576,4096]{1,0:T(8,128)(2,1)} %gather_fusion.2) | data formatting | bytes 14155776 | tf_op jit(solution)/shard_map/convert_element_type | solution.py:55
  32.9 9.3 %multiply_convert_fusion = bf16[64,9,4096]{2,1,0:T(8,128)(2,1)} fusion(f32[64,9,4096]{2,1,0:T(8,128)} %reshape.94, f32[64,9]{1,0:T(8,128)S(1)} %mul.34), kind=kLoop, calls=%fused_computation.4 | loop fusion | flops 4718592 | bytes 14158080 | tf_op jit(solution)/shard_map/convert_element_type | solution.py:55
  42.2 12.3 %all-to-all-start.1 = ((bf16[64,9,4096]{2,1,0:T(8,128)(2,1)}), bf16[64,9,4096]{2,1,0:T(8,128)(2,1)}, u32[]{:S(2)}, u32[]{:S(2)}) async-start(bf16[64,9,4096]{2,1,0:T(8,128)(2,1)} %multiply_convert_fusion), calls=%async_computation.1 | async-start | bytes 16777216 | tf_op jit(solution)/shard_map/all_to_all | solution.py:56
  54.6 0.7 all-gather.2.cloned.1.call-update
  55.3 0.5 copy.11
  55.9 0.4 reshape.86
  56.3 184.6 %all-to-all-done.1 = bf16[64,9,4096]{2,1,0:T(8,128)(2,1)} async-done(((bf16[64,9,4096]{2,1,0:T(8,128)(2,1)}), bf16[64,9,4096]{2,1,0:T(8,128)(2,1)}, u32[]{:S(2)}, u32[]{:S(2)}) %all-to-all-start.1) | async-done | bytes 4718624 | tf_op jit(solution)/shard_map/all_to_all | solution.py:56
  241.0 8.6 %reshape.92 = bf16[576,4096]{1,0:T(8,128)(2,1)} reshape(bf16[64,9,4096]{2,1,0:T(8,128)(2,1)} %all-to-all-done.1) | data formatting | bytes 9437184 | tf_op jit(solution)/shard_map/reshape | solution.py:63
  249.6 9.4 %fusion.7 = bf16[1,768,4096]{1,2,0:T(8,128)(2,1)} fusion(bf16[576,4096]{1,0:T(8,128)(2,1)} %reshape.92, bf16[576,768]{1,0:T(8,128)(2,1)S(1)} %reshape.86), kind=kOutput, calls=%fused_computation.11 | convolution fusion | flops 3627024384 | bytes 11894784 | tf_op jit(solution)/shard_map/rf,rd->fd/dot_general | solution.py:64
  259.0 8.3 %fusion.4 = bf16[576,4096]{1,0:T(8,128)(2,1)} fusion(bf16[576,768]{1,0:T(8,128)(2,1)S(1)} %reshape.86, bf16[1,768,4096]{2,1,0:T(8,128)(2,1)} %all-gather.2.cloned.1.call-done), kind=kOutput, calls=%fused_computation.10 | convolution fusion | flops 3626237952 | bytes 11894784 | tf_op jit(solution)/shard_map/dot_general | solution.py:36
  267.3 8.4 %reshape.87 = bf16[64,9,4096]{2,1,0:T(8,128)(2,1)} reshape(bf16[576,4096]{1,0:T(8,128)(2,1)} %fusion.4) | data formatting | bytes 9437184 | tf_op jit(solution)/shard_map/reshape | solution.py:42
  275.7 6.4 %all-to-all-start = ((bf16[64,9,4096]{2,1,0:T(8,128)(2,1)}), bf16[64,9,4096]{2,1,0:T(8,128)(2,1)}, u32[]{:S(2)}, u32[]{:S(2)}) async-start(bf16[64,9,4096]{2,1,0:T(8,128)(2,1)} %reshape.87), calls=%async_computation | async-start | bytes 16777216 | tf_op jit(solution)/shard_map/all_to_all | solution.py:41
  282.1 0.7 copy.19
  282.8 8.1 %fusion.12 = bf16[576,768]{1,0:T(8,128)(2,1)S(1)} fusion(bf16[576,4096]{1,0:T(8,128)(2,1)} %reshape.92, bf16[1,768,4096]{2,1,0:T(8,128)(2,1)} %all-gather.2.cloned.1.call-done), kind=kOutput, calls=%fused_computation.16 | convolution fusion | flops 3624321024 | bytes 11894784 | tf_op jit(solution)/shard_map/rd,fd->rf/dot_general | solution.py:70
  291.0 0.4 reshape.93
  291.4 1.2 copy.17
  292.6 175.9 %all-to-all-done = bf16[64,9,4096]{2,1,0:T(8,128)(2,1)} async-done(((bf16[64,9,4096]{2,1,0:T(8,128)(2,1)}), bf16[64,9,4096]{2,1,0:T(8,128)(2,1)}, u32[]{:S(2)}, u32[]{:S(2)}) %all-to-all-start) | async-done | bytes 4718624 | tf_op jit(solution)/shard_map/all_to_all | solution.py:41
  468.5 8.4 %reshape.88 = bf16[576,4096]{1,0:T(8,128)(2,1)} reshape(bf16[64,9,4096]{2,1,0:T(8,128)(2,1)} %all-to-all-done) | data formatting | bytes 9437184 | tf_op jit(solution)/shard_map/reshape | solution.py:48
  476.9 10.5 %gather_fusion = bf16[384,4096]{1,0:T(8,128)(2,1)S(1)} fusion(bf16[576,4096]{1,0:T(8,128)(2,1)} %reshape.88, s32[1024]{0:T(1024)S(1)} %pad_clamp_fusion.2), kind=kCustom, calls=%fused_computation | custom fusion | bytes 6292992 | tf_op jit(solution)/shard_map/gather | solution.py:48
  487.4 1.7 fusion.10
  489.1 1.2 copy.28
  490.3 2.7 fusion.8
  493.0 1.4 copy.22
  494.4 3.1 copy.18
  (26 shorter events, 0.9 us)
Async XLA Ops:
  7.2 11.2 %copy-start = (bf16[48,4096]{1,0:T(8,128)(2,1)S(1)}, bf16[48,4096]{1,0:T(8,128)(2,1)}, u32[]{:S(2)}) copy-start(bf16[48,4096]{1,0:T(8,128)(2,1)} %param.9) | copy-start | bytes 1179652
  42.2 13.1 %copy-start.1 = (bf16[1,1,64,9,768]{4,2,3,1,0:T(8,128)(2,1)S(1)}, bf16[1,1,64,9,768]{4,2,3,1,0:T(8,128)(2,1)}, u32[]{:S(2)}) copy-start(bf16[1,1,64,9,768]{4,2,3,1,0:T(8,128)(2,1)} %param.7) | copy-start | bytes 2654212
  42.2 198.7 %all-to-all-start.1 = ((bf16[64,9,4096]{2,1,0:T(8,128)(2,1)}), bf16[64,9,4096]{2,1,0:T(8,128)(2,1)}, u32[]{:S(2)}, u32[]{:S(2)}) async-start(bf16[64,9,4096]{2,1,0:T(8,128)(2,1)} %multiply_convert_fusion), calls=%async_computation.1 | async-start | bytes 16777216 | tf_op jit(solution)/shard_map/all_to_all | solution.py:56
  54.6 204.5 %all-gather.2.cloned.1.call-start = ((), (), s32[]{:S(2)}) async-start(), calls=%async_computation.3 | async-start | bytes 7864320 | tf_op jit(solution)/shard_map/all_gather | solution.py:38
  55.3 439.1 %reduce-scatter.2.cloned.1.call-start = ((), (), s32[]{:S(2)}) async-start(), calls=%async_computation.4 | async-start | bytes 7864320 | tf_op jit(solution)/shard_map/reduce_scatter | solution.py:67
  275.7 6.4 %copy-start.2 = (f32[48,8]{0,1:T(8,128)S(1)}, f32[48,8]{0,1:T(8,128)}, u32[]{:S(2)}) copy-start(f32[48,8]{0,1:T(8,128)} %param.6) | copy-start | bytes 4612
  275.7 192.8 %all-to-all-start = ((bf16[64,9,4096]{2,1,0:T(8,128)(2,1)}), bf16[64,9,4096]{2,1,0:T(8,128)(2,1)}, u32[]{:S(2)}, u32[]{:S(2)}) async-start(bf16[64,9,4096]{2,1,0:T(8,128)(2,1)} %reshape.87), calls=%async_computation | async-start | bytes 16777216 | tf_op jit(solution)/shard_map/all_to_all | solution.py:41
Sparse Core Ops, SparseCore 0:
  57.2 68.9 all-gather.1
  259.1 62.0 reduce-scatter.1
where the time goes:
time: 506 us; the launch traced here: 504 us
  waiting for transfers between devices  361 us (71%)
  local copies, waits for them, and re-layouts  68.6 us (14%)
  matrix products  30.3 us (6%)
  starting transfers between devices  18.8 us (4%)
  between operations  14.2 us (3%)
  other arithmetic  11.1 us (2%)
    all_to_all x1, waiting for transfers between devices, shards(): lax.all_to_all(scaled.reshape(expert_count, capacity, model_width), 'expe...  185 us
    all_to_all x1, waiting for transfers between devices, shards(): lax.all_to_all(slot_out.reshape(expert_count, capacity, model_width), 'ex...  176 us
    all_to_all x1, starting transfers between devices, shards(): lax.all_to_all(scaled.reshape(expert_count, capacity, model_width), 'expe...  12.3 us
    gather x1, local copies, waits for them, and re-layouts, shards(): returned.reshape(slot_count, model_width)[slot_index]  10.5 us
  transfers between devices with their start and end apart: 4, of which 2 were waited for; matrix products, arithmetic and copies ran while one was open for 14% of the time, Pallas kernels for 0%

commit v1 on v0

--- a/solution.py
+++ b/solution.py
@@ -39,7 +39,7 @@
         preferred_element_type=jnp.float32,
     ).astype(jnp.bfloat16)
     returned = lax.all_to_all(
-        slot_out.reshape(expert_count, capacity, model_width),
+        slot_out.reshape(expert_count, capacity, model_width // 128, 128),
         "expert",
         split_axis=0,
         concat_axis=0,
@@ -54,7 +54,7 @@
     prob_grad = jnp.einsum("td,tkd->tk", out_grad, route_out, preferred_element_type=jnp.float32)
     scaled = (slot_prob[:, None] * out_grad[safe_owner // top_count]).astype(jnp.bfloat16)
     arrived = lax.all_to_all(
-        scaled.reshape(expert_count, capacity, model_width),
+        scaled.reshape(expert_count, capacity, model_width // 128, 128),
         "expert",
         split_axis=0,
         concat_axis=0,

time: 506 us -> 332 us (0.66)
  waiting for transfers between devices: 361 us -> 203 us
  local copies, waits for them, and re-layouts: 68.6 us -> 49.1 us
  matrix products: 30.3 us -> 38.3 us
    all_to_all x2, waiting for transfers between devices: 361 us -> 202 us  [the longest x1 105 us: shards(): lax.all_to_all(scaled.reshape(expert_count, capacity, model_width // 128,...]
    reshape x3 -> x0, local copies, waits for them, and re-layouts: 25.4 us -> none  [the longest x1 8.59 us: shards(): arrived = arrived.reshape(-1, model_width)]
    unnamed x12 -> x15, local copies, waits for them, and re-layouts: 7.11 us -> 22.1 us
    convert_element_type x1 -> x0, local copies, waits for them, and re-layouts: 9.39 us -> none  [shards(): slot_prob[:, None] * out_grad[safe_owner // top_count]]
    dot_general x1, matrix products: 9.42 us -> 18.4 us  [shards(): jnp.einsum('rf,rd->fd', hidden_rows, arrived, preferred_element_type=jnp....]
    convert_element_type x1, other arithmetic: 9.32 us -> 2.59 us  [shards(): (slot_prob[:, None] * out_grad[safe_owner // top_count]).astype(jnp.bfloa...]
  transfers between devices with their start and end apart: 4 -> 4, of which waited for: 2 -> 2; matrix products, arithmetic and copies ran while one was open for 14% -> 20% of each run, Pallas kernels for 0% -> 0%
where the time goes in v1:
time: 332 us; the launch traced here: 331 us
  waiting for transfers between devices  203 us (61%)
  local copies, waits for them, and re-layouts  49.1 us (15%)
  matrix products  38.3 us (12%)
  starting transfers between devices  18.5 us (6%)
  between operations  14.2 us (4%)
  other arithmetic  7.98 us (2%)
    all_to_all x1, waiting for transfers between devices, shards(): lax.all_to_all(scaled.reshape(expert_count, capacity, model_width // 128,...  105 us
    all_to_all x1, waiting for transfers between devices, shards(): lax.all_to_all(slot_out.reshape(expert_count, capacity, model_width // 12...  96.5 us
    unnamed x15, local copies, waits for them, and re-layouts  22.1 us
    dot_general x1, matrix products, shards(): jnp.einsum('rf,rd->fd', hidden_rows, arrived, preferred_element_type=jnp....  18.4 us
    all_to_all x1, starting transfers between devices, shards(): lax.all_to_all(scaled.reshape(expert_count, capacity, model_width // 128,...  12.3 us
    gather x1, local copies, waits for them, and re-layouts, shards(): returned.reshape(slot_count, model_width)[slot_index]  10.7 us
    dot_general x1, matrix products, shards(): jnp.einsum('rd,fd->rf', arrived, lax.all_gather(down_weight, 'dp', axis=2...  8.59 us
    dot_general x1, matrix products, shards(): jnp.dot(hidden_rows, lax.all_gather(down_weight, 'dp', axis=2, tiled=True...  6.87 us
  transfers between devices with their start and end apart: 4, of which 2 were waited for; matrix products, arithmetic and copies ran while one was open for 20% of the time, Pallas kernels for 0%

profile of v1, /device:TPU:18, one launch (start us, length us, event | category | flops | bytes accessed | tf_op | source)
XLA Modules:
  0.0 330.7 jit_solution(6433251341222709527)
XLA Ops:
  7.2 0.8 copy.13
  8.2 0.7 broadcast_multiply_fusion
  8.9 0.9 reduce-window.6
  9.8 0.2 slice_reduce_fusion
  10.4 2.9 scatter_custom_fusion
  13.3 0.8 copy.16
  14.2 4.0 %gather_fusion.1 = f32[576]{0:T(1024)S(1)} fusion(f32[384]{0:T(512)S(1)} %reshape.91, s32[1024]{0:T(1024)S(1)} %get-tuple-element.15), kind=kCustom, calls=%fused_computation.1 | custom fusion | bytes 6912 | tf_op jit(solution)/shard_map/gather | solution.py:35
  18.3 5.2 %gather_fusion.2 = bf16[576,4096]{1,0:T(8,128)(2,1)} fusion(bf16[48,4096]{1,0:T(8,128)(2,1)S(1)} %copy-done, s32[1024]{0:T(1024)S(1)} %get-tuple-element.14), kind=kCustom, calls=%fused_computation.2 | custom fusion | bytes 9439488 | tf_op jit(solution)/shard_map/gather | solution.py:55
  23.5 3.6 %convert_bitcast_fusion = f32[72,8,32,128]{3,1,2,0:T(8,128)S(1)} fusion(bf16[576,4096]{1,0:T(8,128)(2,1)} %gather_fusion.2), kind=kLoop, calls=%fused_computation.4 | loop fusion | flops 2359296 | bytes 14155776
  27.1 2.1 copy.26
  29.2 2.6 multiply_convert_fusion
  31.8 12.3 %all-to-all-start.1 = ((bf16[64,9,32,128]{3,2,1,0:T(8,128)(2,1)}), bf16[64,9,32,128]{3,2,1,0:T(8,128)(2,1)}, u32[]{:S(2)}, u32[]{:S(2)}) async-start(bf16[64,9,32,128]{3,2,1,0:T(8,128)(2,1)} %multiply_convert_fusion), calls=%async_computation.1 | async-start | bytes 9437184 | tf_op jit(solution)/shard_map/all_to_all | solution.py:56
  44.2 0.7 all-gather.2.cloned.1.call-update
  45.1 0.5 copy.11
  45.6 0.4 reshape.86
  46.1 105.4 %all-to-all-done.1 = bf16[64,9,32,128]{3,2,1,0:T(8,128)(2,1)} async-done(((bf16[64,9,32,128]{3,2,1,0:T(8,128)(2,1)}), bf16[64,9,32,128]{3,2,1,0:T(8,128)(2,1)}, u32[]{:S(2)}, u32[]{:S(2)}) %all-to-all-start.1) | async-done | bytes 4718624 | tf_op jit(solution)/shard_map/all_to_all | solution.py:56
  151.5 18.4 %fusion.7 = bf16[1,768,4096]{1,2,0:T(8,128)(2,1)} fusion(bf16[576,768]{1,0:T(8,128)(2,1)S(1)} %reshape.86, bf16[72,8,32,128]{3,2,1,0:T(8,128)(2,1)} %bitcast.22), kind=kOutput, calls=%fused_computation.12 | convolution fusion | flops 3627024384 | bytes 11894784 | tf_op jit(solution)/shard_map/rf,rd->fd/dot_general | solution.py:64
  169.9 6.9 %fusion.16 = bf16[72,8,32,128]{3,1,2,0:T(8,128)(2,1)S(1)} fusion(bf16[576,768]{1,0:T(8,128)(2,1)S(1)} %reshape.86, bf16[1,768,4096]{2,1,0:T(8,128)(2,1)} %all-gather.2.cloned.1.call-done), kind=kOutput, calls=%fused_computation.22 | convolution fusion | flops 3626237952 | bytes 11894784 | tf_op jit(solution)/shard_map/dot_general | solution.py:36
  176.8 3.6 %copy.24 = bf16[72,8,32,128]{3,2,1,0:T(8,128)(2,1)} copy(bf16[72,8,32,128]{3,1,2,0:T(8,128)(2,1)S(1)} %fusion.16) | data formatting | bytes 9437184
  180.4 5.9 %all-to-all-start = ((bf16[64,9,32,128]{3,2,1,0:T(8,128)(2,1)}), bf16[64,9,32,128]{3,2,1,0:T(8,128)(2,1)}, u32[]{:S(2)}, u32[]{:S(2)}) async-start(bf16[64,9,32,128]{3,2,1,0:T(8,128)(2,1)} %bitcast.74), calls=%async_computation | async-start | bytes 9437184 | tf_op jit(solution)/shard_map/all_to_all | solution.py:41
  186.4 0.7 copy.19
  187.1 8.6 %fusion.19 = bf16[576,768]{1,0:T(8,128)(2,1)S(1)} fusion(bf16[1,768,4096]{2,1,0:T(8,128)(2,1)} %all-gather.2.cloned.1.call-done, bf16[72,8,32,128]{3,2,1,0:T(8,128)(2,1)} %bitcast.22), kind=kOutput, calls=%fused_computation.23 | convolution fusion | flops 3624321024 | bytes 11894784 | tf_op jit(solution)/shard_map/rd,fd->rf/dot_general | solution.py:70
  195.7 0.4 reshape.93
  196.1 1.2 copy.17
  197.3 96.5 %all-to-all-done = bf16[64,9,32,128]{3,2,1,0:T(8,128)(2,1)} async-done(((bf16[64,9,32,128]{3,2,1,0:T(8,128)(2,1)}), bf16[64,9,32,128]{3,2,1,0:T(8,128)(2,1)}, u32[]{:S(2)}, u32[]{:S(2)}) %all-to-all-start) | async-done | bytes 4718624 | tf_op jit(solution)/shard_map/all_to_all | solution.py:41
  293.8 9.3 %copy.43 = bf16[72,8,32,128]{3,1,2,0:T(8,128)(2,1)} copy(bf16[72,8,32,128]{3,2,1,0:T(8,128)(2,1)} %bitcast.16) | data formatting | bytes 9437184
  303.0 10.7 %gather_fusion = bf16[384,4096]{1,0:T(8,128)(2,1)S(1)} fusion(bf16[576,4096]{1,0:T(8,128)(2,1)} %bitcast.72, s32[1024]{0:T(1024)S(1)} %pad_clamp_fusion.2), kind=kCustom, calls=%fused_computation | custom fusion | bytes 6292992 | tf_op jit(solution)/shard_map/gather | solution.py:48
  313.8 1.7 fusion.14
  315.5 1.2 copy.44
  316.6 2.7 fusion.12
  319.4 1.4 copy.22
  320.8 3.1 copy.18
  (26 shorter events, 1.1 us)
Async XLA Ops:
  7.2 11.2 %copy-start = (bf16[48,4096]{1,0:T(8,128)(2,1)S(1)}, bf16[48,4096]{1,0:T(8,128)(2,1)}, u32[]{:S(2)}) copy-start(bf16[48,4096]{1,0:T(8,128)(2,1)} %param.9) | copy-start | bytes 1179652
  31.8 13.3 %copy-start.1 = (bf16[1,1,64,9,768]{4,2,3,1,0:T(8,128)(2,1)S(1)}, bf16[1,1,64,9,768]{4,2,3,1,0:T(8,128)(2,1)}, u32[]{:S(2)}) copy-start(bf16[1,1,64,9,768]{4,2,3,1,0:T(8,128)(2,1)} %param.7) | copy-start | bytes 2654212
  31.8 119.7 %all-to-all-start.1 = ((bf16[64,9,32,128]{3,2,1,0:T(8,128)(2,1)}), bf16[64,9,32,128]{3,2,1,0:T(8,128)(2,1)}, u32[]{:S(2)}, u32[]{:S(2)}) async-start(bf16[64,9,32,128]{3,2,1,0:T(8,128)(2,1)} %multiply_convert_fusion), calls=%async_computation.1 | async-start | bytes 9437184 | tf_op jit(solution)/shard_map/all_to_all | solution.py:56
  44.1 125.8 %all-gather.2.cloned.1.call-start = ((), (), s32[]{:S(2)}) async-start(), calls=%async_computation.3 | async-start | bytes 7864320 | tf_op jit(solution)/shard_map/all_gather | solution.py:38
  44.8 275.9 %reduce-scatter.2.cloned.1.call-start = ((), (), s32[]{:S(2)}) async-start(), calls=%async_computation.4 | async-start | bytes 7864320 | tf_op jit(solution)/shard_map/reduce_scatter | solution.py:67
  180.4 5.9 %copy-start.2 = (f32[48,8]{0,1:T(8,128)S(1)}, f32[48,8]{0,1:T(8,128)}, u32[]{:S(2)}) copy-start(f32[48,8]{0,1:T(8,128)} %param.6) | copy-start | bytes 4612
  180.4 113.3 %all-to-all-start = ((bf16[64,9,32,128]{3,2,1,0:T(8,128)(2,1)}), bf16[64,9,32,128]{3,2,1,0:T(8,128)(2,1)}, u32[]{:S(2)}, u32[]{:S(2)}) async-start(bf16[64,9,32,128]{3,2,1,0:T(8,128)(2,1)} %bitcast.74), calls=%async_computation | async-start | bytes 9437184 | tf_op jit(solution)/shard_map/all_to_all | solution.py:41
Sparse Core Ops, SparseCore 0:
  46.8 68.9 all-gather.1
  170.0 61.4 reduce-scatter.1

commit v2 on v1

--- a/solution.py
+++ b/solution.py
@@ -1,7 +1,87 @@
+import functools
+
 import jax
 import jax.numpy as jnp
 from jax import lax
+from jax.experimental import pallas as pl
+from jax.experimental.pallas import tpu as pltpu
 from jax.sharding import PartitionSpec as P
+
+MESH = pl.DeviceIdType.MESH
+
+
+def exchange_kernel(n, fwd_in, bwd_in, fwd_out, bwd_out, send_sem, recv_sem, own_sem):
+    me = lax.axis_index("expert")
+    row = lax.axis_index("dp")
+    pairs = ((fwd_in, fwd_out), (bwd_in, bwd_out))
+
+    barrier = pltpu.get_barrier_semaphore()
+
+    def greet(i, carry):
+        peer = lax.rem(me + i, n)
+        pl.semaphore_signal(barrier, inc=1, device_id=(row, peer), device_id_type=MESH)
+        return carry
+
+    lax.fori_loop(1, n, greet, 0)
+    pl.semaphore_wait(barrier, n - 1)
+
+    own = [
+        pltpu.make_async_copy(src.at[me], dst.at[me], own_sem.at[a])
+        for a, (src, dst) in enumerate(pairs)
+    ]
+    for copy in own:
+        copy.start()
+
+    def remote(a, peer, source):
+        src, dst = pairs[a]
+        return pltpu.make_async_remote_copy(
+            src_ref=src.at[peer],
+            dst_ref=dst.at[source],
+            send_sem=send_sem.at[a, peer],
+            recv_sem=recv_sem.at[a, source],
+            device_id=(row, peer),
+            device_id_type=MESH,
+        )
+
+    def start(i, carry):
+        peer = lax.rem(me + i, n)
+        for a in range(2):
+            remote(a, peer, me).start()
+        return carry
+
+    lax.fori_loop(1, n, start, 0)
+
+    def finish(i, carry):
+        peer = lax.rem(me + i, n)
+        source = lax.rem(me + n - i, n)
+        for a in range(2):
+            remote(a, peer, me).wait_send()
+            remote(a, source, source).wait_recv()
+        return carry
+
+    lax.fori_loop(1, n, finish, 0)
+    for copy in own:
+        copy.wait()
+
+
+def exchange(fwd, bwd):
+    n = lax.axis_size("expert")
+    any_spec = pl.BlockSpec(memory_space=pl.ANY)
+    return pl.pallas_call(
+        functools.partial(exchange_kernel, n),
+        out_shape=(
+            jax.ShapeDtypeStruct(fwd.shape, fwd.dtype),
+            jax.ShapeDtypeStruct(bwd.shape, bwd.dtype),
+        ),
+        in_specs=[any_spec, any_spec],
+        out_specs=(any_spec, any_spec),
+        scratch_shapes=[
+            pltpu.SemaphoreType.DMA((2, n)),
+            pltpu.SemaphoreType.DMA((2, n)),
+            pltpu.SemaphoreType.DMA((2,)),
+        ],
+        compiler_params=pltpu.CompilerParams(collective_id=0, has_side_effects=True),
+    )(fwd, bwd)
 
 
 def rounded_partial(values):
@@ -38,12 +118,10 @@
         lax.all_gather(down_weight, "dp", axis=2, tiled=True)[0],
         preferred_element_type=jnp.float32,
     ).astype(jnp.bfloat16)
-    returned = lax.all_to_all(
+    scaled = (slot_prob[:, None] * out_grad[safe_owner // top_count]).astype(jnp.bfloat16)
+    returned, arrived = exchange(
         slot_out.reshape(expert_count, capacity, model_width // 128, 128),
-        "expert",
-        split_axis=0,
-        concat_axis=0,
-        tiled=True,
+        scaled.reshape(expert_count, capacity, model_width // 128, 128),
     )
     route_out = returned.reshape(slot_count, model_width)[slot_index].reshape(
         tok_count, top_count, model_width
@@ -52,14 +130,6 @@
         "tk,tkd->td", route_probs, route_out, preferred_element_type=jnp.float32
     ).astype(jnp.bfloat16)
     prob_grad = jnp.einsum("td,tkd->tk", out_grad, route_out, preferred_element_type=jnp.float32)
-    scaled = (slot_prob[:, None] * out_grad[safe_owner // top_count]).astype(jnp.bfloat16)
-    arrived = lax.all_to_all(
-        scaled.reshape(expert_count, capacity, model_width // 128, 128),
-        "expert",
-        split_axis=0,
-        concat_axis=0,
-        tiled=True,
-    )
     arrived = arrived.reshape(-1, model_width)
     partial_value = jnp.einsum(
         "rf,rd->fd", hidden_rows, arrived, preferred_element_type=jnp.float32

time: 332 us -> 458 us (1.38)
  Pallas kernels: 0 us -> 231 us
  waiting for transfers between devices: 203 us -> 106 us
  starting transfers between devices: 18.5 us -> 0.08 us
    pallas_call x0 -> x1, Pallas kernels: none -> 231 us  [exchange(): pl.pallas_call(functools.partial(exchange_kernel, n), out_shape=(jax.Shap...]
    all_to_all x2 -> x0, waiting for transfers between devices: 202 us -> none  [the longest x1 105 us: shards(): lax.all_to_all(scaled.reshape(expert_count, capacity, model_width // 128,...]
    reduce_scatter x1, waiting for transfers between devices: 0.01 us -> 65.3 us  [shards(): lax.psum_scatter(rounded_partial(partial_value).astype(jnp.bfloat16), 'dp...]
    all_gather x1, waiting for transfers between devices: 0.02 us -> 39.8 us  [shards(): lax.all_gather(down_weight, 'dp', axis=2, tiled=True)[0]]
    all_to_all x2 -> x0, starting transfers between devices: 18.2 us -> none  [the longest x1 12.3 us: shards(): lax.all_to_all(scaled.reshape(expert_count, capacity, model_width // 128,...]
  transfers between devices with their start and end apart: 4 -> 2, of which waited for: 2 -> 2; matrix products, arithmetic and copies ran while one was open for 20% -> 15% of each run, Pallas kernels for 0% -> 0%
where the time goes in v2:
time: 458 us; the launch traced here: 455 us
  Pallas kernels  231 us (50%)
  waiting for transfers between devices  106 us (23%)
  local copies, waits for them, and re-layouts  53.2 us (12%)
  matrix products  38.3 us (8%)
  between operations  14.2 us (3%)
  other arithmetic  11.7 us (3%)
    pallas_call x1, Pallas kernels, exchange(): pl.pallas_call(functools.partial(exchange_kernel, n), out_shape=(jax.Shap...  231 us
    reduce_scatter x1, waiting for transfers between devices, shards(): lax.psum_scatter(rounded_partial(partial_value).astype(jnp.bfloat16), 'dp...  65.3 us
    all_gather x1, waiting for transfers between devices, shards(): lax.all_gather(down_weight, 'dp', axis=2, tiled=True)[0]  39.8 us
    unnamed x15, local copies, waits for them, and re-layouts  26.3 us
    dot_general x1, matrix products, shards(): jnp.einsum('rf,rd->fd', hidden_rows, arrived, preferred_element_type=jnp....  18.6 us
    gather x1, local copies, waits for them, and re-layouts, shards(): returned.reshape(slot_count, model_width)[slot_index]  10.7 us
  transfers between devices with their start and end apart: 2, of which 2 were waited for; matrix products, arithmetic and copies ran while one was open for 15% of the time, Pallas kernels for 0%

profile of v2, /device:TPU:18, one launch (start us, length us, event | category | flops | bytes accessed | tf_op | source)
XLA Modules:
  0.0 454.7 jit_solution(5141377236067713287)
XLA Ops:
  7.2 0.7 all-gather.2.cloned.1.call-update
  8.0 0.8 copy.13
  8.9 0.9 reduce-window.6
  9.8 0.2 slice_reduce_fusion
  10.1 0.7 broadcast_multiply_fusion
  11.0 0.8 copy.16
  12.0 2.9 scatter_custom_fusion
  14.9 4.0 gather_fusion
  19.1 5.2 %gather_fusion.1 = bf16[576,4096]{1,0:T(8,128)(2,1)} fusion(bf16[48,4096]{1,0:T(8,128)(2,1)S(1)} %copy-done, s32[1024]{0:T(1024)S(1)} %get-tuple-element.18), kind=kCustom, calls=%fused_computation.1 | custom fusion | bytes 9439488 | tf_op jit(solution)/shard_map/gather | solution.py:121
  24.3 4.2 convert_bitcast_fusion
  28.5 5.6 %copy.25 = f32[72,8,32,128]{3,2,1,0:T(8,128)} copy(f32[72,8,32,128]{3,1,2,0:T(8,128)S(1)} %convert_bitcast_fusion) | data formatting | bytes 18874368
  34.1 0.5 copy.11
  34.6 0.4 reshape.86
  35.1 5.7 %multiply_convert_fusion.bwd_in = bf16[64,9,32,128]{3,2,1,0:T(8,128)(2,1)} fusion(f32[64,9,32,128]{3,2,1,0:T(8,128)} %bitcast.73, f32[64,9]{1,0:T(8,128)S(1)} %mul.34), kind=kLoop, calls=%fused_computation.5 | loop fusion | flops 4718592 | bytes 14158080 | tf_op jit(solution)/shard_map/convert_element_type | solution.py:121
  40.8 39.8 %all-gather.2.cloned.1.call-done = bf16[1,768,4096]{2,1,0:T(8,128)(2,1)} async-done(((bf16[1,768,1024]{2,1,0:T(8,128)(2,1)}), bf16[1,768,4096]{2,1,0:T(8,128)(2,1)}) %all-gather.2.cloned.1.call-update) | async-done | bytes 6291472 | tf_op jit(solution)/shard_map/all_gather | solution.py:118
  80.5 6.8 %fusion.16 = bf16[72,8,32,128]{3,1,2,0:T(8,128)(2,1)S(1)} fusion(bf16[576,768]{1,0:T(8,128)(2,1)S(1)} %reshape.86, bf16[1,768,4096]{2,1,0:T(8,128)(2,1)} %all-gather.2.cloned.1.call-done), kind=kOutput, calls=%fused_computation.22 | convolution fusion | flops 3626237952 | bytes 11894784 | tf_op jit(solution)/shard_map/dot_general | solution.py:116
  87.4 3.6 copy.24
  91.0 231.5 %shard_map.84 = (bf16[64,9,32,128]{3,2,1,0:T(8,128)(2,1)}, bf16[64,9,32,128]{3,2,1,0:T(8,128)(2,1)}) custom-call(bf16[64,9,32,128]{3,2,1,0:T(8,128)(2,1)} %bitcast.74, bf16[64,9,32,128]{3,2,1,0:T(8,128)(2,1)} %multiply_convert_fusion.bwd_in), custom_call_target="tpu_custom_call" | custom-call | tf_op jit(solution)/shard_map/pallas_call | solution.py:70
  322.5 18.6 %fusion.7 = bf16[1,768,4096]{1,2,0:T(8,128)(2,1)} fusion(bf16[576,768]{1,0:T(8,128)(2,1)S(1)} %reshape.86, bf16[72,8,32,128]{3,2,1,0:T(8,128)(2,1)} %bitcast.80), kind=kOutput, calls=%fused_computation.12 | convolution fusion | flops 3627024384 | bytes 11894784 | tf_op jit(solution)/shard_map/rf,rd->fd/dot_general | solution.py:134
  341.1 0.7 copy-done.2
  341.8 0.7 copy.19
  342.5 9.3 %copy.43 = bf16[72,8,32,128]{3,1,2,0:T(8,128)(2,1)} copy(bf16[72,8,32,128]{3,2,1,0:T(8,128)(2,1)} %bitcast.75) | data formatting | bytes 9437184
  351.8 10.7 %gather_fusion.2 = bf16[384,4096]{1,0:T(8,128)(2,1)S(1)} fusion(bf16[576,4096]{1,0:T(8,128)(2,1)} %bitcast.72, s32[1024]{0:T(1024)S(1)} %pad_clamp_fusion), kind=kCustom, calls=%fused_computation.2 | custom fusion | bytes 6292992 | tf_op jit(solution)/shard_map/gather | solution.py:126
  362.4 1.7 fusion.14
  364.1 1.2 copy.44
  365.3 2.7 fusion.12
  368.1 1.4 copy.22
  369.5 8.5 %fusion.19 = bf16[576,768]{1,0:T(8,128)(2,1)S(1)} fusion(bf16[1,768,4096]{2,1,0:T(8,128)(2,1)} %all-gather.2.cloned.1.call-done, bf16[72,8,32,128]{3,2,1,0:T(8,128)(2,1)} %bitcast.81), kind=kOutput, calls=%fused_computation.23 | convolution fusion | flops 3624321024 | bytes 11894784 | tf_op jit(solution)/shard_map/rd,fd->rf/dot_general | solution.py:140
  377.9 0.4 reshape.93
  378.3 1.2 copy.17
  379.5 65.3 %reduce-scatter.2.cloned.1.call-done = bf16[1,768,1024]{1,2,0:T(8,128)(2,1)} async-done(((bf16[1,768,4096]{1,2,0:T(8,128)(2,1)}), bf16[1,768,1024]{1,2,0:T(8,128)(2,1)}) %reduce-scatter.2.cloned.1.call-update) | async-done | bytes 1572880 | tf_op jit(solution)/shard_map/reduce_scatter | solution.py:137
  444.8 3.1 copy.18
  (23 shorter events, 0.9 us)
Async XLA Ops:
  7.2 11.9 %copy-start = (bf16[48,4096]{1,0:T(8,128)(2,1)S(1)}, bf16[48,4096]{1,0:T(8,128)(2,1)}, u32[]{:S(2)}) copy-start(bf16[48,4096]{1,0:T(8,128)(2,1)} %param.9) | copy-start | bytes 1179652
  7.2 73.4 %all-gather.2.cloned.1.call-start = ((), (), s32[]{:S(2)}) async-start(), calls=%async_computation.1 | async-start | bytes 7864320 | tf_op jit(solution)/shard_map/all_gather | solution.py:118
  7.9 436.9 %reduce-scatter.2.cloned.1.call-start = ((), (), s32[]{:S(2)}) async-start(), calls=%async_computation.2 | async-start | bytes 7864320 | tf_op jit(solution)/shard_map/reduce_scatter | solution.py:137
  28.5 5.6 %copy-start.1 = (bf16[1,1,64,9,768]{4,2,3,1,0:T(8,128)(2,1)S(1)}, bf16[1,1,64,9,768]{4,2,3,1,0:T(8,128)(2,1)}, u32[]{:S(2)}) copy-start(bf16[1,1,64,9,768]{4,2,3,1,0:T(8,128)(2,1)} %param.7) | copy-start | bytes 2654212
  341.1 0.7 copy-start.2
Sparse Core Ops, SparseCore 0:
  9.8 70.6 all-gather.1
  341.2 103.5 reduce-scatter.1

commit v3 on v2

v3 whole, which is shorter than its diff:
```python
import functools

import jax
import jax.numpy as jnp
from jax import lax
from jax.experimental import pallas as pl
from jax.experimental.pallas import tpu as pltpu
from jax.sharding import PartitionSpec as P

MESH = pl.DeviceIdType.MESH


def exchange_kernel(n, src, dst, send_sem, recv_sem, own_sem):
    me = lax.axis_index("expert")
    row = lax.axis_index("dp")

    barrier = pltpu.get_barrier_semaphore()

    def greet(i, carry):
        peer = lax.rem(me + i, n)
        pl.semaphore_signal(barrier, inc=1, device_id=(row, peer), device_id_type=MESH)
        return carry

    lax.fori_loop(1, n, greet, 0)
    pl.semaphore_wait(barrier, n - 1)

    own = pltpu.make_async_copy(src.at[me], dst.at[me], own_sem)
    own.start()

    def remote(peer, source):
        return pltpu.make_async_remote_copy(
            src_ref=src.at[peer],
            dst_ref=dst.at[source],
            send_sem=send_sem.at[peer],
            recv_sem=recv_sem.at[source],
            device_id=(row, peer),
            device_id_type=MESH,
        )

    def start(i, carry):
        remote(lax.rem(me + i, n), me).start()
        return carry

    lax.fori_loop(1, n, start, 0)

    def finish(i, carry):
        source = lax.rem(me + n - i, n)
        remote(lax.rem(me + i, n), me).wait_send()
        remote(source, source).wait_recv()
        return carry

    lax.fori_loop(1, n, finish, 0)
    own.wait()


def exchange(x, collective):
    n = lax.axis_size("expert")
    any_spec = pl.BlockSpec(memory_space=pl.ANY)
    return pl.pallas_call(
        functools.partial(exchange_kernel, n),
        out_shape=jax.ShapeDtypeStruct(x.shape, x.dtype),
        in_specs=[any_spec],
        out_specs=any_spec,
        scratch_shapes=[
            pltpu.SemaphoreType.DMA((n,)),
            pltpu.SemaphoreType.DMA((n,)),
            pltpu.SemaphoreType.DMA(()),
        ],
        compiler_params=pltpu.CompilerParams(collective_id=collective, has_side_effects=True),
    )(x)


def shards(expert_ids, route_probs, expert_hidden, down_weight, out_grad):
    tok_count, top_count = expert_ids.shape
    expert_count = lax.axis_size("expert")
    capacity = expert_hidden.shape[3]
    hidden_width = down_weight.shape[1]
    model_width = out_grad.shape[1]
    slot_count = expert_count * capacity
    flat_ids = expert_ids.reshape(-1)
    onehot = (flat_ids[:, None] == jnp.arange(expert_count, dtype=jnp.int32)[None, :]).astype(
        jnp.int32
    )
    earlier = jnp.cumsum(onehot, axis=0) - onehot
    position = jnp.sum(earlier * onehot, axis=1)
    slot_index = flat_ids * capacity + position
    slot_owner = (
        jnp.full((slot_count,), -1, dtype=jnp.int32)
        .at[slot_index]
        .set(jnp.arange(tok_count * top_count, dtype=jnp.int32))
    )
    filled = slot_owner >= 0
    safe_owner = jnp.maximum(slot_owner, 0)
    hidden_rows = expert_hidden.reshape(-1, hidden_width)
    flat_probs = route_probs.reshape(-1)
    slot_prob = jnp.where(filled, flat_probs[safe_owner], jnp.float32(0.0))
    scaled = (slot_prob[:, None] * out_grad[safe_owner // top_count]).astype(jnp.bfloat16)
    arrived = exchange(scaled.reshape(expert_count, capacity, model_width // 128, 128), 0)
    gathered_weight = lax.all_gather(down_weight, "dp", axis=2, tiled=True)[0]
    slot_out = jnp.dot(
        hidden_rows, gathered_weight, preferred_element_type=jnp.float32
    ).astype(jnp.bfloat16)
    arrived = arrived.reshape(-1, model_width)
    partial_value = jnp.einsum(
        "rf,rd->fd", hidden_rows, arrived, preferred_element_type=jnp.float32
    )[None]
    slot_out, narrow = lax.optimization_barrier((slot_out, partial_value.astype(jnp.bfloat16)))
    weight_grad = lax.psum_scatter(narrow, "dp", scatter_dimension=2, tiled=True).astype(
        jnp.float32
    )
    returned = exchange(slot_out.reshape(expert_count, capacity, model_width // 128, 128), 1)
    route_out = returned.reshape(slot_count, model_width)[slot_index].reshape(
        tok_count, top_count, model_width
    )
    layer_out = jnp.einsum(
        "tk,tkd->td", route_probs, route_out, preferred_element_type=jnp.float32
    ).astype(jnp.bfloat16)
    prob_grad = jnp.einsum("td,tkd->tk", out_grad, route_out, preferred_element_type=jnp.float32)
    hidden_total = jnp.einsum(
        "rd,fd->rf",
        arrived,
        gathered_weight,
        preferred_element_type=jnp.float32,
    )
    hidden_grad = hidden_total.astype(jnp.bfloat16).reshape(expert_hidden.shape)
    return (layer_out, prob_grad, hidden_grad, weight_grad)


def solution(mesh):
    placed = (
        P(("dp", "expert"), None),
        P(("dp", "expert"), None),
        P("dp", "expert", None, None, None),
        P("expert", None, "dp"),
        P(("dp", "expert"), None),
    )
    return jax.shard_map(
        shards,
        mesh=mesh,
        in_specs=placed,
        out_specs=(
            P(("dp", "expert"), None),
            P(("dp", "expert"), None),
            P("dp", "expert", None, None, None),
            P("expert", None, "dp"),
        ),
        check_vma=False,
    )
```

time: 458 us -> 374 us (0.82)
  waiting for transfers between devices: 106 us -> 0.7 us
  Pallas kernels: 231 us -> 252 us
    reduce_scatter x1, waiting for transfers between devices: 65.3 us -> 0.01 us  [shards(): lax.psum_scatter(narrow, 'dp', scatter_dimension=2, tiled=True)]
    all_gather x1, waiting for transfers between devices: 39.8 us -> 0.01 us  [shards(): gathered_weight = lax.all_gather(down_weight, 'dp', axis=2, tiled=True)[0]]
    pallas_call x1 -> x2, Pallas kernels: 231 us -> 252 us  [exchange(): pl.pallas_call(functools.partial(exchange_kernel, n), out_shape=jax.Shape...]
    unnamed x15 -> x17, local copies, waits for them, and re-layouts: 26.3 us -> 25 us
  transfers between devices with their start and end apart: 2 -> 2, of which waited for: 2 -> 0; matrix products, arithmetic and copies ran while one was open for 15% -> 24% of each run, Pallas kernels for 0% -> 69%
where the time goes in v3:
time: 374 us; the launch traced here: 368 us
  Pallas kernels  252 us (67%)
  local copies, waits for them, and re-layouts  52.7 us (14%)
  matrix products  39.6 us (11%)
  between operations  14.2 us (4%)
  other arithmetic  8.45 us (2%)
    pallas_call x2, Pallas kernels, exchange(): pl.pallas_call(functools.partial(exchange_kernel, n), out_shape=jax.Shape...  252 us
    unnamed x17, local copies, waits for them, and re-layouts  25 us
    dot_general x1, matrix products, shards(): jnp.einsum('rf,rd->fd', hidden_rows, arrived, preferred_element_type=jnp....  18.5 us
    gather x1, local copies, waits for them, and re-layouts, shards(): returned.reshape(slot_count, model_width)[slot_index]  10.7 us
    dot_general x1, matrix products, shards(): jnp.einsum('rd,fd->rf', arrived, gathered_weight, preferred_element_type=...  8.46 us
    dot_general x1, matrix products, shards(): jnp.dot(hidden_rows, gathered_weight, preferred_element_type=jnp.float32)  8.25 us
  transfers between devices with their start and end apart: 2, of which 0 were waited for; matrix products, arithmetic and copies ran while one was open for 24% of the time, Pallas kernels for 69%

profile of v3, /device:TPU:18, one launch (start us, length us, event | category | flops | bytes accessed | tf_op | source)
XLA Modules:
  0.0 368.1 jit_solution(17143950958411188600)
XLA Ops:
  7.2 0.7 all-gather.2.cloned.1.call-update
  8.0 0.8 copy.13
  8.9 0.7 broadcast_multiply_fusion
  9.8 0.8 copy.16
  10.7 0.9 reduce-window.6
  11.6 0.2 slice_reduce_fusion
  12.0 2.9 scatter_custom_fusion
  15.0 4.0 %gather_fusion = f32[576]{0:T(1024)S(1)} fusion(f32[384]{0:T(512)S(1)} %reshape.88, s32[1024]{0:T(1024)S(1)} %get-tuple-element.19), kind=kCustom, calls=%fused_computation | custom fusion | bytes 6912 | tf_op jit(solution)/shard_map/gather | solution.py:96
  18.9 0.1 mul.34
  19.1 0.5 copy.11
  19.6 1.2 reshape.86
  20.8 5.2 %gather_fusion.1 = bf16[576,4096]{1,0:T(8,128)(2,1)} fusion(bf16[48,4096]{1,0:T(8,128)(2,1)S(1)} %copy-done, s32[1024]{0:T(1024)S(1)} %get-tuple-element.18), kind=kCustom, calls=%fused_computation.1 | custom fusion | bytes 9439488 | tf_op jit(solution)/shard_map/gather | solution.py:97
  26.0 3.9 %convert_bitcast_fusion = f32[72,8,32,128]{3,1,2,0:T(8,128)S(1)} fusion(bf16[576,4096]{1,0:T(8,128)(2,1)} %gather_fusion.1), kind=kLoop, calls=%fused_computation.4 | loop fusion | flops 2359296 | bytes 14155776
  29.9 2.1 copy.24
  32.0 2.7 multiply_convert_fusion.src
  34.8 126.9 %shard_map.84 = bf16[64,9,32,128]{3,2,1,0:T(8,128)(2,1)} custom-call(bf16[64,9,32,128]{3,2,1,0:T(8,128)(2,1)} %multiply_convert_fusion.src), custom_call_target="tpu_custom_call" | custom-call | tf_op jit(solution)/shard_map/pallas_call | solution.py:59
  161.7 18.5 %fusion.7 = bf16[1,768,4096]{1,2,0:T(8,128)(2,1)} fusion(bf16[576,768]{1,0:T(8,128)(2,1)S(1)} %copy-done.2, bf16[72,8,32,128]{3,2,1,0:T(8,128)(2,1)} %bitcast.74), kind=kOutput, calls=%fused_computation.12 | convolution fusion | flops 3627024384 | bytes 11894784 | tf_op jit(solution)/shard_map/rf,rd->fd/dot_general | solution.py:104
  180.1 8.3 %fusion.4 = bf16[576,4096]{1,0:T(8,128)(2,1)} fusion(bf16[576,768]{1,0:T(8,128)(2,1)S(1)} %copy-done.2, bf16[1,768,4096]{2,1,0:T(8,128)(2,1)} %all-gather.2.cloned.1.call-done), kind=kOutput, calls=%fused_computation.11 | convolution fusion | flops 3626237952 | bytes 11894784 | tf_op jit(solution)/shard_map/dot_general | solution.py:100
  188.4 0.7 copy-done.3
  189.1 0.7 copy.19
  189.8 6.0 %copy.26 = bf16[72,8,32,128]{3,2,1,0:T(8,128)(2,1)} copy(bf16[72,8,32,128]{3,1,2,0:T(8,128)(2,1)} %bitcast.76) | data formatting | bytes 9437184
  195.8 125.4 %shard_map.85 = bf16[64,9,32,128]{3,2,1,0:T(8,128)(2,1)} custom-call(bf16[64,9,32,128]{3,2,1,0:T(8,128)(2,1)} %bitcast.72), custom_call_target="tpu_custom_call" | custom-call | tf_op jit(solution)/shard_map/pallas_call | solution.py:59
  321.2 9.2 %copy.43 = bf16[72,8,32,128]{3,1,2,0:T(8,128)(2,1)} copy(bf16[72,8,32,128]{3,2,1,0:T(8,128)(2,1)} %bitcast.73) | data formatting | bytes 9437184
  330.4 10.7 %gather_fusion.2 = bf16[384,4096]{1,0:T(8,128)(2,1)S(1)} fusion(bf16[576,4096]{1,0:T(8,128)(2,1)} %bitcast.70, s32[1024]{0:T(1024)S(1)} %pad_clamp_fusion), kind=kCustom, calls=%fused_computation.2 | custom fusion | bytes 6292992 | tf_op jit(solution)/shard_map/gather | solution.py:112
  341.1 1.7 fusion.14
  342.8 1.2 copy.44
  344.0 2.7 fusion.12
  346.7 1.4 copy.22
  348.1 8.5 %fusion.16 = bf16[576,768]{1,0:T(8,128)(2,1)S(1)} fusion(bf16[1,768,4096]{2,1,0:T(8,128)(2,1)} %all-gather.2.cloned.1.call-done, bf16[72,8,32,128]{3,2,1,0:T(8,128)(2,1)} %bitcast.75), kind=kOutput, calls=%fused_computation.22 | convolution fusion | flops 3624321024 | bytes 11894784 | tf_op jit(solution)/shard_map/rd,fd->rf/dot_general | solution.py:119
  356.6 0.4 reshape.93
  357.0 1.2 copy.17
  358.2 3.1 copy.18
  (26 shorter events, 0.8 us)
Async XLA Ops:
  7.2 13.6 %copy-start = (bf16[48,4096]{1,0:T(8,128)(2,1)S(1)}, bf16[48,4096]{1,0:T(8,128)(2,1)}, u32[]{:S(2)}) copy-start(bf16[48,4096]{1,0:T(8,128)(2,1)} %param.9) | copy-start | bytes 1179652
  7.2 11.9 %copy-start.1 = (bf16[1,1,64,9,768]{4,2,3,1,0:T(8,128)(2,1)S(1)}, bf16[1,1,64,9,768]{4,2,3,1,0:T(8,128)(2,1)}, u32[]{:S(2)}) copy-start(bf16[1,1,64,9,768]{4,2,3,1,0:T(8,128)(2,1)} %param.7) | copy-start | bytes 2654212
  7.2 173.0 %all-gather.2.cloned.1.call-start = ((), (), s32[]{:S(2)}) async-start(), calls=%async_computation.1 | async-start | bytes 7864320 | tf_op jit(solution)/shard_map/all_gather | solution.py:99
  7.9 350.3 %reduce-scatter.2.cloned.1.call-start = ((), (), s32[]{:S(2)}) async-start(), calls=%async_computation.2 | async-start | bytes 7864320 | tf_op jit(solution)/shard_map/reduce_scatter | solution.py:108
  34.8 126.9 %copy-start.2 = (bf16[576,768]{1,0:T(8,128)(2,1)S(1)}, bf16[576,768]{1,0:T(8,128)(2,1)}, u32[]{:S(2)}) copy-start(bf16[576,768]{1,0:T(8,128)(2,1)} %reshape.86) | copy-start | bytes 2654212
  188.4 0.7 copy-start.3
Sparse Core Ops, SparseCore 0:
  9.8 70.6 all-gather.1
  188.5 70.2 reduce-scatter.1

commit v4 on v1

--- a/solution.py
+++ b/solution.py
@@ -33,34 +33,38 @@
     hidden_rows = expert_hidden.reshape(-1, hidden_width)
     flat_probs = route_probs.reshape(-1)
     slot_prob = jnp.where(filled, flat_probs[safe_owner], jnp.float32(0.0))
+    lanes = 128
+    grad_tiles = out_grad.reshape(tok_count, model_width // lanes, lanes)
+    gathered_weight = lax.all_gather(down_weight, "dp", axis=2, tiled=True)[0]
     slot_out = jnp.dot(
-        hidden_rows,
-        lax.all_gather(down_weight, "dp", axis=2, tiled=True)[0],
-        preferred_element_type=jnp.float32,
+        hidden_rows, gathered_weight, preferred_element_type=jnp.float32
     ).astype(jnp.bfloat16)
     returned = lax.all_to_all(
-        slot_out.reshape(expert_count, capacity, model_width // 128, 128),
+        slot_out.reshape(expert_count, capacity, model_width // lanes, lanes),
         "expert",
         split_axis=0,
         concat_axis=0,
         tiled=True,
     )
-    route_out = returned.reshape(slot_count, model_width)[slot_index].reshape(
-        tok_count, top_count, model_width
+    route_out = returned.reshape(slot_count, model_width // lanes, lanes)[slot_index].reshape(
+        tok_count, top_count, model_width // lanes, lanes
+    ).astype(jnp.float32)
+    layer_out = jnp.sum(route_probs[:, :, None, None] * route_out, axis=1)
+    layer_out = layer_out.astype(jnp.bfloat16).reshape(tok_count, model_width)
+    prob_grad = jnp.sum(
+        grad_tiles[:, None].astype(jnp.float32) * route_out, axis=(2, 3)
     )
-    layer_out = jnp.einsum(
-        "tk,tkd->td", route_probs, route_out, preferred_element_type=jnp.float32
+    scaled = (
+        slot_prob[:, None, None] * grad_tiles[safe_owner // top_count].astype(jnp.float32)
     ).astype(jnp.bfloat16)
-    prob_grad = jnp.einsum("td,tkd->tk", out_grad, route_out, preferred_element_type=jnp.float32)
-    scaled = (slot_prob[:, None] * out_grad[safe_owner // top_count]).astype(jnp.bfloat16)
     arrived = lax.all_to_all(
-        scaled.reshape(expert_count, capacity, model_width // 128, 128),
+        scaled.reshape(expert_count, capacity, model_width // lanes, lanes),
         "expert",
         split_axis=0,
         concat_axis=0,
         tiled=True,
     )
-    arrived = arrived.reshape(-1, model_width)
+    arrived = lax.optimization_barrier(arrived.reshape(-1, model_width))
     partial_value = jnp.einsum(
         "rf,rd->fd", hidden_rows, arrived, preferred_element_type=jnp.float32
     )[None]
@@ -68,10 +72,7 @@
         rounded_partial(partial_value).astype(jnp.bfloat16), "dp", scatter_dimension=2, tiled=True
     ).astype(jnp.float32)
     hidden_total = jnp.einsum(
-        "rd,fd->rf",
-        arrived,
-        lax.all_gather(down_weight, "dp", axis=2, tiled=True)[0],
-        preferred_element_type=jnp.float32,
+        "rd,fd->rf", arrived, gathered_weight, preferred_element_type=jnp.float32
     )
     hidden_grad = hidden_total.astype(jnp.bfloat16).reshape(expert_hidden.shape)
     return (layer_out, prob_grad, hidden_grad, weight_grad)

time: 332 us -> 307 us (0.925)
  matrix products: 38.3 us -> 22.1 us
  local copies, waits for them, and re-layouts: 49.1 us -> 36.8 us
  other arithmetic: 7.98 us -> 11.7 us
    dot_general x1, matrix products: 18.4 us -> 7.04 us  [shards(): jnp.einsum('rf,rd->fd', hidden_rows, arrived, preferred_element_type=jnp....]
    gather x2, local copies, waits for them, and re-layouts: 15.9 us -> 7.49 us  [the longest x1 3.91 us: shards(): grad_tiles[safe_owner // top_count].astype(jnp.float32)]
    dot_general x4 -> x2, matrix products: 19.9 us -> 15.1 us  [the longest x1 8.21 us: shards(): jnp.einsum('rd,fd->rf', arrived, gathered_weight, preferred_element_type=...]
    reduce_sum x0 -> x1, other arithmetic: none -> 4.43 us  [shards(): jnp.sum(grad_tiles[:, None].astype(jnp.float32) * route_out, axis=(2, 3))]
    unnamed x1 -> x0, other arithmetic: 3.58 us -> none
    unnamed x15 -> x16, local copies, waits for them, and re-layouts: 22.1 us -> 20.8 us
  transfers between devices with their start and end apart: 4 -> 4, of which waited for: 2 -> 2; matrix products, arithmetic and copies ran while one was open for 20% -> 15% of each run, Pallas kernels for 0% -> 0%
where the time goes in v4:
time: 307 us; the launch traced here: 306 us
  waiting for transfers between devices  203 us (66%)
  local copies, waits for them, and re-layouts  36.8 us (12%)
  matrix products  22.1 us (7%)
  starting transfers between devices  18.3 us (6%)
  between operations  14.2 us (5%)
  other arithmetic  11.7 us (4%)
    all_to_all x1, waiting for transfers between devices, shards(): lax.all_to_all(scaled.reshape(expert_count, capacity, model_width // lane...  105 us
    all_to_all x1, waiting for transfers between devices, shards(): lax.all_to_all(slot_out.reshape(expert_count, capacity, model_width // la...  96.6 us
    unnamed x16, local copies, waits for them, and re-layouts  20.8 us
    all_to_all x1, starting transfers between devices, shards(): lax.all_to_all(scaled.reshape(expert_count, capacity, model_width // lane...  12.3 us
    dot_general x1, matrix products, shards(): jnp.einsum('rd,fd->rf', arrived, gathered_weight, preferred_element_type=...  8.21 us
    dot_general x1, matrix products, shards(): jnp.einsum('rf,rd->fd', hidden_rows, arrived, preferred_element_type=jnp....  7.04 us
    dot_general x1, matrix products, shards(): jnp.dot(hidden_rows, gathered_weight, preferred_element_type=jnp.float32)  6.87 us
  transfers between devices with their start and end apart: 4, of which 2 were waited for; matrix products, arithmetic and copies ran while one was open for 15% of the time, Pallas kernels for 0%

profile of v4, /device:TPU:18, one launch (start us, length us, event | category | flops | bytes accessed | tf_op | source)
XLA Modules:
  0.0 305.8 jit_solution(15485443383557292338)
XLA Ops:
  7.2 0.8 copy.24
  8.2 0.7 broadcast_multiply_fusion
  8.9 0.9 reduce-window.6
  9.8 0.2 slice_reduce_fusion
  10.4 2.9 scatter_custom_fusion
  13.3 0.8 copy.21
  14.2 4.0 %gather_fusion.1 = f32[576]{0:T(1024)S(1)} fusion(f32[384]{0:T(512)S(1)} %reshape.109, s32[1024]{0:T(1024)S(1)} %get-tuple-element.21), kind=kCustom, calls=%fused_computation.1 | custom fusion | bytes 6912 | tf_op jit(solution)/shard_map/gather | solution.py:35
  18.2 0.1 mul.58
  18.4 3.9 %gather_fusion.2 = bf16[576,32,128]{2,1,0:T(8,128)(2,1)} fusion(bf16[48,32,128]{2,1,0:T(8,128)(2,1)S(1)} %bitcast.60, s32[1024]{0:T(1024)S(1)} %get-tuple-element.20), kind=kCustom, calls=%fused_computation.2 | custom fusion | bytes 9439488 | tf_op jit(solution)/shard_map/gather | solution.py:58
  22.3 4.4 %fusion = bf16[64,9,32,128]{3,2,1,0:T(8,128)(2,1)} fusion(bf16[64,9,32,128]{3,2,1,0:T(8,128)(2,1)} %bitcast.62, f32[64,9]{1,0:T(8,128)S(1)} %mul.58), kind=kLoop, calls=%fused_computation.5 | loop fusion | flops 7077888 | bytes 9439488 | tf_op jit(solution)/shard_map/convert_element_type | solution.py:59
  26.7 12.3 %all-to-all-start.1 = ((bf16[64,9,32,128]{3,2,1,0:T(8,128)(2,1)}), bf16[64,9,32,128]{3,2,1,0:T(8,128)(2,1)}, u32[]{:S(2)}, u32[]{:S(2)}) async-start(bf16[64,9,32,128]{3,2,1,0:T(8,128)(2,1)} %fusion), calls=%async_computation.1 | async-start | bytes 9437184 | tf_op jit(solution)/shard_map/all_to_all | solution.py:60
  39.1 0.7 all-gather.2.cloned.1.call-update
  39.7 0.2 reduce-scatter.2.cloned.1.call-start
  40.0 0.5 copy.22
  40.5 0.4 reshape.105
  41.0 105.4 %all-to-all-done.1 = bf16[64,9,32,128]{3,2,1,0:T(8,128)(2,1)} async-done(((bf16[64,9,32,128]{3,2,1,0:T(8,128)(2,1)}), bf16[64,9,32,128]{3,2,1,0:T(8,128)(2,1)}, u32[]{:S(2)}, u32[]{:S(2)}) %all-to-all-start.1) | async-done | bytes 4718624 | tf_op jit(solution)/shard_map/all_to_all | solution.py:60
  146.4 7.0 %copy.39 = bf16[72,8,32,128]{3,1,2,0:T(8,128)(2,1)S(1)} copy(bf16[72,8,32,128]{3,2,1,0:T(8,128)(2,1)} %bitcast.20) | data formatting | bytes 9437184
  153.5 2.1 copy-done
  155.5 7.0 %fusion.10 = bf16[1,768,4096]{1,2,0:T(8,128)(2,1)} fusion(bf16[576,4096]{1,0:T(8,128)(2,1)S(1)} %bitcast.64, bf16[576,768]{1,0:T(8,128)(2,1)S(1)} %reshape.105), kind=kOutput, calls=%fused_computation.16 | convolution fusion | flops 3627024384 | bytes 11894784 | tf_op jit(solution)/shard_map/rf,rd->fd/dot_general | solution.py:68
  162.6 6.9 %fusion.11 = bf16[72,8,32,128]{3,1,2,0:T(8,128)(2,1)S(1)} fusion(bf16[576,768]{1,0:T(8,128)(2,1)S(1)} %reshape.105, bf16[1,768,4096]{2,1,0:T(8,128)(2,1)} %all-gather.2.cloned.1.call-done), kind=kOutput, calls=%fused_computation.18 | convolution fusion | flops 3626237952 | bytes 11894784 | tf_op jit(solution)/shard_map/dot_general | solution.py:39
  169.5 3.6 %copy.32 = bf16[72,8,32,128]{3,2,1,0:T(8,128)(2,1)} copy(bf16[72,8,32,128]{3,1,2,0:T(8,128)(2,1)S(1)} %fusion.11) | data formatting | bytes 9437184
  173.2 5.8 %all-to-all-start = ((bf16[64,9,32,128]{3,2,1,0:T(8,128)(2,1)}), bf16[64,9,32,128]{3,2,1,0:T(8,128)(2,1)}, u32[]{:S(2)}, u32[]{:S(2)}) async-start(bf16[64,9,32,128]{3,2,1,0:T(8,128)(2,1)} %bitcast.61), calls=%async_computation | async-start | bytes 9437184 | tf_op jit(solution)/shard_map/all_to_all | solution.py:42
  179.0 1.0 bitcast_convert_fusion
  180.0 8.2 %fusion.14 = bf16[576,768]{1,0:T(8,128)(2,1)S(1)} fusion(bf16[576,4096]{1,0:T(8,128)(2,1)} %bitcast.65, bf16[1,768,4096]{2,1,0:T(8,128)(2,1)} %all-gather.2.cloned.1.call-done), kind=kOutput, calls=%fused_computation.19 | convolution fusion | flops 3624321024 | bytes 11894784 | tf_op jit(solution)/shard_map/rd,fd->rf/dot_general | solution.py:74
  188.2 0.4 reshape.111
  188.6 1.2 copy.29
  189.8 96.6 %all-to-all-done = bf16[64,9,32,128]{3,2,1,0:T(8,128)(2,1)} async-done(((bf16[64,9,32,128]{3,2,1,0:T(8,128)(2,1)}), bf16[64,9,32,128]{3,2,1,0:T(8,128)(2,1)}, u32[]{:S(2)}, u32[]{:S(2)}) %all-to-all-start) | async-done | bytes 4718624 | tf_op jit(solution)/shard_map/all_to_all | solution.py:42
  286.4 3.6 %gather_fusion = bf16[384,32,128]{2,1,0:T(8,128)(2,1)S(1)} fusion(bf16[576,32,128]{2,1,0:T(8,128)(2,1)} %bitcast.1, s32[1024]{0:T(1024)S(1)} %pad_clamp_fusion.2), kind=kCustom, calls=%fused_computation | custom fusion | bytes 6292992 | tf_op jit(solution)/shard_map/gather | solution.py:49
  289.9 4.4 %fusion.2 = (f32[48,8]{1,0:T(8,128)S(1)}, bf16[48,32,128]{2,1,0:T(8,128)(2,1)S(1)}) fusion(bf16[48,8,32,128]{3,2,1,0:T(8,128)(2,1)S(1)} %bitcast.63, f32[48,32,128]{2,1,0:T(8,128)} %bitcast_convert_fusion, f32[48,8]{1,0:T(8,128)S(1)} %copy.21), kind=kLoop, calls=%fused_computation.10 | loop fusion | flops 7667328 | bytes 4328448 | tf_op jit(solution)/shard_map/reduce_sum | solution.py:54
  294.4 0.9 copy.40
  295.3 0.7 copy.28
  295.9 3.1 %copy.30 = f32[1,768,1024]{2,1,0:T(8,128)} copy(bf16[1,768,1024]{1,2,0:T(8,128)(2,1)} %reduce-scatter.2.cloned.1.call-done) | data formatting | bytes 4718592
  (24 shorter events, 0.8 us)
Async XLA Ops:
  7.2 11.2 %copy-start.2 = (bf16[48,4096]{1,0:T(8,128)(2,1)S(1)}, bf16[48,4096]{1,0:T(8,128)(2,1)}, u32[]{:S(2)}) copy-start(bf16[48,4096]{1,0:T(8,128)(2,1)} %param.9) | copy-start | bytes 1179652
  26.7 13.3 %copy-start.1 = (bf16[1,1,64,9,768]{4,2,3,1,0:T(8,128)(2,1)S(1)}, bf16[1,1,64,9,768]{4,2,3,1,0:T(8,128)(2,1)}, u32[]{:S(2)}) copy-start(bf16[1,1,64,9,768]{4,2,3,1,0:T(8,128)(2,1)} %param.7) | copy-start | bytes 2654212
  26.7 119.7 %all-to-all-start.1 = ((bf16[64,9,32,128]{3,2,1,0:T(8,128)(2,1)}), bf16[64,9,32,128]{3,2,1,0:T(8,128)(2,1)}, u32[]{:S(2)}, u32[]{:S(2)}) async-start(bf16[64,9,32,128]{3,2,1,0:T(8,128)(2,1)} %fusion), calls=%async_computation.1 | async-start | bytes 9437184 | tf_op jit(solution)/shard_map/all_to_all | solution.py:60
  39.0 123.6 %all-gather.2.cloned.1.call-start = ((), (), s32[]{:S(2)}) async-start(), calls=%async_computation.3 | async-start | bytes 7864320 | tf_op jit(solution)/shard_map/all_gather | solution.py:38
  39.7 256.2 %reduce-scatter.2.cloned.1.call-start = ((), (), s32[]{:S(2)}) async-start(), calls=%async_computation.4 | async-start | bytes 7864320 | tf_op jit(solution)/shard_map/reduce_scatter | solution.py:71
  153.4 2.1 copy-start
  173.2 113.2 %all-to-all-start = ((bf16[64,9,32,128]{3,2,1,0:T(8,128)(2,1)}), bf16[64,9,32,128]{3,2,1,0:T(8,128)(2,1)}, u32[]{:S(2)}, u32[]{:S(2)}) async-start(bf16[64,9,32,128]{3,2,1,0:T(8,128)(2,1)} %bitcast.61), calls=%async_computation | async-start | bytes 9437184 | tf_op jit(solution)/shard_map/all_to_all | solution.py:42
Sparse Core Ops, SparseCore 0:
  41.7 68.9 all-gather.1
  162.7 61.4 reduce-scatter.1

commit v5 on v3

--- a/solution.py
+++ b/solution.py
@@ -37,15 +37,19 @@
             device_id_type=MESH,
         )
 
+    def offset(i):
+        odd = i % 2
+        return odd * ((i + 1) // 2) + (1 - odd) * (n - i // 2)
+
     def start(i, carry):
-        remote(lax.rem(me + i, n), me).start()
+        remote(lax.rem(me + offset(i), n), me).start()
         return carry
 
     lax.fori_loop(1, n, start, 0)
 
     def finish(i, carry):
-        source = lax.rem(me + n - i, n)
-        remote(lax.rem(me + i, n), me).wait_send()
+        source = lax.rem(me + n - offset(i), n)
+        remote(lax.rem(me + offset(i), n), me).wait_send()
         remote(source, source).wait_recv()
         return carry
 
@@ -94,8 +98,12 @@
     hidden_rows = expert_hidden.reshape(-1, hidden_width)
     flat_probs = route_probs.reshape(-1)
     slot_prob = jnp.where(filled, flat_probs[safe_owner], jnp.float32(0.0))
-    scaled = (slot_prob[:, None] * out_grad[safe_owner // top_count]).astype(jnp.bfloat16)
-    arrived = exchange(scaled.reshape(expert_count, capacity, model_width // 128, 128), 0)
+    lanes = 128
+    grad_tiles = out_grad.reshape(tok_count, model_width // lanes, lanes)
+    scaled = (
+        slot_prob[:, None, None] * grad_tiles[safe_owner // top_count].astype(jnp.float32)
+    ).astype(jnp.bfloat16)
+    arrived = exchange(scaled.reshape(expert_count, capacity, model_width // lanes, lanes), 0)
     gathered_weight = lax.all_gather(down_weight, "dp", axis=2, tiled=True)[0]
     slot_out = jnp.dot(
         hidden_rows, gathered_weight, preferred_element_type=jnp.float32
@@ -108,19 +116,17 @@
     weight_grad = lax.psum_scatter(narrow, "dp", scatter_dimension=2, tiled=True).astype(
         jnp.float32
     )
-    returned = exchange(slot_out.reshape(expert_count, capacity, model_width // 128, 128), 1)
-    route_out = returned.reshape(slot_count, model_width)[slot_index].reshape(
-        tok_count, top_count, model_width
+    returned = exchange(slot_out.reshape(expert_count, capacity, model_width // lanes, lanes), 1)
+    route_out = returned.reshape(slot_count, model_width // lanes, lanes)[slot_index].reshape(
+        tok_count, top_count, model_width // lanes, lanes
+    ).astype(jnp.float32)
+    layer_out = jnp.sum(route_probs[:, :, None, None] * route_out, axis=1)
+    layer_out = layer_out.astype(jnp.bfloat16).reshape(tok_count, model_width)
+    prob_grad = jnp.sum(
+        grad_tiles[:, None].astype(jnp.float32) * route_out, axis=(2, 3)
     )
-    layer_out = jnp.einsum(
-        "tk,tkd->td", route_probs, route_out, preferred_element_type=jnp.float32
-    ).astype(jnp.bfloat16)
-    prob_grad = jnp.einsum("td,tkd->tk", out_grad, route_out, preferred_element_type=jnp.float32)
     hidden_total = jnp.einsum(
-        "rd,fd->rf",
-        arrived,
-        gathered_weight,
-        preferred_element_type=jnp.float32,
+        "rd,fd->rf", arrived, gathered_weight, preferred_element_type=jnp.float32
     )
     hidden_grad = hidden_total.astype(jnp.bfloat16).reshape(expert_hidden.shape)
     return (layer_out, prob_grad, hidden_grad, weight_grad)

time: 374 us -> 351 us (0.939)
  the two profiles are of different devices: /device:TPU:18 before, /device:TPU:31 now
where the time goes in v5:
time: 351 us
  Pallas kernels  257 us (73%)
  matrix products  35.2 us (10%)
  local copies, waits for them, and re-layouts  31.2 us (9%)
  between operations  14.2 us (4%)
  other arithmetic  13 us (4%)
    pallas_call x2, Pallas kernels, exchange(): pl.pallas_call(functools.partial(exchange_kernel, n), out_shape=jax.Shape...  257 us
    dot_general x1, matrix products, shards(): jnp.einsum('rf,rd->fd', hidden_rows, arrived, preferred_element_type=jnp....  18.5 us
    unnamed x15, local copies, waits for them, and re-layouts  15.2 us
    dot_general x1, matrix products, shards(): jnp.einsum('rd,fd->rf', arrived, gathered_weight, preferred_element_type=...  8.46 us
    dot_general x1, matrix products, shards(): jnp.dot(hidden_rows, gathered_weight, preferred_element_type=jnp.float32)  8.25 us
  transfers between devices with their start and end apart: 2, of which 0 were waited for; matrix products, arithmetic and copies ran while one was open for 19% of the time, Pallas kernels for 73%

profile of v5, /device:TPU:31, one launch (start us, length us, event | category | flops | bytes accessed | tf_op | source)
XLA Modules:
  0.0 350.9 jit_solution(5031939502229214564)
XLA Ops:
  7.2 0.7 all-gather.2.cloned.1.call-update
  8.0 0.8 copy.24
  8.7 0.1 eq.29
  8.8 0.1 eq.25
  8.9 0.7 broadcast_multiply_fusion
  9.7 0.1 mul.53
  9.8 0.8 copy.21
  10.6 0.5 copy-done.2
  11.2 0.9 reduce-window.6
  12.1 0.2 slice_reduce_fusion
  12.3 0.1 fusion.22
  12.5 2.9 scatter_custom_fusion
  15.5 4.0 %gather_fusion = f32[576]{0:T(1024)S(1)} fusion(f32[384]{0:T(512)S(1)} %reshape.109, s32[1024]{0:T(1024)S(1)} %get-tuple-element.25), kind=kCustom, calls=%fused_computation | custom fusion | bytes 6912 | tf_op jit(solution)/shard_map/gather | solution.py:100
  19.4 0.1 mul.55
  19.7 0.5 copy.22
  20.2 0.4 reshape.107
  20.6 3.9 %gather_fusion.1 = bf16[576,32,128]{2,1,0:T(8,128)(2,1)} fusion(bf16[48,32,128]{2,1,0:T(8,128)(2,1)S(1)} %bitcast.60, s32[1024]{0:T(1024)S(1)} %get-tuple-element.24), kind=kCustom, calls=%fused_computation.1 | custom fusion | bytes 9439488 | tf_op jit(solution)/shard_map/gather | solution.py:104
  24.6 5.0 %fusion.src = bf16[64,9,32,128]{3,2,1,0:T(8,128)(2,1)} fusion(bf16[64,9,32,128]{3,2,1,0:T(8,128)(2,1)} %bitcast.61, f32[64,9]{1,0:T(8,128)S(1)} %mul.55), kind=kLoop, calls=%fused_computation.5 | loop fusion | flops 7077888 | bytes 9439488 | tf_op jit(solution)/shard_map/convert_element_type | solution.py:105
  29.5 127.3 %shard_map.84 = bf16[64,9,32,128]{3,2,1,0:T(8,128)(2,1)} custom-call(bf16[64,9,32,128]{3,2,1,0:T(8,128)(2,1)} %fusion.src), custom_call_target="tpu_custom_call" | custom-call | tf_op jit(solution)/shard_map/pallas_call | solution.py:63
  156.8 18.5 %fusion.10 = bf16[1,768,4096]{1,2,0:T(8,128)(2,1)} fusion(bf16[576,768]{1,0:T(8,128)(2,1)S(1)} %reshape.107, bf16[72,8,32,128]{3,2,1,0:T(8,128)(2,1)} %bitcast.65), kind=kOutput, calls=%fused_computation.16 | convolution fusion | flops 3627024384 | bytes 11894784 | tf_op jit(solution)/shard_map/rf,rd->fd/dot_general | solution.py:112
  175.3 8.3 %fusion.7 = bf16[576,4096]{1,0:T(8,128)(2,1)} fusion(bf16[576,768]{1,0:T(8,128)(2,1)S(1)} %reshape.107, bf16[1,768,4096]{2,1,0:T(8,128)(2,1)} %all-gather.2.cloned.1.call-done), kind=kOutput, calls=%fused_computation.15 | convolution fusion | flops 3626237952 | bytes 11894784 | tf_op jit(solution)/shard_map/dot_general | solution.py:108
  183.6 1.0 bitcast_convert_fusion
  184.6 6.0 %copy.34 = bf16[72,8,32,128]{3,2,1,0:T(8,128)(2,1)} copy(bf16[72,8,32,128]{3,1,2,0:T(8,128)(2,1)} %bitcast.67) | data formatting | bytes 9437184
  190.6 129.3 %shard_map.85 = bf16[64,9,32,128]{3,2,1,0:T(8,128)(2,1)} custom-call(bf16[64,9,32,128]{3,2,1,0:T(8,128)(2,1)} %bitcast.62), custom_call_target="tpu_custom_call" | custom-call | tf_op jit(solution)/shard_map/pallas_call | solution.py:63
  319.9 3.6 %gather_fusion.2 = bf16[384,32,128]{2,1,0:T(8,128)(2,1)S(1)} fusion(bf16[576,32,128]{2,1,0:T(8,128)(2,1)} %bitcast.63, s32[1024]{0:T(1024)S(1)} %pad_clamp_fusion), kind=kCustom, calls=%fused_computation.2 | custom fusion | bytes 6292992 | tf_op jit(solution)/shard_map/gather | solution.py:120
  323.4 5.2 %fusion.2 = (f32[48,8]{1,0:T(8,128)}, bf16[48,32,128]{2,1,0:T(8,128)(2,1)S(1)}) fusion(bf16[48,8,32,128]{3,2,1,0:T(8,128)(2,1)S(1)} %bitcast.64, f32[48,32,128]{2,1,0:T(8,128)} %bitcast_convert_fusion, f32[48,8]{1,0:T(8,128)} %copy-done.2), kind=kLoop, calls=%fused_computation.10 | loop fusion | flops 7667328 | bytes 4328448 | tf_op jit(solution)/shard_map/reduce_sum | solution.py:125
  328.7 1.4 copy.28
  330.0 0.9 copy.48
  330.9 8.5 %fusion.15 = bf16[576,768]{1,0:T(8,128)(2,1)S(1)} fusion(bf16[1,768,4096]{2,1,0:T(8,128)(2,1)} %all-gather.2.cloned.1.call-done, bf16[72,8,32,128]{3,2,1,0:T(8,128)(2,1)} %bitcast.66), kind=kOutput, calls=%fused_computation.21 | convolution fusion | flops 3624321024 | bytes 11894784 | tf_op jit(solution)/shard_map/rd,fd->rf/dot_general | solution.py:128
  339.4 0.4 reshape.114
  339.8 1.2 copy.29
  341.0 3.1 copy.30
  (21 shorter events, 0.4 us)
Async XLA Ops:
  7.2 12.4 %copy-start.1 = (bf16[48,4096]{1,0:T(8,128)(2,1)S(1)}, bf16[48,4096]{1,0:T(8,128)(2,1)}, u32[]{:S(2)}) copy-start(bf16[48,4096]{1,0:T(8,128)(2,1)} %param.9) | copy-start | bytes 1179652
  7.2 12.5 %copy-start = (bf16[1,1,64,9,768]{4,2,3,1,0:T(8,128)(2,1)S(1)}, bf16[1,1,64,9,768]{4,2,3,1,0:T(8,128)(2,1)}, u32[]{:S(2)}) copy-start(bf16[1,1,64,9,768]{4,2,3,1,0:T(8,128)(2,1)} %param.7) | copy-start | bytes 2654212
  7.2 168.1 %all-gather.2.cloned.1.call-start = ((), (), s32[]{:S(2)}) async-start(), calls=%async_computation.1 | async-start | bytes 7864320 | tf_op jit(solution)/shard_map/all_gather | solution.py:107
  7.9 333.1 %reduce-scatter.2.cloned.1.call-start = ((), (), s32[]{:S(2)}) async-start(), calls=%async_computation.2 | async-start | bytes 7864320 | tf_op jit(solution)/shard_map/reduce_scatter | solution.py:116
  10.6 0.6 copy-start.2
Sparse Core Ops, SparseCore 0:
  9.8 69.6 all-gather.1
  183.7 65.1 reduce-scatter.1

commit v6 on v4

--- a/solution.py
+++ b/solution.py
@@ -23,24 +23,20 @@
     earlier = jnp.cumsum(onehot, axis=0) - onehot
     position = jnp.sum(earlier * onehot, axis=1)
     slot_index = flat_ids * capacity + position
-    slot_owner = (
-        jnp.full((slot_count,), -1, dtype=jnp.int32)
-        .at[slot_index]
-        .set(jnp.arange(tok_count * top_count, dtype=jnp.int32))
-    )
-    filled = slot_owner >= 0
-    safe_owner = jnp.maximum(slot_owner, 0)
+    holds = slot_index[None, :] == jnp.arange(slot_count, dtype=jnp.int32)[:, None]
+    route_token = jnp.arange(tok_count * top_count, dtype=jnp.int32) // top_count
+    slot_token = jnp.sum(jnp.where(holds, route_token[None, :], 0), axis=1)
+    slot_prob = jnp.sum(jnp.where(holds, route_probs.reshape(-1)[None, :], jnp.float32(0.0)), axis=1)
     hidden_rows = expert_hidden.reshape(-1, hidden_width)
-    flat_probs = route_probs.reshape(-1)
-    slot_prob = jnp.where(filled, flat_probs[safe_owner], jnp.float32(0.0))
     lanes = 128
     grad_tiles = out_grad.reshape(tok_count, model_width // lanes, lanes)
     gathered_weight = lax.all_gather(down_weight, "dp", axis=2, tiled=True)[0]
     slot_out = jnp.dot(
         hidden_rows, gathered_weight, preferred_element_type=jnp.float32
     ).astype(jnp.bfloat16)
+    outgoing = slot_out.reshape(expert_count, capacity, model_width // lanes, lanes)
     returned = lax.all_to_all(
-        slot_out.reshape(expert_count, capacity, model_width // lanes, lanes),
+        outgoing,
         "expert",
         split_axis=0,
         concat_axis=0,
@@ -55,7 +51,7 @@
         grad_tiles[:, None].astype(jnp.float32) * route_out, axis=(2, 3)
     )
     scaled = (
-        slot_prob[:, None, None] * grad_tiles[safe_owner // top_count].astype(jnp.float32)
+        slot_prob[:, None, None] * grad_tiles[slot_token].astype(jnp.float32)
     ).astype(jnp.bfloat16)
     arrived = lax.all_to_all(
         scaled.reshape(expert_count, capacity, model_width // lanes, lanes),
@@ -64,7 +60,8 @@
         concat_axis=0,
         tiled=True,
     )
-    arrived = lax.optimization_barrier(arrived.reshape(-1, model_width))
+    arrived, _ = lax.optimization_barrier((arrived, outgoing))
+    arrived = arrived.reshape(-1, model_width)
     partial_value = jnp.einsum(
         "rf,rd->fd", hidden_rows, arrived, preferred_element_type=jnp.float32
     )[None]

time: 307 us -> 294 us (0.958)
  local copies, waits for them, and re-layouts: 36.8 us -> 22.5 us
  matrix products: 22.1 us -> 34.7 us
  waiting for transfers between devices: 203 us -> 192 us
    all_to_all x1, waiting for transfers between devices: 105 us -> 49.7 us  [shards(): lax.all_to_all(scaled.reshape(expert_count, capacity, model_width // lane...]
    all_gather x1, waiting for transfers between devices: 0.02 us -> 46.2 us  [shards(): gathered_weight = lax.all_gather(down_weight, 'dp', axis=2, tiled=True)[0]]
    dot_general x1, matrix products: 7.04 us -> 18.5 us  [shards(): jnp.einsum('rf,rd->fd', hidden_rows, arrived, preferred_element_type=jnp....]
    unnamed x16 -> x15, local copies, waits for them, and re-layouts: 20.8 us -> 13.3 us
    gather x2 -> x1, local copies, waits for them, and re-layouts: 7.87 us -> 3.93 us  [shards(): grad_tiles[slot_token].astype(jnp.float32)]
  transfers between devices with their start and end apart: 4 -> 4, of which waited for: 2 -> 3; matrix products, arithmetic and copies ran while one was open for 15% -> 16% of each run, Pallas kernels for 0% -> 0%
where the time goes in v6:
time: 294 us; the launch traced here: 293 us
  waiting for transfers between devices  192 us (65%)
  matrix products  34.7 us (12%)
  local copies, waits for them, and re-layouts  22.5 us (8%)
  starting transfers between devices  18.2 us (6%)
  between operations  14.2 us (5%)
  other arithmetic  11.9 us (4%)
    all_to_all x1, waiting for transfers between devices, shards(): lax.all_to_all(outgoing, 'expert', split_axis=0, concat_axis=0, tiled=True)  95.2 us
    all_to_all x1, waiting for transfers between devices, shards(): lax.all_to_all(scaled.reshape(expert_count, capacity, model_width // lane...  49.7 us
    all_gather x1, waiting for transfers between devices, shards(): gathered_weight = lax.all_gather(down_weight, 'dp', axis=2, tiled=True)[0]  46.2 us
    dot_general x1, matrix products, shards(): jnp.einsum('rf,rd->fd', hidden_rows, arrived, preferred_element_type=jnp....  18.5 us
    unnamed x15, local copies, waits for them, and re-layouts  13.3 us
    all_to_all x1, starting transfers between devices, shards(): lax.all_to_all(scaled.reshape(expert_count, capacity, model_width // lane...  12.3 us
    dot_general x1, matrix products, shards(): jnp.einsum('rd,fd->rf', arrived, gathered_weight, preferred_element_type=...  9.41 us
    dot_general x1, matrix products, shards(): jnp.dot(hidden_rows, gathered_weight, preferred_element_type=jnp.float32)  6.85 us
  transfers between devices with their start and end apart: 4, of which 3 were waited for; matrix products, arithmetic and copies ran while one was open for 16% of the time, Pallas kernels for 0%

profile of v6, /device:TPU:18, one launch (start us, length us, event | category | flops | bytes accessed | tf_op | source)
XLA Modules:
  0.0 293.3 jit_solution(15856457285774149650)
XLA Ops:
  7.2 0.7 all-gather.2.cloned.1.call-update
  7.9 0.8 copy.34
  8.9 0.9 reduce-window.6
  9.8 0.2 slice_reduce_fusion
  10.0 1.1 copy.44
  11.1 0.8 copy.31
  12.0 0.1 fusion.25
  12.1 0.2 select_reduce_fusion.1
  12.3 0.1 mul.68
  12.4 0.2 select_reduce_fusion
  12.6 3.9 %gather_fusion.1 = bf16[576,32,128]{2,1,0:T(8,128)(2,1)} fusion(bf16[48,32,128]{2,1,0:T(8,128)(2,1)S(1)} %bitcast.62, s32[1024]{0:T(1024)S(1)} %pad_clamp_fusion), kind=kCustom, calls=%fused_computation.1 | custom fusion | bytes 9439488 | tf_op jit(solution)/shard_map/gather | solution.py:54
  16.6 4.4 %fusion = bf16[64,9,32,128]{3,2,1,0:T(8,128)(2,1)} fusion(bf16[64,9,32,128]{3,2,1,0:T(8,128)(2,1)} %bitcast.64, f32[64,9]{1,0:T(8,128)S(1)} %mul.68), kind=kLoop, calls=%fused_computation.3 | loop fusion | flops 7077888 | bytes 9439488 | tf_op jit(solution)/shard_map/convert_element_type | solution.py:55
  21.0 12.3 %all-to-all-start.1 = ((bf16[64,9,32,128]{3,2,1,0:T(8,128)(2,1)}), bf16[64,9,32,128]{3,2,1,0:T(8,128)(2,1)}, u32[]{:S(2)}, u32[]{:S(2)}) async-start(bf16[64,9,32,128]{3,2,1,0:T(8,128)(2,1)} %fusion), calls=%async_computation.1 | async-start | bytes 9437184 | tf_op jit(solution)/shard_map/all_to_all | solution.py:56
  33.3 0.5 copy.32
  33.9 0.4 reshape.137
  34.3 46.2 %all-gather.2.cloned.1.call-done = bf16[1,768,4096]{2,1,0:T(8,128)(2,1)} async-done(((bf16[1,768,1024]{2,1,0:T(8,128)(2,1)}), bf16[1,768,4096]{2,1,0:T(8,128)(2,1)}) %all-gather.2.cloned.1.call-update) | async-done | bytes 6291472 | tf_op jit(solution)/shard_map/all_gather | solution.py:33
  80.5 6.8 %fusion.15 = bf16[72,8,32,128]{3,1,2,0:T(8,128)(2,1)S(1)} fusion(bf16[576,768]{1,0:T(8,128)(2,1)S(1)} %reshape.137, bf16[1,768,4096]{2,1,0:T(8,128)(2,1)} %all-gather.2.cloned.1.call-done), kind=kOutput, calls=%fused_computation.19 | convolution fusion | flops 3626237952 | bytes 11894784 | tf_op jit(solution)/shard_map/dot_general | solution.py:34
  87.4 3.6 %copy.42 = bf16[72,8,32,128]{3,2,1,0:T(8,128)(2,1)} copy(bf16[72,8,32,128]{3,1,2,0:T(8,128)(2,1)S(1)} %fusion.15) | data formatting | bytes 9437184
  91.0 49.7 %all-to-all-done.1 = bf16[64,9,32,128]{3,2,1,0:T(8,128)(2,1)} async-done(((bf16[64,9,32,128]{3,2,1,0:T(8,128)(2,1)}), bf16[64,9,32,128]{3,2,1,0:T(8,128)(2,1)}, u32[]{:S(2)}, u32[]{:S(2)}) %all-to-all-start.1) | async-done | bytes 4718624 | tf_op jit(solution)/shard_map/all_to_all | solution.py:56
  140.7 18.5 %fusion.10 = bf16[1,768,4096]{1,2,0:T(8,128)(2,1)} fusion(bf16[576,768]{1,0:T(8,128)(2,1)S(1)} %reshape.137, bf16[72,8,32,128]{3,2,1,0:T(8,128)(2,1)} %bitcast.20), kind=kOutput, calls=%fused_computation.14 | convolution fusion | flops 3627024384 | bytes 11894784 | tf_op jit(solution)/shard_map/rf,rd->fd/dot_general | solution.py:65
  159.2 5.9 %all-to-all-start = ((bf16[64,9,32,128]{3,2,1,0:T(8,128)(2,1)}), bf16[64,9,32,128]{3,2,1,0:T(8,128)(2,1)}, u32[]{:S(2)}, u32[]{:S(2)}) async-start(bf16[64,9,32,128]{3,2,1,0:T(8,128)(2,1)} %bitcast.63), calls=%async_computation | async-start | bytes 9437184 | tf_op jit(solution)/shard_map/all_to_all | solution.py:38
  165.2 0.1 mul.61
  165.3 1.0 bitcast_convert_fusion
  166.3 9.4 %fusion.18 = bf16[576,768]{1,0:T(8,128)(2,1)S(1)} fusion(bf16[1,768,4096]{2,1,0:T(8,128)(2,1)} %all-gather.2.cloned.1.call-done, bf16[72,8,32,128]{3,2,1,0:T(8,128)(2,1)} %bitcast.20), kind=kOutput, calls=%fused_computation.20 | convolution fusion | flops 3624321024 | bytes 11894784 | tf_op jit(solution)/shard_map/rd,fd->rf/dot_general | solution.py:71
  175.7 0.4 reshape.142
  176.1 1.2 copy.39
  177.3 95.2 %all-to-all-done = bf16[64,9,32,128]{3,2,1,0:T(8,128)(2,1)} async-done(((bf16[64,9,32,128]{3,2,1,0:T(8,128)(2,1)}), bf16[64,9,32,128]{3,2,1,0:T(8,128)(2,1)}, u32[]{:S(2)}, u32[]{:S(2)}) %all-to-all-start) | async-done | bytes 4718624 | tf_op jit(solution)/shard_map/all_to_all | solution.py:38
  272.5 3.6 %gather_fusion = bf16[384,32,128]{2,1,0:T(8,128)(2,1)S(1)} fusion(bf16[576,32,128]{2,1,0:T(8,128)(2,1)} %bitcast.1, s32[1024]{0:T(1024)S(1)} %pad_clamp_fusion.1), kind=kCustom, calls=%fused_computation | custom fusion | bytes 6292992 | tf_op jit(solution)/shard_map/gather | solution.py:45
  276.1 5.0 %fusion.2 = (f32[48,8]{1,0:T(8,128)}, bf16[48,32,128]{2,1,0:T(8,128)(2,1)S(1)}) fusion(bf16[48,8,32,128]{3,2,1,0:T(8,128)(2,1)S(1)} %bitcast.65, f32[48,32,128]{2,1,0:T(8,128)} %bitcast_convert_fusion, f32[48,8]{1,0:T(8,128)} %copy-done.1), kind=kLoop, calls=%fused_computation.8 | loop fusion | flops 7667328 | bytes 4328448 | tf_op jit(solution)/shard_map/reduce_sum | solution.py:50
  281.1 0.9 copy.58
  282.0 1.4 copy.38
  283.4 3.1 %copy.40 = f32[1,768,1024]{2,1,0:T(8,128)} copy(bf16[1,768,1024]{1,2,0:T(8,128)(2,1)} %reduce-scatter.2.cloned.1.call-done) | data formatting | bytes 4718592
  (22 shorter events, 0.6 us)
Async XLA Ops:
  7.2 73.4 %all-gather.2.cloned.1.call-start = ((), (), s32[]{:S(2)}) async-start(), calls=%async_computation.3 | async-start | bytes 7864320 | tf_op jit(solution)/shard_map/all_gather | solution.py:33
  11.9 4.7 %copy-start.1 = (f32[48,8]{1,0:T(8,128)}, f32[48,8]{1,0:T(8,128)S(1)}, u32[]{:S(2)}) copy-start(f32[48,8]{1,0:T(8,128)S(1)} %copy.31) | copy-start | bytes 4612
  21.0 12.3 %copy-start = (bf16[1,1,64,9,768]{4,2,3,1,0:T(8,128)(2,1)S(1)}, bf16[1,1,64,9,768]{4,2,3,1,0:T(8,128)(2,1)}, u32[]{:S(2)}) copy-start(bf16[1,1,64,9,768]{4,2,3,1,0:T(8,128)(2,1)} %param.7) | copy-start | bytes 2654212
  21.0 119.7 %all-to-all-start.1 = ((bf16[64,9,32,128]{3,2,1,0:T(8,128)(2,1)}), bf16[64,9,32,128]{3,2,1,0:T(8,128)(2,1)}, u32[]{:S(2)}, u32[]{:S(2)}) async-start(bf16[64,9,32,128]{3,2,1,0:T(8,128)(2,1)} %fusion), calls=%async_computation.1 | async-start | bytes 9437184 | tf_op jit(solution)/shard_map/all_to_all | solution.py:56
  33.3 250.2 %reduce-scatter.2.cloned.1.call-start = ((), (), s32[]{:S(2)}) async-start(), calls=%async_computation.4 | async-start | bytes 7864320 | tf_op jit(solution)/shard_map/reduce_scatter | solution.py:68
  159.2 5.9 %copy-start.2 = (s32[48,8]{0,1:T(8,128)S(1)}, s32[48,8]{0,1:T(8,128)}, u32[]{:S(2)}) copy-start(s32[48,8]{0,1:T(8,128)} %param.5) | copy-start | bytes 4612
  159.2 113.4 %all-to-all-start = ((bf16[64,9,32,128]{3,2,1,0:T(8,128)(2,1)}), bf16[64,9,32,128]{3,2,1,0:T(8,128)(2,1)}, u32[]{:S(2)}, u32[]{:S(2)}) async-start(bf16[64,9,32,128]{3,2,1,0:T(8,128)(2,1)} %bitcast.63), calls=%async_computation | async-start | bytes 9437184 | tf_op jit(solution)/shard_map/all_to_all | solution.py:38
Sparse Core Ops, SparseCore 0:
  9.8 70.6 all-gather.1
  159.3 61.4 reduce-scatter.1

commit v7 on v6

--- a/solution.py
+++ b/solution.py
@@ -62,12 +62,23 @@
     )
     arrived, _ = lax.optimization_barrier((arrived, outgoing))
     arrived = arrived.reshape(-1, model_width)
-    partial_value = jnp.einsum(
-        "rf,rd->fd", hidden_rows, arrived, preferred_element_type=jnp.float32
-    )[None]
-    weight_grad = lax.psum_scatter(
-        rounded_partial(partial_value).astype(jnp.bfloat16), "dp", scatter_dimension=2, tiled=True
-    ).astype(jnp.float32)
+    shard_count = lax.axis_size("dp")
+    quarter = model_width // shard_count
+    by_quarter = arrived.reshape(slot_count, shard_count, 2, quarter // 2)
+    weight_parts = []
+    for part in range(2):
+        partial_value = jnp.einsum(
+            "rf,rqd->fqd", hidden_rows, by_quarter[:, :, part], preferred_element_type=jnp.float32
+        )
+        weight_parts.append(
+            lax.psum_scatter(
+                rounded_partial(partial_value).astype(jnp.bfloat16),
+                "dp",
+                scatter_dimension=1,
+                tiled=True,
+            ).astype(jnp.float32)
+        )
+    weight_grad = jnp.concatenate(weight_parts, axis=2).reshape(1, hidden_width, quarter)
     hidden_total = jnp.einsum(
         "rd,fd->rf", arrived, gathered_weight, preferred_element_type=jnp.float32
     )

time: 294 us -> 297 us (1.010)
  local copies, waits for them, and re-layouts: 22.5 us -> 42.6 us
  waiting for transfers between devices: 192 us -> 179 us
  matrix products: 34.7 us -> 28.9 us
    all_to_all x1, waiting for transfers between devices: 95.2 us -> 29.8 us  [shards(): lax.all_to_all(outgoing, 'expert', split_axis=0, concat_axis=0, tiled=True)]
    reduce_scatter x1 -> x2, waiting for transfers between devices: 0.01 us -> 53.9 us  [shards(): lax.psum_scatter(rounded_partial(partial_value).astype(jnp.bfloat16), 'dp...]
    slice x1 -> x2, local copies, waits for them, and re-layouts: 0.22 us -> 11.3 us  [the longest x1 11.1 us: shards(): by_quarter[:, :, part]]
    another operation x0 -> x1, local copies, waits for them, and re-layouts: none -> 8.04 us  [shards(): by_quarter = arrived.reshape(slot_count, shard_count, 2, quarter // 2)]
    dot_general x1 -> x2, matrix products: 18.5 us -> 13.5 us  [shards(): jnp.einsum('rf,rqd->fqd', hidden_rows, by_quarter[:, :, part], preferred_...]
  transfers between devices with their start and end apart: 4 -> 5, of which waited for: 3 -> 5; matrix products, arithmetic and copies ran while one was open for 16% -> 17% of each run, Pallas kernels for 0% -> 0%
where the time goes in v7:
time: 297 us; the launch traced here: 296 us
  waiting for transfers between devices  179 us (60%)
  local copies, waits for them, and re-layouts  42.6 us (14%)
  matrix products  28.9 us (10%)
  starting transfers between devices  18.3 us (6%)
  between operations  13.9 us (5%)
  other arithmetic  13.4 us (5%)
    reduce_scatter x2, waiting for transfers between devices, shards(): lax.psum_scatter(rounded_partial(partial_value).astype(jnp.bfloat16), 'dp...  53.9 us
    all_to_all x1, waiting for transfers between devices, shards(): lax.all_to_all(scaled.reshape(expert_count, capacity, model_width // lane...  49.9 us
    all_gather x1, waiting for transfers between devices, shards(): gathered_weight = lax.all_gather(down_weight, 'dp', axis=2, tiled=True)[0]  44.6 us
    all_to_all x1, waiting for transfers between devices, shards(): lax.all_to_all(outgoing, 'expert', split_axis=0, concat_axis=0, tiled=True)  29.8 us
    dot_general x2, matrix products, shards(): jnp.einsum('rf,rqd->fqd', hidden_rows, by_quarter[:, :, part], preferred_...  13.5 us
    unnamed x15, local copies, waits for them, and re-layouts  13.2 us
    all_to_all x1, starting transfers between devices, shards(): lax.all_to_all(scaled.reshape(expert_count, capacity, model_width // lane...  12.3 us
    slice x1, local copies, waits for them, and re-layouts, shards(): by_quarter[:, :, part]  11.1 us
  transfers between devices with their start and end apart: 5, of which 5 were waited for; matrix products, arithmetic and copies ran while one was open for 17% of the time, Pallas kernels for 0%

profile of v7, /device:TPU:18, one launch (start us, length us, event | category | flops | bytes accessed | tf_op | source)
XLA Modules:
  0.0 296.1 jit_solution(14493841769985612619)
XLA Ops:
  7.2 0.7 all-gather.2.cloned.1.call-update
  7.9 0.8 copy.38
  8.8 0.8 copy.35
  9.7 0.5 copy-done.1
  10.2 0.9 reduce-window.6
  11.9 1.1 copy.52
  13.2 3.9 %gather_fusion.1 = bf16[576,32,128]{2,1,0:T(8,128)(2,1)} fusion(bf16[48,32,128]{2,1,0:T(8,128)(2,1)S(1)} %bitcast.78, s32[1024]{0:T(1024)S(1)} %pad_clamp_fusion), kind=kCustom, calls=%fused_computation.1 | custom fusion | bytes 9439488 | tf_op jit(solution)/shard_map/gather | solution.py:54
  17.1 4.3 %fusion = bf16[64,9,32,128]{3,2,1,0:T(8,128)(2,1)} fusion(bf16[64,9,32,128]{3,2,1,0:T(8,128)(2,1)} %bitcast.80, f32[64,9]{1,0:T(8,128)S(1)} %mul.68), kind=kLoop, calls=%fused_computation.3 | loop fusion | flops 7077888 | bytes 9439488 | tf_op jit(solution)/shard_map/convert_element_type | solution.py:55
  21.4 12.3 %all-to-all-start.1 = ((bf16[64,9,32,128]{3,2,1,0:T(8,128)(2,1)}), bf16[64,9,32,128]{3,2,1,0:T(8,128)(2,1)}, u32[]{:S(2)}, u32[]{:S(2)}) async-start(bf16[64,9,32,128]{3,2,1,0:T(8,128)(2,1)} %fusion), calls=%async_computation.1 | async-start | bytes 9437184 | tf_op jit(solution)/shard_map/all_to_all | solution.py:56
  33.7 0.5 copy.36
  34.7 1.2 reshape.142
  35.9 44.6 %all-gather.2.cloned.1.call-done = bf16[1,768,4096]{2,1,0:T(8,128)(2,1)} async-done(((bf16[1,768,1024]{2,1,0:T(8,128)(2,1)}), bf16[1,768,4096]{2,1,0:T(8,128)(2,1)}) %all-gather.2.cloned.1.call-update) | async-done | bytes 6291472 | tf_op jit(solution)/shard_map/all_gather | solution.py:33
  80.5 6.9 %fusion.14 = bf16[72,8,32,128]{3,1,2,0:T(8,128)(2,1)S(1)} fusion(bf16[576,768]{1,0:T(8,128)(2,1)} %reshape.142, bf16[1,768,4096]{2,1,0:T(8,128)(2,1)} %all-gather.2.cloned.1.call-done), kind=kOutput, calls=%fused_computation.21 | convolution fusion | flops 3626237952 | bytes 11894784 | tf_op jit(solution)/shard_map/dot_general | solution.py:34
  87.5 3.7 %copy.50 = bf16[72,8,32,128]{3,2,1,0:T(8,128)(2,1)} copy(bf16[72,8,32,128]{3,1,2,0:T(8,128)(2,1)S(1)} %fusion.14) | data formatting | bytes 9437184
  91.1 49.9 %all-to-all-done.1 = bf16[64,9,32,128]{3,2,1,0:T(8,128)(2,1)} async-done(((bf16[64,9,32,128]{3,2,1,0:T(8,128)(2,1)}), bf16[64,9,32,128]{3,2,1,0:T(8,128)(2,1)}, u32[]{:S(2)}, u32[]{:S(2)}) %all-to-all-start.1) | async-done | bytes 4718624 | tf_op jit(solution)/shard_map/all_to_all | solution.py:56
  141.1 8.0 %reshape_reshape.3 = bf16[576,4,2,512]{3,2,1,0:T(2,128)(2,1)} reshape(bf16[64,9,32,128]{3,2,1,0:T(8,128)(2,1)} %all-to-all-done.1) | data formatting | bytes 9437184 | tf_op jit(solution)/shard_map/reshape;reshape | solution.py:67
  149.1 11.1 %fusion.32 = (bf16[576,4,1,512]{3,2,1,0:T(2,128)(2,1)S(1)}, bf16[576,4,1,512]{3,2,1,0:T(2,128)(2,1)}) fusion(bf16[576,4,2,512]{3,2,1,0:T(2,128)(2,1)} %reshape_reshape.3), kind=kLoop, calls=%fused_computation.54 | loop fusion | bytes 9437184 | tf_op jit(solution)/shard_map/slice | solution.py:71
  160.2 5.1 %convert_bitcast_fusion.1 = bf16[768,4,512]{0,2,1:T(8,128)(2,1)} fusion(bf16[576,768,1]{1,0,2:T(8,128)(2,1)S(1)} %reshape.170, bf16[576,4,1,512]{3,2,1,0:T(2,128)(2,1)S(1)} %get-tuple-element.24), kind=kOutput, calls=%fused_computation.16 | convolution fusion | flops 1813512192 | bytes 6389760 | tf_op jit(solution)/shard_map/rf,rqd->fqd/dot_general | solution.py:70
  165.3 5.9 %all-to-all-start = ((bf16[64,9,32,128]{3,2,1,0:T(8,128)(2,1)}), bf16[64,9,32,128]{3,2,1,0:T(8,128)(2,1)}, u32[]{:S(2)}, u32[]{:S(2)}) async-start(bf16[64,9,32,128]{3,2,1,0:T(8,128)(2,1)} %bitcast.79), calls=%async_computation | async-start | bytes 9437184 | tf_op jit(solution)/shard_map/all_to_all | solution.py:38
  171.3 8.4 %convert_bitcast_fusion = bf16[768,4,512]{0,2,1:T(8,128)(2,1)} fusion(bf16[576,768,1]{1,0,2:T(8,128)(2,1)S(1)} %reshape.170, bf16[576,4,1,512]{3,2,1,0:T(2,128)(2,1)} %get-tuple-element.25), kind=kOutput, calls=%fused_computation.15 | convolution fusion | flops 1813512192 | bytes 6389760 | tf_op jit(solution)/shard_map/rf,rqd->fqd/dot_general | solution.py:70
  179.9 1.0 bitcast_convert_fusion
  180.9 8.6 %fusion.18 = bf16[576,768]{1,0:T(8,128)(2,1)S(1)} fusion(bf16[1,768,4096]{2,1,0:T(8,128)(2,1)} %all-gather.2.cloned.1.call-done, bf16[72,8,32,128]{3,2,1,0:T(8,128)(2,1)} %bitcast.23), kind=kOutput, calls=%fused_computation.24 | convolution fusion | flops 3624321024 | bytes 11894784 | tf_op jit(solution)/shard_map/rd,fd->rf/dot_general | solution.py:82
  189.9 1.2 copy.45
  191.1 10.1 %reduce-scatter.3.cloned.1.call-done = bf16[768,1,512]{0,2,1:T(8,128)(2,1)} async-done(((bf16[768,4,512]{0,2,1:T(8,128)(2,1)}), bf16[768,1,512]{0,2,1:T(8,128)(2,1)}) %reduce-scatter.3.cloned.1.call-update) | async-done | bytes 786448 | tf_op jit(solution)/shard_map/reduce_scatter | solution.py:74
  201.2 43.7 %reduce-scatter.5.cloned.1.call-done = bf16[768,1,512]{0,2,1:T(8,128)(2,1)} async-done(((bf16[768,4,512]{0,2,1:T(8,128)(2,1)}), bf16[768,1,512]{0,2,1:T(8,128)(2,1)}) %reduce-scatter.5.cloned.1.call-update) | async-done | bytes 786448 | tf_op jit(solution)/shard_map/reduce_scatter | solution.py:74
  244.9 1.6 fusion.17
  246.5 2.4 copy.46
  248.9 29.8 %all-to-all-done = bf16[64,9,32,128]{3,2,1,0:T(8,128)(2,1)} async-done(((bf16[64,9,32,128]{3,2,1,0:T(8,128)(2,1)}), bf16[64,9,32,128]{3,2,1,0:T(8,128)(2,1)}, u32[]{:S(2)}, u32[]{:S(2)}) %all-to-all-start) | async-done | bytes 4718624 | tf_op jit(solution)/shard_map/all_to_all | solution.py:38
  278.7 3.6 %gather_fusion = bf16[384,32,128]{2,1,0:T(8,128)(2,1)S(1)} fusion(bf16[576,32,128]{2,1,0:T(8,128)(2,1)} %bitcast.1, s32[1024]{0:T(1024)S(1)} %pad_clamp_fusion.1), kind=kCustom, calls=%fused_computation | custom fusion | bytes 6292992 | tf_op jit(solution)/shard_map/gather | solution.py:45
  282.3 5.0 %fusion.2 = (f32[48,8]{1,0:T(8,128)}, bf16[48,32,128]{2,1,0:T(8,128)(2,1)S(1)}) fusion(bf16[48,8,32,128]{3,2,1,0:T(8,128)(2,1)S(1)} %bitcast.81, f32[48,32,128]{2,1,0:T(8,128)} %bitcast_convert_fusion, f32[48,8]{1,0:T(8,128)} %copy-done.1), kind=kLoop, calls=%fused_computation.7 | loop fusion | flops 7667328 | bytes 4328448 | tf_op jit(solution)/shard_map/reduce_sum | solution.py:50
  287.3 1.4 copy.44
  288.7 0.9 copy.70
  (30 shorter events, 2.4 us)
Async XLA Ops:
  7.2 73.4 %all-gather.2.cloned.1.call-start = ((), (), s32[]{:S(2)}) async-start(), calls=%async_computation.4 | async-start | bytes 7864320 | tf_op jit(solution)/shard_map/all_gather | solution.py:33
  9.6 0.6 copy-start.1
  21.4 12.3 %copy-start = (bf16[1,1,64,9,768]{4,2,3,1,0:T(8,128)(2,1)S(1)}, bf16[1,1,64,9,768]{4,2,3,1,0:T(8,128)(2,1)}, u32[]{:S(2)}) copy-start(bf16[1,1,64,9,768]{4,2,3,1,0:T(8,128)(2,1)} %param.7) | copy-start | bytes 2654212
  21.4 119.7 %all-to-all-start.1 = ((bf16[64,9,32,128]{3,2,1,0:T(8,128)(2,1)}), bf16[64,9,32,128]{3,2,1,0:T(8,128)(2,1)}, u32[]{:S(2)}, u32[]{:S(2)}) async-start(bf16[64,9,32,128]{3,2,1,0:T(8,128)(2,1)} %fusion), calls=%async_computation.1 | async-start | bytes 9437184 | tf_op jit(solution)/shard_map/all_to_all | solution.py:56
  33.7 167.5 %reduce-scatter.3.cloned.1.call-start = ((), (), s32[]{:S(2)}) async-start(), calls=%async_computation.5 | async-start | bytes 3932160 | tf_op jit(solution)/shard_map/reduce_scatter | solution.py:74
  165.3 113.4 %all-to-all-start = ((bf16[64,9,32,128]{3,2,1,0:T(8,128)(2,1)}), bf16[64,9,32,128]{3,2,1,0:T(8,128)(2,1)}, u32[]{:S(2)}, u32[]{:S(2)}) async-start(bf16[64,9,32,128]{3,2,1,0:T(8,128)(2,1)} %bitcast.79), calls=%async_computation | async-start | bytes 9437184 | tf_op jit(solution)/shard_map/all_to_all | solution.py:38
  171.2 73.7 %reduce-scatter.5.cloned.1.call-start = ((), (), s32[]{:S(2)}) async-start(), calls=%async_computation.6 | async-start | bytes 3932160 | tf_op jit(solution)/shard_map/reduce_scatter | solution.py:74
  171.2 8.4 %copy-start.2 = (s32[48,8]{0,1:T(8,128)S(1)}, s32[48,8]{0,1:T(8,128)}, u32[]{:S(2)}) copy-start(s32[48,8]{0,1:T(8,128)} %param.5) | copy-start | bytes 4612
Sparse Core Ops, SparseCore 0:
  9.8 70.6 all-gather.1
  165.4 35.7 reduce-scatter.2
  204.3 40.5 reduce-scatter.4

commit v8 on v7

--- a/solution.py
+++ b/solution.py
@@ -50,8 +50,13 @@
     prob_grad = jnp.sum(
         grad_tiles[:, None].astype(jnp.float32) * route_out, axis=(2, 3)
     )
+    shard_count = lax.axis_size("dp")
+    quarter = model_width // shard_count
+    split = (shard_count, 2, quarter // 2 // lanes, lanes)
+    grad_mixed = out_grad.reshape((tok_count,) + split).transpose(0, 2, 1, 3, 4)
+    grad_mixed = grad_mixed.reshape(tok_count, model_width // lanes, lanes)
     scaled = (
-        slot_prob[:, None, None] * grad_tiles[slot_token].astype(jnp.float32)
+        slot_prob[:, None, None] * grad_mixed[slot_token].astype(jnp.float32)
     ).astype(jnp.bfloat16)
     arrived = lax.all_to_all(
         scaled.reshape(expert_count, capacity, model_width // lanes, lanes),
@@ -61,14 +66,15 @@
         tiled=True,
     )
     arrived, _ = lax.optimization_barrier((arrived, outgoing))
-    arrived = arrived.reshape(-1, model_width)
-    shard_count = lax.axis_size("dp")
-    quarter = model_width // shard_count
-    by_quarter = arrived.reshape(slot_count, shard_count, 2, quarter // 2)
+    arrived = arrived.reshape(slot_count, model_width // lanes, lanes)
+    half_tiles = model_width // lanes // 2
     weight_parts = []
     for part in range(2):
         partial_value = jnp.einsum(
-            "rf,rqd->fqd", hidden_rows, by_quarter[:, :, part], preferred_element_type=jnp.float32
+            "rf,rjl->fjl",
+            hidden_rows,
+            arrived[:, part * half_tiles : (part + 1) * half_tiles],
+            preferred_element_type=jnp.float32,
         )
         weight_parts.append(
             lax.psum_scatter(
@@ -78,9 +84,11 @@
                 tiled=True,
             ).astype(jnp.float32)
         )
-    weight_grad = jnp.concatenate(weight_parts, axis=2).reshape(1, hidden_width, quarter)
+    weight_grad = jnp.stack(weight_parts, axis=1).reshape(1, hidden_width, quarter)
+    weight_mixed = gathered_weight.reshape((hidden_width,) + split).transpose(0, 2, 1, 3, 4)
+    weight_mixed = weight_mixed.reshape(hidden_width, model_width // lanes, lanes)
     hidden_total = jnp.einsum(
-        "rd,fd->rf", arrived, gathered_weight, preferred_element_type=jnp.float32
+        "rjl,fjl->rf", arrived, weight_mixed, preferred_element_type=jnp.float32
     )
     hidden_grad = hidden_total.astype(jnp.bfloat16).reshape(expert_hidden.shape)
     return (layer_out, prob_grad, hidden_grad, weight_grad)

time: 297 us -> 280 us (0.943)
  waiting for transfers between devices: 179 us -> 168 us
  matrix products: 28.9 us -> 25.8 us
    reduce_scatter x2, waiting for transfers between devices: 53.9 us -> 41.7 us  [shards(): lax.psum_scatter(rounded_partial(partial_value).astype(jnp.bfloat16), 'dp...]
    slice x2 -> x1, local copies, waits for them, and re-layouts: 11.3 us -> 0.22 us  [the longest x1 11.1 us: shards(): by_quarter[:, :, part]]
    another operation x1 -> x2, local copies, waits for them, and re-layouts: 8.04 us -> 16.3 us  [shards(): gathered_weight.reshape((hidden_width,) + split).transpose(0, 2, 1, 3, 4)]
    dot_general x3, matrix products: 22 us -> 18.9 us  [the longest x2 12.4 us: shards(): jnp.einsum('rf,rjl->fjl', hidden_rows, arrived[:, part * half_tiles:(part...]
    unnamed x15 -> x17, local copies, waits for them, and re-layouts: 13.2 us -> 12.9 us
  transfers between devices with their start and end apart: 5 -> 5, of which waited for: 5 -> 4; matrix products, arithmetic and copies ran while one was open for 17% -> 22% of each run, Pallas kernels for 0% -> 0%
where the time goes in v8:
time: 280 us; the launch traced here: 279 us
  waiting for transfers between devices  168 us (60%)
  local copies, waits for them, and re-layouts  40.3 us (14%)
  matrix products  25.8 us (9%)
  starting transfers between devices  18.3 us (7%)
  between operations  13.9 us (5%)
  other arithmetic  12.4 us (4%)
    all_to_all x1, waiting for transfers between devices, shards(): lax.all_to_all(scaled.reshape(expert_count, capacity, model_width // lane...  50.6 us
    all_gather x1, waiting for transfers between devices, shards(): gathered_weight = lax.all_gather(down_weight, 'dp', axis=2, tiled=True)[0]  44.9 us
    reduce_scatter x2, waiting for transfers between devices, shards(): lax.psum_scatter(rounded_partial(partial_value).astype(jnp.bfloat16), 'dp...  41.7 us
    all_to_all x1, waiting for transfers between devices, shards(): lax.all_to_all(outgoing, 'expert', split_axis=0, concat_axis=0, tiled=True)  29.9 us
    another operation x2, local copies, waits for them, and re-layouts, shards(): gathered_weight.reshape((hidden_width,) + split).transpose(0, 2, 1, 3, 4)  16.3 us
    unnamed x17, local copies, waits for them, and re-layouts  12.9 us
    dot_general x2, matrix products, shards(): jnp.einsum('rf,rjl->fjl', hidden_rows, arrived[:, part * half_tiles:(part...  12.4 us
    all_to_all x1, starting transfers between devices, shards(): lax.all_to_all(scaled.reshape(expert_count, capacity, model_width // lane...  12.3 us
  transfers between devices with their start and end apart: 5, of which 4 were waited for; matrix products, arithmetic and copies ran while one was open for 22% of the time, Pallas kernels for 0%

profile of v8, /device:TPU:18, one launch (start us, length us, event | category | flops | bytes accessed | tf_op | source)
XLA Modules:
  0.0 278.6 jit_solution(2420135744037366940)
XLA Ops:
  7.2 0.7 all-gather.2.cloned.1.call-update
  7.9 0.8 copy.61
  8.8 0.8 copy.58
  9.7 0.5 copy-done.2
  10.2 0.9 reduce-window.6
  11.9 1.3 reshape.156
  13.6 3.9 %gather_fusion.1 = bf16[576,32,128]{2,1,0:T(8,128)(2,1)} fusion(bf16[48,32,128]{2,1,0:T(8,128)(2,1)S(1)} %copy.66, s32[1024]{0:T(1024)S(1)} %pad_clamp_fusion), kind=kCustom, calls=%fused_computation.1 | custom fusion | bytes 9439488 | tf_op jit(solution)/shard_map/gather | solution.py:59
  17.6 4.4 %fusion = bf16[64,9,32,128]{3,2,1,0:T(8,128)(2,1)} fusion(bf16[64,9,32,128]{3,2,1,0:T(8,128)(2,1)} %bitcast.64, f32[64,9]{1,0:T(8,128)S(1)} %mul.68), kind=kLoop, calls=%fused_computation.3 | loop fusion | flops 7077888 | bytes 9439488 | tf_op jit(solution)/shard_map/convert_element_type | solution.py:60
  21.9 12.3 %all-to-all-start.1 = ((bf16[64,9,32,128]{3,2,1,0:T(8,128)(2,1)}), bf16[64,9,32,128]{3,2,1,0:T(8,128)(2,1)}, u32[]{:S(2)}, u32[]{:S(2)}) async-start(bf16[64,9,32,128]{3,2,1,0:T(8,128)(2,1)} %fusion), calls=%async_computation.1 | async-start | bytes 9437184 | tf_op jit(solution)/shard_map/all_to_all | solution.py:61
  34.3 0.5 copy.59
  34.8 0.4 reshape.185
  35.2 0.4 reshape.152
  35.7 44.9 %all-gather.2.cloned.1.call-done = bf16[1,768,4096]{2,1,0:T(8,128)(2,1)} async-done(((bf16[1,768,1024]{2,1,0:T(8,128)(2,1)}), bf16[1,768,4096]{2,1,0:T(8,128)(2,1)}) %all-gather.2.cloned.1.call-update) | async-done | bytes 6291472 | tf_op jit(solution)/shard_map/all_gather | solution.py:33
  80.5 6.8 %fusion.14 = bf16[72,8,32,128]{3,1,2,0:T(8,128)(2,1)S(1)} fusion(bf16[576,768]{1,0:T(8,128)(2,1)S(1)} %reshape.152, bf16[1,768,4096]{2,1,0:T(8,128)(2,1)} %all-gather.2.cloned.1.call-done), kind=kOutput, calls=%fused_computation.19 | convolution fusion | flops 3626237952 | bytes 11894784 | tf_op jit(solution)/shard_map/dot_general | solution.py:34
  87.4 3.6 %copy.75 = bf16[72,8,32,128]{3,2,1,0:T(8,128)(2,1)} copy(bf16[72,8,32,128]{3,1,2,0:T(8,128)(2,1)S(1)} %fusion.14) | data formatting | bytes 9437184
  91.0 50.6 %all-to-all-done.1 = bf16[64,9,32,128]{3,2,1,0:T(8,128)(2,1)} async-done(((bf16[64,9,32,128]{3,2,1,0:T(8,128)(2,1)}), bf16[64,9,32,128]{3,2,1,0:T(8,128)(2,1)}, u32[]{:S(2)}, u32[]{:S(2)}) %all-to-all-start.1) | async-done | bytes 4718624 | tf_op jit(solution)/shard_map/all_to_all | solution.py:61
  141.6 6.3 %convert_bitcast_fusion.1 = bf16[768,16,128]{0,2,1:T(8,128)(2,1)} fusion(bf16[576,768,1]{1,0,2:T(8,128)(2,1)S(1)} %reshape.185, bf16[576,32,128]{2,1,0:T(8,128)(2,1)} %bitcast.8), kind=kOutput, calls=%fused_computation.18 | convolution fusion | flops 1813512192 | bytes 8749056 | tf_op jit(solution)/shard_map/rf,rjl->fjl/dot_general | solution.py:73
  148.0 5.7 %all-to-all-start = ((bf16[64,9,32,128]{3,2,1,0:T(8,128)(2,1)}), bf16[64,9,32,128]{3,2,1,0:T(8,128)(2,1)}, u32[]{:S(2)}, u32[]{:S(2)}) async-start(bf16[64,9,32,128]{3,2,1,0:T(8,128)(2,1)} %bitcast.63), calls=%async_computation | async-start | bytes 9437184 | tf_op jit(solution)/shard_map/all_to_all | solution.py:38
  153.9 6.1 %convert_bitcast_fusion = bf16[768,16,128]{0,2,1:T(8,128)(2,1)} fusion(bf16[576,768,1]{1,0,2:T(8,128)(2,1)S(1)} %reshape.185, bf16[576,32,128]{2,1,0:T(8,128)(2,1)} %bitcast.8), kind=kOutput, calls=%fused_computation.17 | convolution fusion | flops 1813512192 | bytes 8749056 | tf_op jit(solution)/shard_map/rf,rjl->fjl/dot_general | solution.py:73
  160.3 1.1 copy.77
  161.4 11.1 %reshape_squeeze.3 = bf16[768,4,2,4,128]{4,3,2,1,0:T(4,128)(2,1)} reshape(bf16[1,768,4096]{2,1,0:T(8,128)(2,1)} %all-gather.2.cloned.1.call-done) | data formatting | bytes 12582912 | tf_op jit(solution)/shard_map/reshape;squeeze | solution.py:88
  172.5 5.3 %copy.67 = bf16[768,4,2,4,128]{4,0,3,1,2:T(8,128)(2,1)S(1)} copy(bf16[768,4,2,4,128]{4,3,2,1,0:T(4,128)(2,1)} %reshape_squeeze.3) | data formatting | bytes 12582912 | tf_op jit(solution)/shard_map/reshape;squeeze | solution.py:88
  177.8 6.5 %bitcast_convert_fusion = bf16[576,768]{1,0:T(8,128)(2,1)S(1)} fusion(bf16[768,32,128]{2,0,1:T(8,128)(2,1)S(1)} %bitcast.66, bf16[576,32,128]{2,1,0:T(8,128)(2,1)} %bitcast.8), kind=kOutput, calls=%fused_computation.20 | convolution fusion | flops 3624321024 | bytes 11894784 | tf_op jit(solution)/shard_map/rjl,fjl->rf/dot_general | solution.py:90
  184.7 1.2 copy.72
  185.9 41.7 %reduce-scatter.5.cloned.1.call-done = bf16[768,4,128]{0,2,1:T(8,128)(2,1)} async-done(((bf16[768,16,128]{0,2,1:T(8,128)(2,1)}), bf16[768,4,128]{0,2,1:T(8,128)(2,1)}) %reduce-scatter.5.cloned.1.call-update) | async-done | bytes 786448 | tf_op jit(solution)/shard_map/reduce_scatter | solution.py:80
  227.6 1.5 pad_maximum_fusion
  229.1 2.1 copy.73
  231.2 29.9 %all-to-all-done = bf16[64,9,32,128]{3,2,1,0:T(8,128)(2,1)} async-done(((bf16[64,9,32,128]{3,2,1,0:T(8,128)(2,1)}), bf16[64,9,32,128]{3,2,1,0:T(8,128)(2,1)}, u32[]{:S(2)}, u32[]{:S(2)}) %all-to-all-start) | async-done | bytes 4718624 | tf_op jit(solution)/shard_map/all_to_all | solution.py:38
  261.2 3.6 %gather_fusion = bf16[384,32,128]{2,1,0:T(8,128)(2,1)S(1)} fusion(bf16[576,32,128]{2,1,0:T(8,128)(2,1)} %bitcast.1, s32[1024]{0:T(1024)S(1)} %pad_clamp_fusion.1), kind=kCustom, calls=%fused_computation | custom fusion | bytes 6292992 | tf_op jit(solution)/shard_map/gather | solution.py:45
  264.8 5.0 %fusion.2 = (f32[48,8]{1,0:T(8,128)}, bf16[48,32,128]{2,1,0:T(8,128)(2,1)S(1)}) fusion(bf16[48,8,32,128]{3,2,1,0:T(8,128)(2,1)S(1)} %bitcast.65, f32[48,32,128]{2,1,0:T(8,128)} %bitcast.68, f32[48,8]{1,0:T(8,128)} %copy-done.2), kind=kLoop, calls=%fused_computation.7 | loop fusion | flops 7667328 | bytes 4328448 | tf_op jit(solution)/shard_map/reduce_sum | solution.py:50
  269.8 1.4 copy.71
  271.2 0.9 copy.92
  (35 shorter events, 2.4 us)
Async XLA Ops:
  7.2 73.4 %all-gather.2.cloned.1.call-start = ((), (), s32[]{:S(2)}) async-start(), calls=%async_computation.4 | async-start | bytes 7864320 | tf_op jit(solution)/shard_map/all_gather | solution.py:33
  9.6 0.6 copy-start.2
  21.9 12.3 %copy-start.1 = (bf16[1,1,64,9,768]{4,2,3,1,0:T(8,128)(2,1)S(1)}, bf16[1,1,64,9,768]{4,2,3,1,0:T(8,128)(2,1)}, u32[]{:S(2)}) copy-start(bf16[1,1,64,9,768]{4,2,3,1,0:T(8,128)(2,1)} %param.7) | copy-start | bytes 2654212
  21.9 119.7 %all-to-all-start.1 = ((bf16[64,9,32,128]{3,2,1,0:T(8,128)(2,1)}), bf16[64,9,32,128]{3,2,1,0:T(8,128)(2,1)}, u32[]{:S(2)}, u32[]{:S(2)}) async-start(bf16[64,9,32,128]{3,2,1,0:T(8,128)(2,1)} %fusion), calls=%async_computation.1 | async-start | bytes 9437184 | tf_op jit(solution)/shard_map/all_to_all | solution.py:61
  34.2 151.7 %reduce-scatter.3.cloned.1.call-start = ((), (), s32[]{:S(2)}) async-start(), calls=%async_computation.5 | async-start | bytes 3932160 | tf_op jit(solution)/shard_map/reduce_scatter | solution.py:80
  148.0 113.2 %all-to-all-start = ((bf16[64,9,32,128]{3,2,1,0:T(8,128)(2,1)}), bf16[64,9,32,128]{3,2,1,0:T(8,128)(2,1)}, u32[]{:S(2)}, u32[]{:S(2)}) async-start(bf16[64,9,32,128]{3,2,1,0:T(8,128)(2,1)} %bitcast.63), calls=%async_computation | async-start | bytes 9437184 | tf_op jit(solution)/shard_map/all_to_all | solution.py:38
  153.7 6.4 %copy-start.3 = (s32[48,8]{0,1:T(8,128)S(1)}, s32[48,8]{0,1:T(8,128)}, u32[]{:S(2)}) copy-start(s32[48,8]{0,1:T(8,128)} %param.5) | copy-start | bytes 4612
  153.7 6.6 %copy-start = (bf16[48,4096]{1,0:T(8,128)(2,1)S(1)}, bf16[48,4096]{1,0:T(8,128)(2,1)}, u32[]{:S(2)}) copy-start(bf16[48,4096]{1,0:T(8,128)(2,1)} %param.9) | copy-start | bytes 1179652
  153.7 73.9 %reduce-scatter.5.cloned.1.call-start = ((), (), s32[]{:S(2)}) async-start(), calls=%async_computation.6 | async-start | bytes 3932160 | tf_op jit(solution)/shard_map/reduce_scatter | solution.py:80
Sparse Core Ops, SparseCore 0:
  9.8 70.6 all-gather.1
  148.1 35.7 reduce-scatter.2
  187.0 40.5 reduce-scatter.4

commit v9 on v8

--- a/solution.py
+++ b/solution.py
@@ -1,7 +1,64 @@
+import functools
+
 import jax
 import jax.numpy as jnp
 from jax import lax
+from jax.experimental import pallas as pl
+from jax.experimental.pallas import tpu as pltpu
 from jax.sharding import PartitionSpec as P
+
+
+def combine_kernel(top, index_ref, prob_ref, rows_hbm, grad_ref, layer_ref, dots_ref, held, sems):
+    routes = held.shape[0]
+
+    def fetch(i):
+        return pltpu.make_async_copy(rows_hbm.at[index_ref[i]], held.at[i], sems.at[i])
+
+    def start(i, carry):
+        fetch(i).start()
+        return carry
+
+    lax.fori_loop(0, routes, start, 0)
+
+    def finish(i, carry):
+        fetch(i).wait()
+        return carry
+
+    lax.fori_loop(0, routes, finish, 0)
+
+    def token(t, carry):
+        grad = grad_ref[t].astype(jnp.float32)
+        total = jnp.zeros(grad.shape, jnp.float32)
+        for k in range(top):
+            row = held[t * top + k].astype(jnp.float32)
+            total = total + prob_ref[t * top + k] * row
+            dots_ref[t * top + k] = jnp.sum(grad * row, axis=0, keepdims=True)
+        layer_ref[t] = total.astype(layer_ref.dtype)
+        return carry
+
+    lax.fori_loop(0, grad_ref.shape[0], token, 0)
+
+
+def combine(slot_index, probs, rows, grad_tiles):
+    tokens, tiles, lanes = grad_tiles.shape
+    routes = slot_index.shape[0]
+    top = routes // tokens
+    smem = pl.BlockSpec(memory_space=pltpu.SMEM)
+    vmem = pl.BlockSpec(memory_space=pltpu.VMEM)
+    layer, dots = pl.pallas_call(
+        functools.partial(combine_kernel, top),
+        out_shape=(
+            jax.ShapeDtypeStruct((tokens, tiles, lanes), jnp.bfloat16),
+            jax.ShapeDtypeStruct((routes, 1, lanes), jnp.float32),
+        ),
+        in_specs=[smem, smem, pl.BlockSpec(memory_space=pl.ANY), vmem],
+        out_specs=(vmem, vmem),
+        scratch_shapes=[
+            pltpu.VMEM((routes, tiles, lanes), rows.dtype),
+            pltpu.SemaphoreType.DMA((routes,)),
+        ],
+    )(slot_index, probs, rows, grad_tiles)
+    return layer, jnp.sum(dots, axis=(1, 2)).reshape(tokens, top)
 
 
 def rounded_partial(values):
@@ -42,14 +99,13 @@
         concat_axis=0,
         tiled=True,
     )
-    route_out = returned.reshape(slot_count, model_width // lanes, lanes)[slot_index].reshape(
-        tok_count, top_count, model_width // lanes, lanes
-    ).astype(jnp.float32)
-    layer_out = jnp.sum(route_probs[:, :, None, None] * route_out, axis=1)
-    layer_out = layer_out.astype(jnp.bfloat16).reshape(tok_count, model_width)
-    prob_grad = jnp.sum(
-        grad_tiles[:, None].astype(jnp.float32) * route_out, axis=(2, 3)
+    layer_out, prob_grad = combine(
+        slot_index,
+        route_probs.reshape(-1),
+        returned.reshape(slot_count, model_width // lanes, lanes),
+        grad_tiles,
     )
+    layer_out = layer_out.reshape(tok_count, model_width)
     shard_count = lax.axis_size("dp")
     quarter = model_width // shard_count
     split = (shard_count, 2, quarter // 2 // lanes, lanes)

time: 280 us -> 285 us (1.018)
  Pallas kernels: 0 us -> 12.2 us
  local copies, waits for them, and re-layouts: 40.3 us -> 36.2 us
  other arithmetic: 12.4 us -> 9.36 us
    pallas_call x0 -> x1, Pallas kernels: none -> 12.2 us  [combine(): pl.pallas_call(functools.partial(combine_kernel, top), out_shape=(jax.Sha...]
    gather x1 -> x0, local copies, waits for them, and re-layouts: 3.58 us -> none  [shards(): returned.reshape(slot_count, model_width // lanes, lanes)[slot_index]]
    reduce_sum x1, other arithmetic: 5.01 us -> 1.96 us  [combine(): return (layer, jnp.sum(dots, axis=(1, 2)).reshape(tokens, top))]
  transfers between devices with their start and end apart: 5 -> 5, of which waited for: 4 -> 4; matrix products, arithmetic and copies ran while one was open for 22% -> 21% of each run, Pallas kernels for 0% -> 0%
where the time goes in v9:
time: 285 us; the launch traced here: 284 us
  waiting for transfers between devices  168 us (59%)
  local copies, waits for them, and re-layouts  36.2 us (13%)
  matrix products  25.8 us (9%)
  starting transfers between devices  18.3 us (6%)
  between operations  13.9 us (5%)
  Pallas kernels  12.2 us (4%)
  other arithmetic  9.36 us (3%)
    all_to_all x1, waiting for transfers between devices, shards(): lax.all_to_all(scaled.reshape(expert_count, capacity, model_width // lane...  50.2 us
    all_gather x1, waiting for transfers between devices, shards(): gathered_weight = lax.all_gather(down_weight, 'dp', axis=2, tiled=True)[0]  45.3 us
    reduce_scatter x2, waiting for transfers between devices, shards(): lax.psum_scatter(rounded_partial(partial_value).astype(jnp.bfloat16), 'dp...  42.3 us
    all_to_all x1, waiting for transfers between devices, shards(): lax.all_to_all(outgoing, 'expert', split_axis=0, concat_axis=0, tiled=True)  29.9 us
    another operation x2, local copies, waits for them, and re-layouts, shards(): gathered_weight.reshape((hidden_width,) + split).transpose(0, 2, 1, 3, 4)  16.3 us
    dot_general x2, matrix products, shards(): jnp.einsum('rf,rjl->fjl', hidden_rows, arrived[:, part * half_tiles:(part...  12.4 us
    unnamed x17, local copies, waits for them, and re-layouts  12.4 us
    all_to_all x1, starting transfers between devices, shards(): lax.all_to_all(scaled.reshape(expert_count, capacity, model_width // lane...  12.3 us
  transfers between devices with their start and end apart: 5, of which 4 were waited for; matrix products, arithmetic and copies ran while one was open for 21% of the time, Pallas kernels for 0%

profile of v9, /device:TPU:18, one launch (start us, length us, event | category | flops | bytes accessed | tf_op | source)
XLA Modules:
  0.0 284.1 jit_solution(4000732769300574742)
XLA Ops:
  7.2 0.7 all-gather.2.cloned.1.call-update
  7.9 0.8 copy.39
  8.9 0.9 reduce-window.6
  10.2 0.8 copy.42
  11.4 1.3 reshape.121
  13.1 3.9 %gather_fusion = bf16[576,32,128]{2,1,0:T(8,128)(2,1)} fusion(bf16[48,32,128]{2,1,0:T(8,128)(2,1)S(1)} %copy.45, s32[1024]{0:T(1024)S(1)} %pad_clamp_fusion), kind=kCustom, calls=%fused_computation | custom fusion | bytes 9439488 | tf_op jit(solution)/shard_map/gather | solution.py:115
  17.1 4.4 %fusion = bf16[64,9,32,128]{3,2,1,0:T(8,128)(2,1)} fusion(bf16[64,9,32,128]{3,2,1,0:T(8,128)(2,1)} %bitcast.61, f32[64,9]{1,0:T(8,128)S(1)} %mul.27), kind=kLoop, calls=%fused_computation.2 | loop fusion | flops 7077888 | bytes 9439488 | tf_op jit(solution)/shard_map/convert_element_type | solution.py:116
  21.5 12.3 %all-to-all-start.1 = ((bf16[64,9,32,128]{3,2,1,0:T(8,128)(2,1)}), bf16[64,9,32,128]{3,2,1,0:T(8,128)(2,1)}, u32[]{:S(2)}, u32[]{:S(2)}) async-start(bf16[64,9,32,128]{3,2,1,0:T(8,128)(2,1)} %fusion), calls=%async_computation.1 | async-start | bytes 9437184 | tf_op jit(solution)/shard_map/all_to_all | solution.py:117
  33.8 0.5 copy.43
  34.4 0.4 reshape.140
  34.8 0.4 reshape.115
  35.2 45.3 %all-gather.2.cloned.1.call-done = bf16[1,768,4096]{2,1,0:T(8,128)(2,1)} async-done(((bf16[1,768,1024]{2,1,0:T(8,128)(2,1)}), bf16[1,768,4096]{2,1,0:T(8,128)(2,1)}) %all-gather.2.cloned.1.call-update) | async-done | bytes 6291472 | tf_op jit(solution)/shard_map/all_gather | solution.py:90
  80.5 6.8 %fusion.12 = bf16[72,8,32,128]{3,1,2,0:T(8,128)(2,1)S(1)} fusion(bf16[576,768]{1,0:T(8,128)(2,1)S(1)} %reshape.115, bf16[1,768,4096]{2,1,0:T(8,128)(2,1)} %all-gather.2.cloned.1.call-done), kind=kOutput, calls=%fused_computation.14 | convolution fusion | flops 3626237952 | bytes 11894784 | tf_op jit(solution)/shard_map/dot_general | solution.py:91
  87.4 3.6 %copy.54 = bf16[72,8,32,128]{3,2,1,0:T(8,128)(2,1)} copy(bf16[72,8,32,128]{3,1,2,0:T(8,128)(2,1)S(1)} %fusion.12) | data formatting | bytes 9437184
  91.0 50.2 %all-to-all-done.1 = bf16[64,9,32,128]{3,2,1,0:T(8,128)(2,1)} async-done(((bf16[64,9,32,128]{3,2,1,0:T(8,128)(2,1)}), bf16[64,9,32,128]{3,2,1,0:T(8,128)(2,1)}, u32[]{:S(2)}, u32[]{:S(2)}) %all-to-all-start.1) | async-done | bytes 4718624 | tf_op jit(solution)/shard_map/all_to_all | solution.py:117
  141.2 6.3 %convert_bitcast_fusion.1 = bf16[768,16,128]{0,2,1:T(8,128)(2,1)} fusion(bf16[576,768,1]{1,0,2:T(8,128)(2,1)S(1)} %reshape.140, bf16[576,32,128]{2,1,0:T(8,128)(2,1)} %bitcast.6), kind=kOutput, calls=%fused_computation.13 | convolution fusion | flops 1813512192 | bytes 8749056 | tf_op jit(solution)/shard_map/rf,rjl->fjl/dot_general | solution.py:129
  147.5 5.7 %all-to-all-start = ((bf16[64,9,32,128]{3,2,1,0:T(8,128)(2,1)}), bf16[64,9,32,128]{3,2,1,0:T(8,128)(2,1)}, u32[]{:S(2)}, u32[]{:S(2)}) async-start(bf16[64,9,32,128]{3,2,1,0:T(8,128)(2,1)} %bitcast.60), calls=%async_computation | async-start | bytes 9437184 | tf_op jit(solution)/shard_map/all_to_all | solution.py:95
  153.5 6.1 %convert_bitcast_fusion = bf16[768,16,128]{0,2,1:T(8,128)(2,1)} fusion(bf16[576,768,1]{1,0,2:T(8,128)(2,1)S(1)} %reshape.140, bf16[576,32,128]{2,1,0:T(8,128)(2,1)} %bitcast.6), kind=kOutput, calls=%fused_computation.12 | convolution fusion | flops 1813512192 | bytes 8749056 | tf_op jit(solution)/shard_map/rf,rjl->fjl/dot_general | solution.py:129
  159.6 0.8 copy.55
  160.4 11.1 %reshape_squeeze.3 = bf16[768,4,2,4,128]{4,3,2,1,0:T(4,128)(2,1)} reshape(bf16[1,768,4096]{2,1,0:T(8,128)(2,1)} %all-gather.2.cloned.1.call-done) | data formatting | bytes 12582912 | tf_op jit(solution)/shard_map/reshape;squeeze | solution.py:144
  171.5 5.3 %copy.46 = bf16[768,4,2,4,128]{4,0,3,1,2:T(8,128)(2,1)S(1)} copy(bf16[768,4,2,4,128]{4,3,2,1,0:T(4,128)(2,1)} %reshape_squeeze.3) | data formatting | bytes 12582912 | tf_op jit(solution)/shard_map/reshape;squeeze | solution.py:144
  176.8 6.5 %bitcast_convert_fusion = bf16[576,768]{1,0:T(8,128)(2,1)S(1)} fusion(bf16[768,32,128]{2,0,1:T(8,128)(2,1)S(1)} %bitcast.62, bf16[576,32,128]{2,1,0:T(8,128)(2,1)} %bitcast.6), kind=kOutput, calls=%fused_computation.15 | convolution fusion | flops 3624321024 | bytes 11894784 | tf_op jit(solution)/shard_map/rjl,fjl->rf/dot_general | solution.py:146
  183.3 0.4 reshape.125
  183.7 1.2 copy.51
  184.9 42.3 %reduce-scatter.5.cloned.1.call-done = bf16[768,4,128]{0,2,1:T(8,128)(2,1)} async-done(((bf16[768,16,128]{0,2,1:T(8,128)(2,1)}), bf16[768,4,128]{0,2,1:T(8,128)(2,1)}) %reduce-scatter.5.cloned.1.call-update) | async-done | bytes 786448 | tf_op jit(solution)/shard_map/reduce_scatter | solution.py:136
  227.2 1.5 pad_maximum_fusion
  228.7 2.1 copy.52
  230.8 29.9 %all-to-all-done = bf16[64,9,32,128]{3,2,1,0:T(8,128)(2,1)} async-done(((bf16[64,9,32,128]{3,2,1,0:T(8,128)(2,1)}), bf16[64,9,32,128]{3,2,1,0:T(8,128)(2,1)}, u32[]{:S(2)}, u32[]{:S(2)}) %all-to-all-start) | async-done | bytes 4718624 | tf_op jit(solution)/shard_map/all_to_all | solution.py:95
  260.7 12.2 %shard_map.84 = (bf16[48,32,128]{2,1,0:T(8,128)(2,1)}, f32[384,1,128]{2,1,0:T(1,128)}) custom-call(s32[384]{0:T(512)} %copy-done.2, f32[384]{0:T(512)} %copy-done.3, bf16[576,32,128]{2,1,0:T(8,128)(2,1)} %bitcast.2.rows_hbm, bf16[48,32,128]{2,1,0:T(8,128)(2,1)} %bitcast.65), custom_call_target="tpu_custom_call" | custom-call | tf_op jit(solution)/shard_map/pallas_call | solution.py:48
  272.9 1.9 copy.71
  274.8 2.0 reduce_sum.39
  276.9 0.7 copy.50
  (31 shorter events, 1.9 us)
Async XLA Ops:
  7.2 73.4 %all-gather.2.cloned.1.call-start = ((), (), s32[]{:S(2)}) async-start(), calls=%async_computation.4 | async-start | bytes 7864320 | tf_op jit(solution)/shard_map/all_gather | solution.py:90
  10.2 6.9 %copy-start.2 = (s32[384]{0:T(512)}, s32[384]{0:T(512)S(1)}, u32[]{:S(2)}) copy-start(s32[384]{0:T(512)S(1)} %multiply_add_fusion.index_ref) | copy-start | bytes 4612
  11.0 6.0 %copy-start.3 = (f32[384]{0:T(512)}, f32[384]{0:T(512)S(1)}, u32[]{:S(2)}) copy-start(f32[384]{0:T(512)S(1)} %reshape.114.prob_ref) | copy-start | bytes 4612
  21.5 12.3 %copy-start.1 = (bf16[1,1,64,9,768]{4,2,3,1,0:T(8,128)(2,1)S(1)}, bf16[1,1,64,9,768]{4,2,3,1,0:T(8,128)(2,1)}, u32[]{:S(2)}) copy-start(bf16[1,1,64,9,768]{4,2,3,1,0:T(8,128)(2,1)} %param.7) | copy-start | bytes 2654212
  21.5 119.7 %all-to-all-start.1 = ((bf16[64,9,32,128]{3,2,1,0:T(8,128)(2,1)}), bf16[64,9,32,128]{3,2,1,0:T(8,128)(2,1)}, u32[]{:S(2)}, u32[]{:S(2)}) async-start(bf16[64,9,32,128]{3,2,1,0:T(8,128)(2,1)} %fusion), calls=%async_computation.1 | async-start | bytes 9437184 | tf_op jit(solution)/shard_map/all_to_all | solution.py:117
  33.8 151.1 %reduce-scatter.3.cloned.1.call-start = ((), (), s32[]{:S(2)}) async-start(), calls=%async_computation.5 | async-start | bytes 3932160 | tf_op jit(solution)/shard_map/reduce_scatter | solution.py:136
  147.5 113.2 %all-to-all-start = ((bf16[64,9,32,128]{3,2,1,0:T(8,128)(2,1)}), bf16[64,9,32,128]{3,2,1,0:T(8,128)(2,1)}, u32[]{:S(2)}, u32[]{:S(2)}) async-start(bf16[64,9,32,128]{3,2,1,0:T(8,128)(2,1)} %bitcast.60), calls=%async_computation | async-start | bytes 9437184 | tf_op jit(solution)/shard_map/all_to_all | solution.py:95
  153.3 6.4 %copy-start = (bf16[48,4096]{1,0:T(8,128)(2,1)S(1)}, bf16[48,4096]{1,0:T(8,128)(2,1)}, u32[]{:S(2)}) copy-start(bf16[48,4096]{1,0:T(8,128)(2,1)} %param.9) | copy-start | bytes 1179652
  153.3 73.9 %reduce-scatter.5.cloned.1.call-start = ((), (), s32[]{:S(2)}) async-start(), calls=%async_computation.6 | async-start | bytes 3932160 | tf_op jit(solution)/shard_map/reduce_scatter | solution.py:136
Sparse Core Ops, SparseCore 0:
  9.8 70.6 all-gather.1
  147.7 35.7 reduce-scatter.2
  186.6 40.5 reduce-scatter.4

commit v10 on v8

--- a/solution.py
+++ b/solution.py
@@ -24,9 +24,6 @@
     position = jnp.sum(earlier * onehot, axis=1)
     slot_index = flat_ids * capacity + position
     holds = slot_index[None, :] == jnp.arange(slot_count, dtype=jnp.int32)[:, None]
-    route_token = jnp.arange(tok_count * top_count, dtype=jnp.int32) // top_count
-    slot_token = jnp.sum(jnp.where(holds, route_token[None, :], 0), axis=1)
-    slot_prob = jnp.sum(jnp.where(holds, route_probs.reshape(-1)[None, :], jnp.float32(0.0)), axis=1)
     hidden_rows = expert_hidden.reshape(-1, hidden_width)
     lanes = 128
     grad_tiles = out_grad.reshape(tok_count, model_width // lanes, lanes)
@@ -54,10 +51,16 @@
     quarter = model_width // shard_count
     split = (shard_count, 2, quarter // 2 // lanes, lanes)
     grad_mixed = out_grad.reshape((tok_count,) + split).transpose(0, 2, 1, 3, 4)
-    grad_mixed = grad_mixed.reshape(tok_count, model_width // lanes, lanes)
-    scaled = (
-        slot_prob[:, None, None] * grad_mixed[slot_token].astype(jnp.float32)
-    ).astype(jnp.bfloat16)
+    grad_mixed = grad_mixed.reshape(tok_count, model_width).astype(jnp.float32)
+    dispatch = jnp.sum(
+        jnp.where(
+            holds.reshape(slot_count, tok_count, top_count),
+            route_probs[None],
+            jnp.float32(0.0),
+        ),
+        axis=2,
+    )
+    scaled = jnp.dot(dispatch, grad_mixed, precision=lax.Precision.HIGHEST).astype(jnp.bfloat16)
     arrived = lax.all_to_all(
         scaled.reshape(expert_count, capacity, model_width // lanes, lanes),
         "expert",

time: 280 us -> 279 us (level)
  other arithmetic: 12.4 us -> 8.07 us
  matrix products: 25.8 us -> 29.9 us
    convert_element_type x1 -> x0, other arithmetic: 4.36 us -> none  [shards(): scaled = (slot_prob[:, None, None] * grad_mixed[slot_token].astype(jnp.fl...]
    dot_general x0 -> x1, matrix products: none -> 4.15 us  [shards(): jnp.dot(dispatch, grad_mixed, precision=lax.Precision.HIGHEST)]
    gather x1 -> x0, local copies, waits for them, and re-layouts: 3.93 us -> none  [shards(): grad_mixed[slot_token].astype(jnp.float32)]
    unnamed x17 -> x16, local copies, waits for them, and re-layouts: 12.9 us -> 16 us
where the time goes in v10:
time: 279 us; the launch traced here: 278 us
  waiting for transfers between devices  168 us (60%)
  local copies, waits for them, and re-layouts  39.4 us (14%)
  matrix products  29.9 us (11%)
  starting transfers between devices  18.3 us (7%)
  between operations  13.9 us (5%)
  other arithmetic  8.07 us (3%)
    all_to_all x1, waiting for transfers between devices, shards(): lax.all_to_all(scaled.reshape(expert_count, capacity, model_width // lane...  49.6 us
    all_gather x1, waiting for transfers between devices, shards(): gathered_weight = lax.all_gather(down_weight, 'dp', axis=2, tiled=True)[0]  45.9 us
    reduce_scatter x2, waiting for transfers between devices, shards(): lax.psum_scatter(rounded_partial(partial_value).astype(jnp.bfloat16), 'dp...  41.8 us
    all_to_all x1, waiting for transfers between devices, shards(): lax.all_to_all(outgoing, 'expert', split_axis=0, concat_axis=0, tiled=True)  30.1 us
    another operation x2, local copies, waits for them, and re-layouts, shards(): gathered_weight.reshape((hidden_width,) + split).transpose(0, 2, 1, 3, 4)  16.4 us
    unnamed x16, local copies, waits for them, and re-layouts  16 us
    dot_general x2, matrix products, shards(): jnp.einsum('rf,rjl->fjl', hidden_rows, arrived[:, part * half_tiles:(part...  12.5 us
    all_to_all x1, starting transfers between devices, shards(): lax.all_to_all(scaled.reshape(expert_count, capacity, model_width // lane...  12.3 us
  transfers between devices with their start and end apart: 5, of which 4 were waited for; matrix products, arithmetic and copies ran while one was open for 22% of the time, Pallas kernels for 0%

profile of v10, /device:TPU:18, one launch (start us, length us, event | category | flops | bytes accessed | tf_op | source)
XLA Modules:
  0.0 277.8 jit_solution(3335107304829169578)
XLA Ops:
  7.2 0.7 all-gather.2.cloned.1.call-update
  7.9 0.8 copy.47
  8.8 0.8 copy.45
  9.6 0.9 reduce-window.6
  11.0 1.3 reshape.135
  13.1 4.2 %fusion.16 = bf16[72,8,32,128]{3,1,2,0:T(8,128)(2,1)S(1)} fusion(f32[576,48]{0,1:T(8,128)S(1)} %select_reduce_fusion, bf16[48,4096]{1,0:T(8,128)(2,1)S(1)} %reshape.136), kind=kOutput, calls=%fused_computation.18 | convolution fusion | flops 1361313792 | bytes 5222400 | tf_op jit(solution)/shard_map/dot_general | solution.py:63
  17.3 3.6 %copy.64 = bf16[72,8,32,128]{3,2,1,0:T(8,128)(2,1)} copy(bf16[72,8,32,128]{3,1,2,0:T(8,128)(2,1)S(1)} %fusion.16) | data formatting | bytes 9437184
  20.9 12.3 %all-to-all-start.1 = ((bf16[64,9,32,128]{3,2,1,0:T(8,128)(2,1)}), bf16[64,9,32,128]{3,2,1,0:T(8,128)(2,1)}, u32[]{:S(2)}, u32[]{:S(2)}) async-start(bf16[64,9,32,128]{3,2,1,0:T(8,128)(2,1)} %bitcast.69), calls=%async_computation.1 | async-start | bytes 9437184 | tf_op jit(solution)/shard_map/all_to_all | solution.py:64
  33.3 0.5 copy.46
  33.8 0.4 reshape.156
  34.2 0.4 reshape.131
  34.7 45.9 %all-gather.2.cloned.1.call-done = bf16[1,768,4096]{2,1,0:T(8,128)(2,1)} async-done(((bf16[1,768,1024]{2,1,0:T(8,128)(2,1)}), bf16[1,768,4096]{2,1,0:T(8,128)(2,1)}) %all-gather.2.cloned.1.call-update) | async-done | bytes 6291472 | tf_op jit(solution)/shard_map/all_gather | solution.py:30
  80.5 6.8 %fusion.13 = bf16[72,8,32,128]{3,1,2,0:T(8,128)(2,1)S(1)} fusion(bf16[576,768]{1,0:T(8,128)(2,1)S(1)} %reshape.131, bf16[1,768,4096]{2,1,0:T(8,128)(2,1)} %all-gather.2.cloned.1.call-done), kind=kOutput, calls=%fused_computation.17 | convolution fusion | flops 3626237952 | bytes 11894784 | tf_op jit(solution)/shard_map/dot_general | solution.py:31
  87.4 3.6 %copy.61 = bf16[72,8,32,128]{3,2,1,0:T(8,128)(2,1)} copy(bf16[72,8,32,128]{3,1,2,0:T(8,128)(2,1)S(1)} %fusion.13) | data formatting | bytes 9437184
  91.0 49.6 %all-to-all-done.1 = bf16[64,9,32,128]{3,2,1,0:T(8,128)(2,1)} async-done(((bf16[64,9,32,128]{3,2,1,0:T(8,128)(2,1)}), bf16[64,9,32,128]{3,2,1,0:T(8,128)(2,1)}, u32[]{:S(2)}, u32[]{:S(2)}) %all-to-all-start.1) | async-done | bytes 4718624 | tf_op jit(solution)/shard_map/all_to_all | solution.py:64
  140.6 6.3 %convert_bitcast_fusion.1 = bf16[768,16,128]{0,2,1:T(8,128)(2,1)} fusion(bf16[576,768,1]{1,0,2:T(8,128)(2,1)S(1)} %reshape.156, bf16[576,32,128]{2,1,0:T(8,128)(2,1)} %bitcast.6), kind=kOutput, calls=%fused_computation.16 | convolution fusion | flops 1813512192 | bytes 8749056 | tf_op jit(solution)/shard_map/rf,rjl->fjl/dot_general | solution.py:76
  147.0 5.9 %all-to-all-start = ((bf16[64,9,32,128]{3,2,1,0:T(8,128)(2,1)}), bf16[64,9,32,128]{3,2,1,0:T(8,128)(2,1)}, u32[]{:S(2)}, u32[]{:S(2)}) async-start(bf16[64,9,32,128]{3,2,1,0:T(8,128)(2,1)} %bitcast.68), calls=%async_computation | async-start | bytes 9437184 | tf_op jit(solution)/shard_map/all_to_all | solution.py:35
  152.9 6.1 %convert_bitcast_fusion = bf16[768,16,128]{0,2,1:T(8,128)(2,1)} fusion(bf16[576,768,1]{1,0,2:T(8,128)(2,1)S(1)} %reshape.156, bf16[576,32,128]{2,1,0:T(8,128)(2,1)} %bitcast.6), kind=kOutput, calls=%fused_computation.15 | convolution fusion | flops 1813512192 | bytes 8749056 | tf_op jit(solution)/shard_map/rf,rjl->fjl/dot_general | solution.py:76
  159.2 1.1 copy.63
  160.4 11.1 %reshape_squeeze.3 = bf16[768,4,2,4,128]{4,3,2,1,0:T(4,128)(2,1)} reshape(bf16[1,768,4096]{2,1,0:T(8,128)(2,1)} %all-gather.2.cloned.1.call-done) | data formatting | bytes 12582912 | tf_op jit(solution)/shard_map/reshape;squeeze | solution.py:91
  171.4 5.3 %copy.53 = bf16[768,4,2,4,128]{4,0,3,1,2:T(8,128)(2,1)S(1)} copy(bf16[768,4,2,4,128]{4,3,2,1,0:T(4,128)(2,1)} %reshape_squeeze.3) | data formatting | bytes 12582912 | tf_op jit(solution)/shard_map/reshape;squeeze | solution.py:91
  176.7 6.5 %bitcast_convert_fusion = bf16[576,768]{1,0:T(8,128)(2,1)S(1)} fusion(bf16[768,32,128]{2,0,1:T(8,128)(2,1)S(1)} %bitcast.71, bf16[576,32,128]{2,1,0:T(8,128)(2,1)} %bitcast.6), kind=kOutput, calls=%fused_computation.19 | convolution fusion | flops 3624321024 | bytes 11894784 | tf_op jit(solution)/shard_map/rjl,fjl->rf/dot_general | solution.py:93
  183.2 0.4 reshape.140
  183.6 1.2 copy.58
  184.8 41.8 %reduce-scatter.5.cloned.1.call-done = bf16[768,4,128]{0,2,1:T(8,128)(2,1)} async-done(((bf16[768,16,128]{0,2,1:T(8,128)(2,1)}), bf16[768,4,128]{0,2,1:T(8,128)(2,1)}) %reduce-scatter.5.cloned.1.call-update) | async-done | bytes 786448 | tf_op jit(solution)/shard_map/reduce_scatter | solution.py:83
  226.6 1.5 pad_maximum_fusion
  228.1 2.1 copy.59
  230.2 30.1 %all-to-all-done = bf16[64,9,32,128]{3,2,1,0:T(8,128)(2,1)} async-done(((bf16[64,9,32,128]{3,2,1,0:T(8,128)(2,1)}), bf16[64,9,32,128]{3,2,1,0:T(8,128)(2,1)}, u32[]{:S(2)}, u32[]{:S(2)}) %all-to-all-start) | async-done | bytes 4718624 | tf_op jit(solution)/shard_map/all_to_all | solution.py:35
  260.3 3.6 %gather_fusion = bf16[384,32,128]{2,1,0:T(8,128)(2,1)S(1)} fusion(bf16[576,32,128]{2,1,0:T(8,128)(2,1)} %bitcast.1, s32[1024]{0:T(1024)S(1)} %pad_clamp_fusion), kind=kCustom, calls=%fused_computation | custom fusion | bytes 6292992 | tf_op jit(solution)/shard_map/gather | solution.py:42
  263.9 5.0 %fusion.1 = (f32[48,8]{1,0:T(8,128)}, bf16[48,32,128]{2,1,0:T(8,128)(2,1)S(1)}) fusion(bf16[48,8,32,128]{3,2,1,0:T(8,128)(2,1)S(1)} %bitcast.70, f32[48,32,128]{2,1,0:T(8,128)} %bitcast.73, f32[48,8]{1,0:T(8,128)} %copy-done.2), kind=kLoop, calls=%fused_computation.4 | loop fusion | flops 7667328 | bytes 4328448 | tf_op jit(solution)/shard_map/reduce_sum | solution.py:47
  268.9 1.4 copy.57
  270.3 0.9 copy.80
  (27 shorter events, 1.8 us)
Async XLA Ops:
  7.2 73.4 %all-gather.2.cloned.1.call-start = ((), (), s32[]{:S(2)}) async-start(), calls=%async_computation.4 | async-start | bytes 7864320 | tf_op jit(solution)/shard_map/all_gather | solution.py:30
  9.6 11.3 %copy-start.2 = (f32[48,8]{1,0:T(8,128)}, f32[48,8]{1,0:T(8,128)S(1)}, u32[]{:S(2)}) copy-start(f32[48,8]{1,0:T(8,128)S(1)} %copy.45) | copy-start | bytes 4612
  20.9 12.3 %copy-start.1 = (bf16[1,1,64,9,768]{4,2,3,1,0:T(8,128)(2,1)S(1)}, bf16[1,1,64,9,768]{4,2,3,1,0:T(8,128)(2,1)}, u32[]{:S(2)}) copy-start(bf16[1,1,64,9,768]{4,2,3,1,0:T(8,128)(2,1)} %param.7) | copy-start | bytes 2654212
  20.9 119.7 %all-to-all-start.1 = ((bf16[64,9,32,128]{3,2,1,0:T(8,128)(2,1)}), bf16[64,9,32,128]{3,2,1,0:T(8,128)(2,1)}, u32[]{:S(2)}, u32[]{:S(2)}) async-start(bf16[64,9,32,128]{3,2,1,0:T(8,128)(2,1)} %bitcast.69), calls=%async_computation.1 | async-start | bytes 9437184 | tf_op jit(solution)/shard_map/all_to_all | solution.py:64
  33.2 151.6 %reduce-scatter.3.cloned.1.call-start = ((), (), s32[]{:S(2)}) async-start(), calls=%async_computation.5 | async-start | bytes 3932160 | tf_op jit(solution)/shard_map/reduce_scatter | solution.py:83
  147.0 113.4 %all-to-all-start = ((bf16[64,9,32,128]{3,2,1,0:T(8,128)(2,1)}), bf16[64,9,32,128]{3,2,1,0:T(8,128)(2,1)}, u32[]{:S(2)}, u32[]{:S(2)}) async-start(bf16[64,9,32,128]{3,2,1,0:T(8,128)(2,1)} %bitcast.68), calls=%async_computation | async-start | bytes 9437184 | tf_op jit(solution)/shard_map/all_to_all | solution.py:35
  152.9 6.3 %copy-start = (bf16[48,4096]{1,0:T(8,128)(2,1)S(1)}, bf16[48,4096]{1,0:T(8,128)(2,1)}, u32[]{:S(2)}) copy-start(bf16[48,4096]{1,0:T(8,128)(2,1)} %param.9) | copy-start | bytes 1179652
  152.9 73.7 %reduce-scatter.5.cloned.1.call-start = ((), (), s32[]{:S(2)}) async-start(), calls=%async_computation.6 | async-start | bytes 3932160 | tf_op jit(solution)/shard_map/reduce_scatter | solution.py:83
Sparse Core Ops, SparseCore 0:
  9.8 70.6 all-gather.1
  147.1 35.7 reduce-scatter.2
  186.0 40.5 reduce-scatter.4

commit v11 on v10

--- a/solution.py
+++ b/solution.py
@@ -26,8 +26,14 @@
     holds = slot_index[None, :] == jnp.arange(slot_count, dtype=jnp.int32)[:, None]
     hidden_rows = expert_hidden.reshape(-1, hidden_width)
     lanes = 128
-    grad_tiles = out_grad.reshape(tok_count, model_width // lanes, lanes)
-    gathered_weight = lax.all_gather(down_weight, "dp", axis=2, tiled=True)[0]
+    shard_count = lax.axis_size("dp")
+    quarter = model_width // shard_count
+    split = (shard_count, 2, quarter // 2 // lanes, lanes)
+    local_halves = down_weight.reshape(hidden_width, 2, quarter // 2)
+    gathered_weight = lax.all_gather(local_halves, "dp", axis=2, tiled=False)
+    gathered_weight = gathered_weight.reshape(hidden_width, model_width)
+    grad_mixed = out_grad.reshape((tok_count,) + split).transpose(0, 2, 1, 3, 4)
+    grad_mixed = grad_mixed.reshape(tok_count, model_width // lanes, lanes)
     slot_out = jnp.dot(
         hidden_rows, gathered_weight, preferred_element_type=jnp.float32
     ).astype(jnp.bfloat16)
@@ -43,15 +49,12 @@
         tok_count, top_count, model_width // lanes, lanes
     ).astype(jnp.float32)
     layer_out = jnp.sum(route_probs[:, :, None, None] * route_out, axis=1)
-    layer_out = layer_out.astype(jnp.bfloat16).reshape(tok_count, model_width)
+    layer_out = layer_out.astype(jnp.bfloat16).reshape((tok_count, 2) + split[:1] + split[2:])
+    layer_out = layer_out.transpose(0, 2, 1, 3, 4).reshape(tok_count, model_width)
     prob_grad = jnp.sum(
-        grad_tiles[:, None].astype(jnp.float32) * route_out, axis=(2, 3)
+        grad_mixed[:, None].astype(jnp.float32) * route_out, axis=(2, 3)
     )
-    shard_count = lax.axis_size("dp")
-    quarter = model_width // shard_count
-    split = (shard_count, 2, quarter // 2 // lanes, lanes)
-    grad_mixed = out_grad.reshape((tok_count,) + split).transpose(0, 2, 1, 3, 4)
-    grad_mixed = grad_mixed.reshape(tok_count, model_width).astype(jnp.float32)
+    grad_flat = grad_mixed.reshape(tok_count, model_width).astype(jnp.float32)
     dispatch = jnp.sum(
         jnp.where(
             holds.reshape(slot_count, tok_count, top_count),
@@ -60,7 +63,7 @@
         ),
         axis=2,
     )
-    scaled = jnp.dot(dispatch, grad_mixed, precision=lax.Precision.HIGHEST).astype(jnp.bfloat16)
+    scaled = jnp.dot(dispatch, grad_flat, precision=lax.Precision.HIGHEST).astype(jnp.bfloat16)
     arrived = lax.all_to_all(
         scaled.reshape(expert_count, capacity, model_width // lanes, lanes),
         "expert",
@@ -88,8 +91,7 @@
             ).astype(jnp.float32)
         )
     weight_grad = jnp.stack(weight_parts, axis=1).reshape(1, hidden_width, quarter)
-    weight_mixed = gathered_weight.reshape((hidden_width,) + split).transpose(0, 2, 1, 3, 4)
-    weight_mixed = weight_mixed.reshape(hidden_width, model_width // lanes, lanes)
+    weight_mixed = gathered_weight.reshape(hidden_width, model_width // lanes, lanes)
     hidden_total = jnp.einsum(
         "rjl,fjl->rf", arrived, weight_mixed, preferred_element_type=jnp.float32
     )

time: 279 us -> 279 us (level)
  local copies, waits for them, and re-layouts: 39.4 us -> 24.9 us
  waiting for transfers between devices: 168 us -> 181 us
    another operation x2 -> x1, local copies, waits for them, and re-layouts: 16.4 us -> 0.29 us  [shards(): grad_flat = grad_mixed.reshape(tok_count, model_width).astype(jnp.float32)]
    reduce_scatter x2, waiting for transfers between devices: 41.8 us -> 57.2 us  [shards(): lax.psum_scatter(rounded_partial(partial_value).astype(jnp.bfloat16), 'dp...]
    unnamed x16 -> x19, local copies, waits for them, and re-layouts: 16 us -> 15.4 us
  transfers between devices with their start and end apart: 5 -> 5, of which waited for: 4 -> 5; matrix products, arithmetic and copies ran while one was open for 22% -> 16% of each run, Pallas kernels for 0% -> 0%
where the time goes in v11:
time: 279 us; the launch traced here: 278 us
  waiting for transfers between devices  181 us (65%)
  matrix products  31 us (11%)
  local copies, waits for them, and re-layouts  24.9 us (9%)
  starting transfers between devices  18.5 us (7%)
  between operations  14 us (5%)
  other arithmetic  8.09 us (3%)
    reduce_scatter x2, waiting for transfers between devices, shards(): lax.psum_scatter(rounded_partial(partial_value).astype(jnp.bfloat16), 'dp...  57.2 us
    all_to_all x1, waiting for transfers between devices, shards(): lax.all_to_all(scaled.reshape(expert_count, capacity, model_width // lane...  48.7 us
    all_gather x1, waiting for transfers between devices, shards(): gathered_weight = lax.all_gather(local_halves, 'dp', axis=2, tiled=False)  45.7 us
    all_to_all x1, waiting for transfers between devices, shards(): lax.all_to_all(outgoing, 'expert', split_axis=0, concat_axis=0, tiled=True)  29.9 us
    unnamed x19, local copies, waits for them, and re-layouts  15.4 us
    dot_general x2, matrix products, shards(): jnp.einsum('rf,rjl->fjl', hidden_rows, arrived[:, part * half_tiles:(part...  12.5 us
    all_to_all x1, starting transfers between devices, shards(): lax.all_to_all(scaled.reshape(expert_count, capacity, model_width // lane...  12.3 us
    dot_general x1, matrix products, shards(): jnp.einsum('rjl,fjl->rf', arrived, weight_mixed, preferred_element_type=j...  7.42 us
  transfers between devices with their start and end apart: 5, of which 5 were waited for; matrix products, arithmetic and copies ran while one was open for 16% of the time, Pallas kernels for 0%

profile of v11, /device:TPU:18, one launch (start us, length us, event | category | flops | bytes accessed | tf_op | source)
XLA Modules:
  0.0 277.9 jit_solution(1926013025540471449)
XLA Ops:
  7.2 2.6 copy.91
  10.3 0.9 reduce-window.6
  11.7 0.3 reshape.137
  12.3 0.3 reshape_reshape.6
  12.6 0.4 select_reduce_fusion
  12.9 4.2 %fusion.9 = bf16[72,8,32,128]{3,1,2,0:T(8,128)(2,1)S(1)} fusion(f32[576,48]{0,1:T(8,128)S(1)} %select_reduce_fusion, bf16[48,4096]{1,0:T(8,128)(2,1)S(1)} %reshape_reshape.6), kind=kOutput, calls=%fused_computation.16 | convolution fusion | flops 1361313792 | bytes 5222400 | tf_op jit(solution)/shard_map/dot_general | solution.py:66
  17.1 3.7 %copy.112 = bf16[72,8,32,128]{3,2,1,0:T(8,128)(2,1)} copy(bf16[72,8,32,128]{3,1,2,0:T(8,128)(2,1)S(1)} %fusion.9) | data formatting | bytes 9437184
  20.8 12.3 %all-to-all-start.1 = ((bf16[64,9,32,128]{3,2,1,0:T(8,128)(2,1)}), bf16[64,9,32,128]{3,2,1,0:T(8,128)(2,1)}, u32[]{:S(2)}, u32[]{:S(2)}) async-start(bf16[64,9,32,128]{3,2,1,0:T(8,128)(2,1)} %bitcast.63), calls=%async_computation.1 | async-start | bytes 9437184 | tf_op jit(solution)/shard_map/all_to_all | solution.py:67
  33.3 0.5 copy.90
  33.8 0.4 reshape.156
  34.3 1.2 reshape.131
  35.5 45.7 %all-gather.2.cloned.1.call-done = bf16[768,2,4,512]{0,3,2,1:T(8,128)(2,1)} async-done(((bf16[768,2,1,512]{0,3,2,1:T(8,128)(2,1)}), bf16[768,2,4,512]{0,3,2,1:T(8,128)(2,1)}) %all-gather.2.cloned.1.call-update) | async-done | bytes 6291472 | tf_op jit(solution)/shard_map/all_gather | solution.py:33
  81.2 6.9 %fusion.8 = bf16[72,8,32,128]{3,1,2,0:T(8,128)(2,1)S(1)} fusion(bf16[576,768]{1,0:T(8,128)(2,1)} %reshape.131, bf16[768,4096]{0,1:T(8,128)(2,1)} %bitcast.72), kind=kOutput, calls=%fused_computation.15 | convolution fusion | flops 3626237952 | bytes 11894784 | tf_op jit(solution)/shard_map/dot_general | solution.py:37
  88.1 3.7 %copy.111 = bf16[72,8,32,128]{3,2,1,0:T(8,128)(2,1)} copy(bf16[72,8,32,128]{3,1,2,0:T(8,128)(2,1)S(1)} %fusion.8) | data formatting | bytes 9437184
  91.8 48.7 %all-to-all-done.1 = bf16[64,9,32,128]{3,2,1,0:T(8,128)(2,1)} async-done(((bf16[64,9,32,128]{3,2,1,0:T(8,128)(2,1)}), bf16[64,9,32,128]{3,2,1,0:T(8,128)(2,1)}, u32[]{:S(2)}, u32[]{:S(2)}) %all-to-all-start.1) | async-done | bytes 4718624 | tf_op jit(solution)/shard_map/all_to_all | solution.py:67
  140.5 6.4 %convert_bitcast_fusion.1 = bf16[768,16,128]{0,2,1:T(8,128)(2,1)} fusion(bf16[576,768,1]{1,0,2:T(8,128)(2,1)S(1)} %reshape.156, bf16[576,32,128]{2,1,0:T(8,128)(2,1)} %bitcast.10), kind=kOutput, calls=%fused_computation.14 | convolution fusion | flops 1813512192 | bytes 8749056 | tf_op jit(solution)/shard_map/rf,rjl->fjl/dot_general | solution.py:79
  146.8 5.7 %all-to-all-start = ((bf16[64,9,32,128]{3,2,1,0:T(8,128)(2,1)}), bf16[64,9,32,128]{3,2,1,0:T(8,128)(2,1)}, u32[]{:S(2)}, u32[]{:S(2)}) async-start(bf16[64,9,32,128]{3,2,1,0:T(8,128)(2,1)} %bitcast.62), calls=%async_computation | async-start | bytes 9437184 | tf_op jit(solution)/shard_map/all_to_all | solution.py:41
  152.6 0.3 reduce-scatter.5.cloned.1.call-start
  152.8 6.1 %convert_bitcast_fusion = bf16[768,16,128]{0,2,1:T(8,128)(2,1)} fusion(bf16[576,768,1]{1,0,2:T(8,128)(2,1)S(1)} %reshape.156, bf16[576,32,128]{2,1,0:T(8,128)(2,1)} %bitcast.10), kind=kOutput, calls=%fused_computation.13 | convolution fusion | flops 1813512192 | bytes 8749056 | tf_op jit(solution)/shard_map/rf,rjl->fjl/dot_general | solution.py:79
  159.1 1.1 copy.99
  160.3 7.4 %bitcast_convert_fusion = bf16[576,768]{1,0:T(8,128)(2,1)S(1)} fusion(bf16[768,32,128]{0,2,1:T(8,128)(2,1)} %bitcast.73, bf16[576,32,128]{2,1,0:T(8,128)(2,1)} %bitcast.10), kind=kOutput, calls=%fused_computation.17 | convolution fusion | flops 3624321024 | bytes 11894784 | tf_op jit(solution)/shard_map/rjl,fjl->rf/dot_general | solution.py:95
  167.7 0.4 reshape.140
  168.1 1.2 copy.107
  169.3 13.5 %reduce-scatter.3.cloned.1.call-done = bf16[768,4,128]{0,2,1:T(8,128)(2,1)} async-done(((bf16[768,16,128]{0,2,1:T(8,128)(2,1)}), bf16[768,4,128]{0,2,1:T(8,128)(2,1)}) %reduce-scatter.3.cloned.1.call-update) | async-done | bytes 786448 | tf_op jit(solution)/shard_map/reduce_scatter | solution.py:86
  182.8 43.7 %reduce-scatter.5.cloned.1.call-done = bf16[768,4,128]{0,2,1:T(8,128)(2,1)} async-done(((bf16[768,16,128]{0,2,1:T(8,128)(2,1)}), bf16[768,4,128]{0,2,1:T(8,128)(2,1)}) %reduce-scatter.5.cloned.1.call-update) | async-done | bytes 786448 | tf_op jit(solution)/shard_map/reduce_scatter | solution.py:86
  226.5 1.5 pad_maximum_fusion
  228.0 2.1 copy.108
  230.1 29.9 %all-to-all-done = bf16[64,9,32,128]{3,2,1,0:T(8,128)(2,1)} async-done(((bf16[64,9,32,128]{3,2,1,0:T(8,128)(2,1)}), bf16[64,9,32,128]{3,2,1,0:T(8,128)(2,1)}, u32[]{:S(2)}, u32[]{:S(2)}) %all-to-all-start) | async-done | bytes 4718624 | tf_op jit(solution)/shard_map/all_to_all | solution.py:41
  260.0 3.6 %gather_fusion = bf16[384,32,128]{2,1,0:T(8,128)(2,1)S(1)} fusion(bf16[576,32,128]{2,1,0:T(8,128)(2,1)} %bitcast.2, s32[1024]{0:T(1024)S(1)} %pad_clamp_fusion), kind=kCustom, calls=%fused_computation | custom fusion | bytes 6292992 | tf_op jit(solution)/shard_map/gather | solution.py:48
  263.6 5.0 %fusion.1 = (f32[48,8]{1,0:T(8,128)}, bf16[48,32,128]{2,1,0:T(8,128)(2,1)S(1)}) fusion(bf16[48,8,32,128]{3,2,1,0:T(8,128)(2,1)S(1)} %bitcast.64, f32[48,32,128]{2,1,0:T(8,128)} %copy.99, f32[48,8]{1,0:T(8,128)} %copy-done.2), kind=kLoop, calls=%fused_computation.4 | loop fusion | flops 7667328 | bytes 4328448 | tf_op jit(solution)/shard_map/reduce_sum | solution.py:54
  268.6 1.4 copy.106
  270.4 1.0 reshape.136
  (33 shorter events, 2.0 us)
Async XLA Ops:
  7.2 2.7 copy-start.3
  7.2 3.0 %copy-start.4 = (f32[48,8]{0,1:T(8,128)S(1)}, f32[48,8]{0,1:T(8,128)}, u32[]{:S(2)}) copy-start(f32[48,8]{0,1:T(8,128)} %param.6) | copy-start | bytes 4612
  7.2 4.5 %copy-start.1 = (bf16[48,4096]{1,0:T(8,128)(2,1)S(1)}, bf16[48,4096]{1,0:T(8,128)(2,1)}, u32[]{:S(2)}) copy-start(bf16[48,4096]{1,0:T(8,128)(2,1)} %param.9) | copy-start | bytes 1179652
  7.2 74.0 %all-gather.2.cloned.1.call-start = ((), (), s32[]{:S(2)}) async-start(), calls=%async_computation.4 | async-start | bytes 7864320 | tf_op jit(solution)/shard_map/all_gather | solution.py:33
  10.3 10.5 %copy-start.2 = (f32[48,8]{1,0:T(8,128)}, f32[48,8]{1,0:T(8,128)S(1)}, u32[]{:S(2)}) copy-start(f32[48,8]{1,0:T(8,128)S(1)} %copy.89) | copy-start | bytes 4612
  20.8 12.5 %copy-start = (bf16[1,1,64,9,768]{4,2,3,1,0:T(8,128)(2,1)S(1)}, bf16[1,1,64,9,768]{4,2,3,1,0:T(8,128)(2,1)}, u32[]{:S(2)}) copy-start(bf16[1,1,64,9,768]{4,2,3,1,0:T(8,128)(2,1)} %param.7) | copy-start | bytes 2654212
  20.8 119.7 %all-to-all-start.1 = ((bf16[64,9,32,128]{3,2,1,0:T(8,128)(2,1)}), bf16[64,9,32,128]{3,2,1,0:T(8,128)(2,1)}, u32[]{:S(2)}, u32[]{:S(2)}) async-start(bf16[64,9,32,128]{3,2,1,0:T(8,128)(2,1)} %bitcast.63), calls=%async_computation.1 | async-start | bytes 9437184 | tf_op jit(solution)/shard_map/all_to_all | solution.py:67
  33.1 149.7 %reduce-scatter.3.cloned.1.call-start = ((), (), s32[]{:S(2)}) async-start(), calls=%async_computation.5 | async-start | bytes 3932160 | tf_op jit(solution)/shard_map/reduce_scatter | solution.py:86
  146.8 113.2 %all-to-all-start = ((bf16[64,9,32,128]{3,2,1,0:T(8,128)(2,1)}), bf16[64,9,32,128]{3,2,1,0:T(8,128)(2,1)}, u32[]{:S(2)}, u32[]{:S(2)}) async-start(bf16[64,9,32,128]{3,2,1,0:T(8,128)(2,1)} %bitcast.62), calls=%async_computation | async-start | bytes 9437184 | tf_op jit(solution)/shard_map/all_to_all | solution.py:41
  152.6 73.9 %reduce-scatter.5.cloned.1.call-start = ((), (), s32[]{:S(2)}) async-start(), calls=%async_computation.6 | async-start | bytes 3932160 | tf_op jit(solution)/shard_map/reduce_scatter | solution.py:86
Sparse Core Ops, SparseCore 0:
  10.4 70.7 all-gather.1
  147.0 35.7 reduce-scatter.2
  185.9 40.5 reduce-scatter.4

commit v12 on v11

--- a/solution.py
+++ b/solution.py
@@ -45,14 +45,15 @@
         concat_axis=0,
         tiled=True,
     )
-    route_out = returned.reshape(slot_count, model_width // lanes, lanes)[slot_index].reshape(
+    route_rows = returned.reshape(slot_count, model_width // lanes, lanes)[slot_index].reshape(
         tok_count, top_count, model_width // lanes, lanes
-    ).astype(jnp.float32)
+    )
+    route_out = route_rows.astype(jnp.float32)
     layer_out = jnp.sum(route_probs[:, :, None, None] * route_out, axis=1)
     layer_out = layer_out.astype(jnp.bfloat16).reshape((tok_count, 2) + split[:1] + split[2:])
     layer_out = layer_out.transpose(0, 2, 1, 3, 4).reshape(tok_count, model_width)
-    prob_grad = jnp.sum(
-        grad_mixed[:, None].astype(jnp.float32) * route_out, axis=(2, 3)
+    prob_grad = jnp.einsum(
+        "tjl,tkjl->tk", grad_mixed, route_rows, preferred_element_type=jnp.float32
     )
     grad_flat = grad_mixed.reshape(tok_count, model_width).astype(jnp.float32)
     dispatch = jnp.sum(

time: 279 us -> 280 us (level)
  matrix products: 31 us -> 35.1 us
  other arithmetic: 8.09 us -> 4.92 us
    dot_general x0 -> x1, matrix products: none -> 4.2 us  [shards(): jnp.einsum('tjl,tkjl->tk', grad_mixed, route_rows, preferred_element_type...]
    reduce_sum x1, other arithmetic: 5.01 us -> 1.92 us  [shards(): layer_out = jnp.sum(route_probs[:, :, None, None] * route_out, axis=1)]
    unnamed x19 -> x18, local copies, waits for them, and re-layouts: 15.4 us -> 14 us
  transfers between devices with their start and end apart: 5 -> 5, of which waited for: 5 -> 5; matrix products, arithmetic and copies ran while one was open for 16% -> 15% of each run, Pallas kernels for 0% -> 0%
where the time goes in v12:
time: 280 us; the launch traced here: 279 us
  waiting for transfers between devices  182 us (65%)
  matrix products  35.1 us (13%)
  local copies, waits for them, and re-layouts  24.5 us (9%)
  starting transfers between devices  18.5 us (7%)
  between operations  14 us (5%)
  other arithmetic  4.92 us (2%)
    reduce_scatter x2, waiting for transfers between devices, shards(): lax.psum_scatter(rounded_partial(partial_value).astype(jnp.bfloat16), 'dp...  57.5 us
    all_to_all x1, waiting for transfers between devices, shards(): lax.all_to_all(scaled.reshape(expert_count, capacity, model_width // lane...  48.5 us
    all_gather x1, waiting for transfers between devices, shards(): gathered_weight = lax.all_gather(local_halves, 'dp', axis=2, tiled=False)  45.9 us
    all_to_all x1, waiting for transfers between devices, shards(): lax.all_to_all(outgoing, 'expert', split_axis=0, concat_axis=0, tiled=True)  29.9 us
    unnamed x18, local copies, waits for them, and re-layouts  14 us
    dot_general x2, matrix products, shards(): jnp.einsum('rf,rjl->fjl', hidden_rows, arrived[:, part * half_tiles:(part...  12.5 us
    all_to_all x1, starting transfers between devices, shards(): lax.all_to_all(scaled.reshape(expert_count, capacity, model_width // lane...  12.3 us
    dot_general x1, matrix products, shards(): jnp.einsum('rjl,fjl->rf', arrived, weight_mixed, preferred_element_type=j...  7.4 us
  transfers between devices with their start and end apart: 5, of which 5 were waited for; matrix products, arithmetic and copies ran while one was open for 15% of the time, Pallas kernels for 0%

profile of v12, /device:TPU:18, one launch (start us, length us, event | category | flops | bytes accessed | tf_op | source)
XLA Modules:
  0.0 278.8 jit_solution(8108463808617898993)
XLA Ops:
  7.2 2.6 copy.67
  10.3 0.9 reduce-window.6
  11.7 0.3 reshape.122
  12.1 0.3 reshape_reshape.6
  12.4 0.4 select_reduce_fusion
  12.8 4.2 %fusion.9 = bf16[72,8,32,128]{3,1,2,0:T(8,128)(2,1)S(1)} fusion(f32[576,48]{0,1:T(8,128)S(1)} %select_reduce_fusion, bf16[48,4096]{1,0:T(8,128)(2,1)S(1)} %reshape_reshape.6), kind=kOutput, calls=%fused_computation.15 | convolution fusion | flops 1361313792 | bytes 5222400 | tf_op jit(solution)/shard_map/dot_general | solution.py:67
  16.9 3.7 %copy.89 = bf16[72,8,32,128]{3,2,1,0:T(8,128)(2,1)} copy(bf16[72,8,32,128]{3,1,2,0:T(8,128)(2,1)S(1)} %fusion.9) | data formatting | bytes 9437184
  20.6 12.3 %all-to-all-start.1 = ((bf16[64,9,32,128]{3,2,1,0:T(8,128)(2,1)}), bf16[64,9,32,128]{3,2,1,0:T(8,128)(2,1)}, u32[]{:S(2)}, u32[]{:S(2)}) async-start(bf16[64,9,32,128]{3,2,1,0:T(8,128)(2,1)} %bitcast.60), calls=%async_computation.1 | async-start | bytes 9437184 | tf_op jit(solution)/shard_map/all_to_all | solution.py:68
  33.1 0.5 copy.66
  33.7 0.4 reshape.142
  34.1 1.2 reshape.115
  35.3 45.9 %all-gather.2.cloned.1.call-done = bf16[768,2,4,512]{0,3,2,1:T(8,128)(2,1)} async-done(((bf16[768,2,1,512]{0,3,2,1:T(8,128)(2,1)}), bf16[768,2,4,512]{0,3,2,1:T(8,128)(2,1)}) %all-gather.2.cloned.1.call-update) | async-done | bytes 6291472 | tf_op jit(solution)/shard_map/all_gather | solution.py:33
  81.2 6.9 %fusion.8 = bf16[72,8,32,128]{3,1,2,0:T(8,128)(2,1)S(1)} fusion(bf16[576,768]{1,0:T(8,128)(2,1)} %reshape.115, bf16[768,4096]{0,1:T(8,128)(2,1)} %bitcast.73), kind=kOutput, calls=%fused_computation.14 | convolution fusion | flops 3626237952 | bytes 11894784 | tf_op jit(solution)/shard_map/dot_general | solution.py:37
  88.1 3.7 %copy.88 = bf16[72,8,32,128]{3,2,1,0:T(8,128)(2,1)} copy(bf16[72,8,32,128]{3,1,2,0:T(8,128)(2,1)S(1)} %fusion.8) | data formatting | bytes 9437184
  91.8 48.5 %all-to-all-done.1 = bf16[64,9,32,128]{3,2,1,0:T(8,128)(2,1)} async-done(((bf16[64,9,32,128]{3,2,1,0:T(8,128)(2,1)}), bf16[64,9,32,128]{3,2,1,0:T(8,128)(2,1)}, u32[]{:S(2)}, u32[]{:S(2)}) %all-to-all-start.1) | async-done | bytes 4718624 | tf_op jit(solution)/shard_map/all_to_all | solution.py:68
  140.3 6.4 %convert_bitcast_fusion.1 = bf16[768,16,128]{0,2,1:T(8,128)(2,1)} fusion(bf16[576,768,1]{1,0,2:T(8,128)(2,1)S(1)} %reshape.142, bf16[576,32,128]{2,1,0:T(8,128)(2,1)} %bitcast.11), kind=kOutput, calls=%fused_computation.13 | convolution fusion | flops 1813512192 | bytes 8749056 | tf_op jit(solution)/shard_map/rf,rjl->fjl/dot_general | solution.py:80
  146.7 5.7 %all-to-all-start = ((bf16[64,9,32,128]{3,2,1,0:T(8,128)(2,1)}), bf16[64,9,32,128]{3,2,1,0:T(8,128)(2,1)}, u32[]{:S(2)}, u32[]{:S(2)}) async-start(bf16[64,9,32,128]{3,2,1,0:T(8,128)(2,1)} %bitcast.59), calls=%async_computation | async-start | bytes 9437184 | tf_op jit(solution)/shard_map/all_to_all | solution.py:41
  152.6 6.1 %convert_bitcast_fusion = bf16[768,16,128]{0,2,1:T(8,128)(2,1)} fusion(bf16[576,768,1]{1,0,2:T(8,128)(2,1)S(1)} %reshape.142, bf16[576,32,128]{2,1,0:T(8,128)(2,1)} %bitcast.11), kind=kOutput, calls=%fused_computation.12 | convolution fusion | flops 1813512192 | bytes 8749056 | tf_op jit(solution)/shard_map/rf,rjl->fjl/dot_general | solution.py:80
  158.8 0.9 copy.74
  159.8 7.4 %bitcast_convert_fusion = bf16[576,768]{1,0:T(8,128)(2,1)S(1)} fusion(bf16[768,32,128]{0,2,1:T(8,128)(2,1)} %bitcast.74, bf16[576,32,128]{2,1,0:T(8,128)(2,1)} %bitcast.11), kind=kOutput, calls=%fused_computation.16 | convolution fusion | flops 3624321024 | bytes 11894784 | tf_op jit(solution)/shard_map/rjl,fjl->rf/dot_general | solution.py:96
  167.2 0.4 reshape.126
  167.6 1.2 copy.81
  168.8 13.8 %reduce-scatter.3.cloned.1.call-done = bf16[768,4,128]{0,2,1:T(8,128)(2,1)} async-done(((bf16[768,16,128]{0,2,1:T(8,128)(2,1)}), bf16[768,4,128]{0,2,1:T(8,128)(2,1)}) %reduce-scatter.3.cloned.1.call-update) | async-done | bytes 786448 | tf_op jit(solution)/shard_map/reduce_scatter | solution.py:87
  182.6 43.7 %reduce-scatter.5.cloned.1.call-done = bf16[768,4,128]{0,2,1:T(8,128)(2,1)} async-done(((bf16[768,16,128]{0,2,1:T(8,128)(2,1)}), bf16[768,4,128]{0,2,1:T(8,128)(2,1)}) %reduce-scatter.5.cloned.1.call-update) | async-done | bytes 786448 | tf_op jit(solution)/shard_map/reduce_scatter | solution.py:87
  226.3 1.5 pad_maximum_fusion
  227.8 2.1 copy.82
  230.0 29.9 %all-to-all-done = bf16[64,9,32,128]{3,2,1,0:T(8,128)(2,1)} async-done(((bf16[64,9,32,128]{3,2,1,0:T(8,128)(2,1)}), bf16[64,9,32,128]{3,2,1,0:T(8,128)(2,1)}, u32[]{:S(2)}, u32[]{:S(2)}) %all-to-all-start) | async-done | bytes 4718624 | tf_op jit(solution)/shard_map/all_to_all | solution.py:41
  259.9 3.6 %gather_fusion = bf16[384,32,128]{2,1,0:T(8,128)(2,1)S(1)} fusion(bf16[576,32,128]{2,1,0:T(8,128)(2,1)} %bitcast.2, s32[1024]{0:T(1024)S(1)} %pad_clamp_fusion), kind=kCustom, calls=%fused_computation | custom fusion | bytes 6292992 | tf_op jit(solution)/shard_map/gather | solution.py:48
  263.4 1.9 multiply_reduce_fusion
  265.4 4.2 %fusion.6 = f32[48,1,8,1]{2,1,3,0:T(1,128)} fusion(bf16[48,8,32,128]{3,2,1,0:T(8,128)(2,1)S(1)} %bitcast.62, bf16[48,32,128,1]{2,0,1,3:T(8,128)(2,1)} %bitcast.70), kind=kOutput, calls=%fused_computation.10 | convolution fusion | flops 3145728 | bytes 3540480 | tf_op jit(solution)/shard_map/tjl,tkjl->tk/dot_general | solution.py:55
  269.6 1.4 copy.85
  271.3 1.0 reshape.121
  (32 shorter events, 2.0 us)
Async XLA Ops:
  7.2 2.7 copy-start.3
  7.2 3.0 %copy-start.4 = (f32[48,8]{0,1:T(8,128)S(1)}, f32[48,8]{0,1:T(8,128)}, u32[]{:S(2)}) copy-start(f32[48,8]{0,1:T(8,128)} %param.6) | copy-start | bytes 4612
  7.2 4.5 %copy-start.1 = (bf16[48,4096]{1,0:T(8,128)(2,1)S(1)}, bf16[48,4096]{1,0:T(8,128)(2,1)}, u32[]{:S(2)}) copy-start(bf16[48,4096]{1,0:T(8,128)(2,1)} %param.9) | copy-start | bytes 1179652
  7.2 74.0 %all-gather.2.cloned.1.call-start = ((), (), s32[]{:S(2)}) async-start(), calls=%async_computation.4 | async-start | bytes 7864320 | tf_op jit(solution)/shard_map/all_gather | solution.py:33
  10.3 10.4 %copy-start.2 = (f32[48,8]{1,0:T(8,128)}, f32[48,8]{1,0:T(8,128)S(1)}, u32[]{:S(2)}) copy-start(f32[48,8]{1,0:T(8,128)S(1)} %copy.65) | copy-start | bytes 4612
  20.6 12.5 %copy-start = (bf16[1,1,64,9,768]{4,2,3,1,0:T(8,128)(2,1)S(1)}, bf16[1,1,64,9,768]{4,2,3,1,0:T(8,128)(2,1)}, u32[]{:S(2)}) copy-start(bf16[1,1,64,9,768]{4,2,3,1,0:T(8,128)(2,1)} %param.7) | copy-start | bytes 2654212
  20.6 119.7 %all-to-all-start.1 = ((bf16[64,9,32,128]{3,2,1,0:T(8,128)(2,1)}), bf16[64,9,32,128]{3,2,1,0:T(8,128)(2,1)}, u32[]{:S(2)}, u32[]{:S(2)}) async-start(bf16[64,9,32,128]{3,2,1,0:T(8,128)(2,1)} %bitcast.60), calls=%async_computation.1 | async-start | bytes 9437184 | tf_op jit(solution)/shard_map/all_to_all | solution.py:68
  32.9 149.7 %reduce-scatter.3.cloned.1.call-start = ((), (), s32[]{:S(2)}) async-start(), calls=%async_computation.5 | async-start | bytes 3932160 | tf_op jit(solution)/shard_map/reduce_scatter | solution.py:87
  146.7 113.2 %all-to-all-start = ((bf16[64,9,32,128]{3,2,1,0:T(8,128)(2,1)}), bf16[64,9,32,128]{3,2,1,0:T(8,128)(2,1)}, u32[]{:S(2)}, u32[]{:S(2)}) async-start(bf16[64,9,32,128]{3,2,1,0:T(8,128)(2,1)} %bitcast.59), calls=%async_computation | async-start | bytes 9437184 | tf_op jit(solution)/shard_map/all_to_all | solution.py:41
  152.4 73.9 %reduce-scatter.5.cloned.1.call-start = ((), (), s32[]{:S(2)}) async-start(), calls=%async_computation.6 | async-start | bytes 3932160 | tf_op jit(solution)/shard_map/reduce_scatter | solution.py:87
Sparse Core Ops, SparseCore 0:
  10.4 70.7 all-gather.1
  146.8 35.7 reduce-scatter.2
  185.7 40.5 reduce-scatter.4

commit v13 on v11

--- a/solution.py
+++ b/solution.py
@@ -54,7 +54,6 @@
     prob_grad = jnp.sum(
         grad_mixed[:, None].astype(jnp.float32) * route_out, axis=(2, 3)
     )
-    grad_flat = grad_mixed.reshape(tok_count, model_width).astype(jnp.float32)
     dispatch = jnp.sum(
         jnp.where(
             holds.reshape(slot_count, tok_count, top_count),
@@ -63,7 +62,16 @@
         ),
         axis=2,
     )
-    scaled = jnp.dot(dispatch, grad_flat, precision=lax.Precision.HIGHEST).astype(jnp.bfloat16)
+    grad_narrow = grad_mixed.reshape(tok_count, model_width)
+    pieces = []
+    rest = dispatch
+    for _ in range(3):
+        piece = rest.astype(jnp.bfloat16)
+        pieces.append(piece)
+        rest = rest - piece.astype(jnp.float32)
+    scaled = sum(
+        jnp.dot(piece, grad_narrow, preferred_element_type=jnp.float32) for piece in pieces
+    ).astype(jnp.bfloat16)
     arrived = lax.all_to_all(
         scaled.reshape(expert_count, capacity, model_width // lanes, lanes),
         "expert",

time: 279 us -> 282 us (1.011)
    all_to_all x1, waiting for transfers between devices: 48.7 us -> 53.4 us  [shards(): lax.all_to_all(scaled.reshape(expert_count, capacity, model_width // lane...]
    all_gather x1, waiting for transfers between devices: 45.7 us -> 41 us  [shards(): gathered_weight = lax.all_gather(local_halves, 'dp', axis=2, tiled=False)]
    dot_general x1 -> x3, matrix products: 4.15 us -> 6.48 us  [shards(): jnp.dot(piece, grad_narrow, preferred_element_type=jnp.float32)]
    unnamed x19 -> x17, local copies, waits for them, and re-layouts: 15.4 us -> 17 us
  transfers between devices with their start and end apart: 5 -> 5, of which waited for: 5 -> 5; matrix products, arithmetic and copies ran while one was open for 16% -> 17% of each run, Pallas kernels for 0% -> 0%
where the time goes in v13:
time: 282 us; the launch traced here: 281 us
  waiting for transfers between devices  182 us (65%)
  matrix products  33.3 us (12%)
  local copies, waits for them, and re-layouts  26.5 us (9%)
  starting transfers between devices  18.5 us (7%)
  between operations  14 us (5%)
  other arithmetic  7.51 us (3%)
    reduce_scatter x2, waiting for transfers between devices, shards(): lax.psum_scatter(rounded_partial(partial_value).astype(jnp.bfloat16), 'dp...  57.1 us
    all_to_all x1, waiting for transfers between devices, shards(): lax.all_to_all(scaled.reshape(expert_count, capacity, model_width // lane...  53.4 us
    all_gather x1, waiting for transfers between devices, shards(): gathered_weight = lax.all_gather(local_halves, 'dp', axis=2, tiled=False)  41 us
    all_to_all x1, waiting for transfers between devices, shards(): lax.all_to_all(outgoing, 'expert', split_axis=0, concat_axis=0, tiled=True)  29.9 us
    unnamed x17, local copies, waits for them, and re-layouts  17 us
    dot_general x2, matrix products, shards(): jnp.einsum('rf,rjl->fjl', hidden_rows, arrived[:, part * half_tiles:(part...  12.5 us
    all_to_all x1, starting transfers between devices, shards(): lax.all_to_all(scaled.reshape(expert_count, capacity, model_width // lane...  12.3 us
    dot_general x1, matrix products, shards(): jnp.einsum('rjl,fjl->rf', arrived, weight_mixed, preferred_element_type=j...  7.42 us
  transfers between devices with their start and end apart: 5, of which 5 were waited for; matrix products, arithmetic and copies ran while one was open for 17% of the time, Pallas kernels for 0%

profile of v13, /device:TPU:18, one launch (start us, length us, event | category | flops | bytes accessed | tf_op | source)
XLA Modules:
  0.0 281.3 jit_solution(4769716597444481797)
XLA Ops:
  7.2 2.6 copy.91
  10.2 0.9 reduce-window.6
  12.3 0.3 reshape_reshape.6
  12.6 0.4 select_reduce_fusion
  12.9 1.4 fusion.21
  14.4 1.4 fusion.23
  15.8 3.7 %fusion.9 = bf16[72,8,32,128]{3,1,2,0:T(8,128)(2,1)} fusion(bf16[48,4096]{1,0:T(8,128)(2,1)S(1)} %reshape_reshape.6, f32[576,4096]{1,0:T(8,128)S(1)} %fusion.21, f32[576,4096]{1,0:T(8,128)S(1)} %fusion.23, f32[576,48]{0,1:T(8,128)S(1)} %select_reduce_fusion), kind=kOutput, calls=%fused_computation.16 | convolution fusion | flops 233763840 | bytes 24096768 | tf_op jit(solution)/shard_map/dot_general | solution.py:73
  19.4 6.0 %copy.112 = bf16[72,8,32,128]{3,2,1,0:T(8,128)(2,1)} copy(bf16[72,8,32,128]{3,1,2,0:T(8,128)(2,1)} %fusion.9) | data formatting | bytes 9437184
  25.5 12.3 %all-to-all-start.1 = ((bf16[64,9,32,128]{3,2,1,0:T(8,128)(2,1)}), bf16[64,9,32,128]{3,2,1,0:T(8,128)(2,1)}, u32[]{:S(2)}, u32[]{:S(2)}) async-start(bf16[64,9,32,128]{3,2,1,0:T(8,128)(2,1)} %bitcast.64), calls=%async_computation.1 | async-start | bytes 9437184 | tf_op jit(solution)/shard_map/all_to_all | solution.py:75
  38.0 0.5 copy.90
  38.5 1.2 reshape.131
  39.7 0.4 reshape.156
  40.1 41.0 %all-gather.2.cloned.1.call-done = bf16[768,2,4,512]{0,3,2,1:T(8,128)(2,1)} async-done(((bf16[768,2,1,512]{0,3,2,1:T(8,128)(2,1)}), bf16[768,2,4,512]{0,3,2,1:T(8,128)(2,1)}) %all-gather.2.cloned.1.call-update) | async-done | bytes 6291472 | tf_op jit(solution)/shard_map/all_gather | solution.py:33
  81.2 6.9 %fusion.8 = bf16[72,8,32,128]{3,1,2,0:T(8,128)(2,1)S(1)} fusion(bf16[576,768]{1,0:T(8,128)(2,1)} %reshape.131, bf16[768,4096]{0,1:T(8,128)(2,1)} %bitcast.73), kind=kOutput, calls=%fused_computation.15 | convolution fusion | flops 3626237952 | bytes 11894784 | tf_op jit(solution)/shard_map/dot_general | solution.py:37
  88.1 3.7 %copy.111 = bf16[72,8,32,128]{3,2,1,0:T(8,128)(2,1)} copy(bf16[72,8,32,128]{3,1,2,0:T(8,128)(2,1)S(1)} %fusion.8) | data formatting | bytes 9437184
  91.8 53.4 %all-to-all-done.1 = bf16[64,9,32,128]{3,2,1,0:T(8,128)(2,1)} async-done(((bf16[64,9,32,128]{3,2,1,0:T(8,128)(2,1)}), bf16[64,9,32,128]{3,2,1,0:T(8,128)(2,1)}, u32[]{:S(2)}, u32[]{:S(2)}) %all-to-all-start.1) | async-done | bytes 4718624 | tf_op jit(solution)/shard_map/all_to_all | solution.py:75
  145.1 6.4 %convert_bitcast_fusion.1 = bf16[768,16,128]{0,2,1:T(8,128)(2,1)} fusion(bf16[576,768,1]{1,0,2:T(8,128)(2,1)S(1)} %reshape.156, bf16[576,32,128]{2,1,0:T(8,128)(2,1)} %bitcast.10), kind=kOutput, calls=%fused_computation.14 | convolution fusion | flops 1813512192 | bytes 8749056 | tf_op jit(solution)/shard_map/rf,rjl->fjl/dot_general | solution.py:87
  151.5 5.7 %all-to-all-start = ((bf16[64,9,32,128]{3,2,1,0:T(8,128)(2,1)}), bf16[64,9,32,128]{3,2,1,0:T(8,128)(2,1)}, u32[]{:S(2)}, u32[]{:S(2)}) async-start(bf16[64,9,32,128]{3,2,1,0:T(8,128)(2,1)} %bitcast.63), calls=%async_computation | async-start | bytes 9437184 | tf_op jit(solution)/shard_map/all_to_all | solution.py:41
  157.5 6.1 %convert_bitcast_fusion = bf16[768,16,128]{0,2,1:T(8,128)(2,1)} fusion(bf16[576,768,1]{1,0,2:T(8,128)(2,1)S(1)} %reshape.156, bf16[576,32,128]{2,1,0:T(8,128)(2,1)} %bitcast.10), kind=kOutput, calls=%fused_computation.13 | convolution fusion | flops 1813512192 | bytes 8749056 | tf_op jit(solution)/shard_map/rf,rjl->fjl/dot_general | solution.py:87
  163.8 1.1 copy.99
  165.0 7.4 %bitcast_convert_fusion = bf16[576,768]{1,0:T(8,128)(2,1)S(1)} fusion(bf16[768,32,128]{0,2,1:T(8,128)(2,1)} %bitcast.74, bf16[576,32,128]{2,1,0:T(8,128)(2,1)} %bitcast.10), kind=kOutput, calls=%fused_computation.17 | convolution fusion | flops 3624321024 | bytes 11894784 | tf_op jit(solution)/shard_map/rjl,fjl->rf/dot_general | solution.py:103
  172.4 0.4 reshape.140
  172.8 1.2 copy.107
  174.0 13.4 %reduce-scatter.3.cloned.1.call-done = bf16[768,4,128]{0,2,1:T(8,128)(2,1)} async-done(((bf16[768,16,128]{0,2,1:T(8,128)(2,1)}), bf16[768,4,128]{0,2,1:T(8,128)(2,1)}) %reduce-scatter.3.cloned.1.call-update) | async-done | bytes 786448 | tf_op jit(solution)/shard_map/reduce_scatter | solution.py:94
  187.4 43.7 %reduce-scatter.5.cloned.1.call-done = bf16[768,4,128]{0,2,1:T(8,128)(2,1)} async-done(((bf16[768,16,128]{0,2,1:T(8,128)(2,1)}), bf16[768,4,128]{0,2,1:T(8,128)(2,1)}) %reduce-scatter.5.cloned.1.call-update) | async-done | bytes 786448 | tf_op jit(solution)/shard_map/reduce_scatter | solution.py:94
  231.1 1.5 pad_maximum_fusion
  232.7 2.1 copy.108
  234.8 29.9 %all-to-all-done = bf16[64,9,32,128]{3,2,1,0:T(8,128)(2,1)} async-done(((bf16[64,9,32,128]{3,2,1,0:T(8,128)(2,1)}), bf16[64,9,32,128]{3,2,1,0:T(8,128)(2,1)}, u32[]{:S(2)}, u32[]{:S(2)}) %all-to-all-start) | async-done | bytes 4718624 | tf_op jit(solution)/shard_map/all_to_all | solution.py:41
  264.7 3.6 %gather_fusion = bf16[384,32,128]{2,1,0:T(8,128)(2,1)S(1)} fusion(bf16[576,32,128]{2,1,0:T(8,128)(2,1)} %bitcast.2, s32[1024]{0:T(1024)S(1)} %pad_clamp_fusion), kind=kCustom, calls=%fused_computation | custom fusion | bytes 6292992 | tf_op jit(solution)/shard_map/gather | solution.py:48
  268.3 4.4 %fusion.1 = (f32[48,8]{1,0:T(8,128)S(1)}, bf16[48,32,128]{2,1,0:T(8,128)(2,1)S(1)}) fusion(bf16[48,8,32,128]{3,2,1,0:T(8,128)(2,1)S(1)} %bitcast.65, f32[48,32,128]{2,1,0:T(8,128)} %copy.99, f32[48,8]{1,0:T(8,128)S(1)} %copy.89), kind=kLoop, calls=%fused_computation.5 | loop fusion | flops 7667328 | bytes 4328448 | tf_op jit(solution)/shard_map/reduce_sum | solution.py:54
  273.1 1.0 reshape.136
  274.1 0.7 copy.106
  (33 shorter events, 2.5 us)
Async XLA Ops:
  7.2 2.7 copy-start.2
  7.2 4.4 %copy-start.3 = (f32[48,8]{0,1:T(8,128)S(1)}, f32[48,8]{0,1:T(8,128)}, u32[]{:S(2)}) copy-start(f32[48,8]{0,1:T(8,128)} %param.6) | copy-start | bytes 4612
  7.2 4.5 %copy-start.1 = (bf16[48,4096]{1,0:T(8,128)(2,1)S(1)}, bf16[48,4096]{1,0:T(8,128)(2,1)}, u32[]{:S(2)}) copy-start(bf16[48,4096]{1,0:T(8,128)(2,1)} %param.9) | copy-start | bytes 1179652
  7.2 74.0 %all-gather.2.cloned.1.call-start = ((), (), s32[]{:S(2)}) async-start(), calls=%async_computation.4 | async-start | bytes 7864320 | tf_op jit(solution)/shard_map/all_gather | solution.py:33
  25.4 12.5 %copy-start = (bf16[1,1,64,9,768]{4,2,3,1,0:T(8,128)(2,1)S(1)}, bf16[1,1,64,9,768]{4,2,3,1,0:T(8,128)(2,1)}, u32[]{:S(2)}) copy-start(bf16[1,1,64,9,768]{4,2,3,1,0:T(8,128)(2,1)} %param.7) | copy-start | bytes 2654212
  25.5 119.7 %all-to-all-start.1 = ((bf16[64,9,32,128]{3,2,1,0:T(8,128)(2,1)}), bf16[64,9,32,128]{3,2,1,0:T(8,128)(2,1)}, u32[]{:S(2)}, u32[]{:S(2)}) async-start(bf16[64,9,32,128]{3,2,1,0:T(8,128)(2,1)} %bitcast.64), calls=%async_computation.1 | async-start | bytes 9437184 | tf_op jit(solution)/shard_map/all_to_all | solution.py:75
  37.8 149.7 %reduce-scatter.3.cloned.1.call-start = ((), (), s32[]{:S(2)}) async-start(), calls=%async_computation.5 | async-start | bytes 3932160 | tf_op jit(solution)/shard_map/reduce_scatter | solution.py:94
  151.5 113.2 %all-to-all-start = ((bf16[64,9,32,128]{3,2,1,0:T(8,128)(2,1)}), bf16[64,9,32,128]{3,2,1,0:T(8,128)(2,1)}, u32[]{:S(2)}, u32[]{:S(2)}) async-start(bf16[64,9,32,128]{3,2,1,0:T(8,128)(2,1)} %bitcast.63), calls=%async_computation | async-start | bytes 9437184 | tf_op jit(solution)/shard_map/all_to_all | solution.py:41
  157.2 73.9 %reduce-scatter.5.cloned.1.call-start = ((), (), s32[]{:S(2)}) async-start(), calls=%async_computation.6 | async-start | bytes 3932160 | tf_op jit(solution)/shard_map/reduce_scatter | solution.py:94
Sparse Core Ops, SparseCore 0:
  10.4 70.6 all-gather.1
  151.6 35.7 reduce-scatter.2
  190.6 40.5 reduce-scatter.4

commit v14 on v11

--- a/solution.py
+++ b/solution.py
@@ -63,7 +63,7 @@
         ),
         axis=2,
     )
-    scaled = jnp.dot(dispatch, grad_flat, precision=lax.Precision.HIGHEST).astype(jnp.bfloat16)
+    scaled = jnp.dot(dispatch, grad_flat, precision=lax.Precision.HIGH).astype(jnp.bfloat16)
     arrived = lax.all_to_all(
         scaled.reshape(expert_count, capacity, model_width // lanes, lanes),
         "expert",

time: 279 us -> 277 us (level)
  transfers between devices with their start and end apart: 5 -> 5, of which waited for: 5 -> 5; matrix products, arithmetic and copies ran while one was open for 16% -> 15% of each run, Pallas kernels for 0% -> 0%
where the time goes in v14:
time: 277 us
  waiting for transfers between devices  181 us (65%)
  matrix products  29.7 us (11%)
  local copies, waits for them, and re-layouts  24.9 us (9%)
  starting transfers between devices  18.5 us (7%)
  between operations  14 us (5%)
  other arithmetic  8.09 us (3%)
    reduce_scatter x2, waiting for transfers between devices, shards(): lax.psum_scatter(rounded_partial(partial_value).astype(jnp.bfloat16), 'dp...  57.1 us
    all_to_all x1, waiting for transfers between devices, shards(): lax.all_to_all(scaled.reshape(expert_count, capacity, model_width // lane...  47.5 us
    all_gather x1, waiting for transfers between devices, shards(): gathered_weight = lax.all_gather(local_halves, 'dp', axis=2, tiled=False)  46.9 us
    all_to_all x1, waiting for transfers between devices, shards(): lax.all_to_all(outgoing, 'expert', split_axis=0, concat_axis=0, tiled=True)  29.9 us
    unnamed x19, local copies, waits for them, and re-layouts  15.4 us
    dot_general x2, matrix products, shards(): jnp.einsum('rf,rjl->fjl', hidden_rows, arrived[:, part * half_tiles:(part...  12.5 us
    all_to_all x1, starting transfers between devices, shards(): lax.all_to_all(scaled.reshape(expert_count, capacity, model_width // lane...  12.3 us
    dot_general x1, matrix products, shards(): jnp.einsum('rjl,fjl->rf', arrived, weight_mixed, preferred_element_type=j...  7.42 us
  transfers between devices with their start and end apart: 5, of which 5 were waited for; matrix products, arithmetic and copies ran while one was open for 15% of the time, Pallas kernels for 0%

profile of v14, /device:TPU:18, one launch (start us, length us, event | category | flops | bytes accessed | tf_op | source)
XLA Modules:
  0.0 276.7 jit_solution(2959827323705562599)
XLA Ops:
  7.2 2.6 copy.91
  10.3 0.9 reduce-window.6
  11.7 0.3 reshape.137
  12.3 0.3 reshape_reshape.6
  12.6 0.4 select_reduce_fusion
  12.9 2.9 %fusion.9 = bf16[72,8,32,128]{3,1,2,0:T(8,128)(2,1)S(1)} fusion(f32[576,48]{0,1:T(8,128)S(1)} %select_reduce_fusion, bf16[48,4096]{1,0:T(8,128)(2,1)S(1)} %reshape_reshape.6), kind=kOutput, calls=%fused_computation.16 | convolution fusion | flops 681836544 | bytes 5222400 | tf_op jit(solution)/shard_map/dot_general | solution.py:66
  15.9 3.7 %copy.112 = bf16[72,8,32,128]{3,2,1,0:T(8,128)(2,1)} copy(bf16[72,8,32,128]{3,1,2,0:T(8,128)(2,1)S(1)} %fusion.9) | data formatting | bytes 9437184
  19.6 12.3 %all-to-all-start.1 = ((bf16[64,9,32,128]{3,2,1,0:T(8,128)(2,1)}), bf16[64,9,32,128]{3,2,1,0:T(8,128)(2,1)}, u32[]{:S(2)}, u32[]{:S(2)}) async-start(bf16[64,9,32,128]{3,2,1,0:T(8,128)(2,1)} %bitcast.63), calls=%async_computation.1 | async-start | bytes 9437184 | tf_op jit(solution)/shard_map/all_to_all | solution.py:67
  32.1 0.5 copy.90
  32.6 0.4 reshape.156
  33.1 1.2 reshape.131
  34.2 46.9 %all-gather.2.cloned.1.call-done = bf16[768,2,4,512]{0,3,2,1:T(8,128)(2,1)} async-done(((bf16[768,2,1,512]{0,3,2,1:T(8,128)(2,1)}), bf16[768,2,4,512]{0,3,2,1:T(8,128)(2,1)}) %all-gather.2.cloned.1.call-update) | async-done | bytes 6291472 | tf_op jit(solution)/shard_map/all_gather | solution.py:33
  81.2 6.9 %fusion.8 = bf16[72,8,32,128]{3,1,2,0:T(8,128)(2,1)S(1)} fusion(bf16[576,768]{1,0:T(8,128)(2,1)} %reshape.131, bf16[768,4096]{0,1:T(8,128)(2,1)} %bitcast.72), kind=kOutput, calls=%fused_computation.15 | convolution fusion | flops 3626237952 | bytes 11894784 | tf_op jit(solution)/shard_map/dot_general | solution.py:37
  88.1 3.7 %copy.111 = bf16[72,8,32,128]{3,2,1,0:T(8,128)(2,1)} copy(bf16[72,8,32,128]{3,1,2,0:T(8,128)(2,1)S(1)} %fusion.8) | data formatting | bytes 9437184
  91.8 47.5 %all-to-all-done.1 = bf16[64,9,32,128]{3,2,1,0:T(8,128)(2,1)} async-done(((bf16[64,9,32,128]{3,2,1,0:T(8,128)(2,1)}), bf16[64,9,32,128]{3,2,1,0:T(8,128)(2,1)}, u32[]{:S(2)}, u32[]{:S(2)}) %all-to-all-start.1) | async-done | bytes 4718624 | tf_op jit(solution)/shard_map/all_to_all | solution.py:67
  139.2 6.4 %convert_bitcast_fusion.1 = bf16[768,16,128]{0,2,1:T(8,128)(2,1)} fusion(bf16[576,768,1]{1,0,2:T(8,128)(2,1)S(1)} %reshape.156, bf16[576,32,128]{2,1,0:T(8,128)(2,1)} %bitcast.10), kind=kOutput, calls=%fused_computation.14 | convolution fusion | flops 1813512192 | bytes 8749056 | tf_op jit(solution)/shard_map/rf,rjl->fjl/dot_general | solution.py:79
  145.6 5.7 %all-to-all-start = ((bf16[64,9,32,128]{3,2,1,0:T(8,128)(2,1)}), bf16[64,9,32,128]{3,2,1,0:T(8,128)(2,1)}, u32[]{:S(2)}, u32[]{:S(2)}) async-start(bf16[64,9,32,128]{3,2,1,0:T(8,128)(2,1)} %bitcast.62), calls=%async_computation | async-start | bytes 9437184 | tf_op jit(solution)/shard_map/all_to_all | solution.py:41
  151.3 0.3 reduce-scatter.5.cloned.1.call-start
  151.6 6.1 %convert_bitcast_fusion = bf16[768,16,128]{0,2,1:T(8,128)(2,1)} fusion(bf16[576,768,1]{1,0,2:T(8,128)(2,1)S(1)} %reshape.156, bf16[576,32,128]{2,1,0:T(8,128)(2,1)} %bitcast.10), kind=kOutput, calls=%fused_computation.13 | convolution fusion | flops 1813512192 | bytes 8749056 | tf_op jit(solution)/shard_map/rf,rjl->fjl/dot_general | solution.py:79
  157.9 1.1 copy.99
  159.1 7.4 %bitcast_convert_fusion = bf16[576,768]{1,0:T(8,128)(2,1)S(1)} fusion(bf16[768,32,128]{0,2,1:T(8,128)(2,1)} %bitcast.73, bf16[576,32,128]{2,1,0:T(8,128)(2,1)} %bitcast.10), kind=kOutput, calls=%fused_computation.17 | convolution fusion | flops 3624321024 | bytes 11894784 | tf_op jit(solution)/shard_map/rjl,fjl->rf/dot_general | solution.py:95
  166.5 0.4 reshape.140
  166.9 1.2 copy.107
  168.1 13.4 %reduce-scatter.3.cloned.1.call-done = bf16[768,4,128]{0,2,1:T(8,128)(2,1)} async-done(((bf16[768,16,128]{0,2,1:T(8,128)(2,1)}), bf16[768,4,128]{0,2,1:T(8,128)(2,1)}) %reduce-scatter.3.cloned.1.call-update) | async-done | bytes 786448 | tf_op jit(solution)/shard_map/reduce_scatter | solution.py:86
  181.5 43.7 %reduce-scatter.5.cloned.1.call-done = bf16[768,4,128]{0,2,1:T(8,128)(2,1)} async-done(((bf16[768,16,128]{0,2,1:T(8,128)(2,1)}), bf16[768,4,128]{0,2,1:T(8,128)(2,1)}) %reduce-scatter.5.cloned.1.call-update) | async-done | bytes 786448 | tf_op jit(solution)/shard_map/reduce_scatter | solution.py:86
  225.2 1.5 pad_maximum_fusion
  226.8 2.1 copy.108
  228.9 29.9 %all-to-all-done = bf16[64,9,32,128]{3,2,1,0:T(8,128)(2,1)} async-done(((bf16[64,9,32,128]{3,2,1,0:T(8,128)(2,1)}), bf16[64,9,32,128]{3,2,1,0:T(8,128)(2,1)}, u32[]{:S(2)}, u32[]{:S(2)}) %all-to-all-start) | async-done | bytes 4718624 | tf_op jit(solution)/shard_map/all_to_all | solution.py:41
  258.8 3.6 %gather_fusion = bf16[384,32,128]{2,1,0:T(8,128)(2,1)S(1)} fusion(bf16[576,32,128]{2,1,0:T(8,128)(2,1)} %bitcast.2, s32[1024]{0:T(1024)S(1)} %pad_clamp_fusion), kind=kCustom, calls=%fused_computation | custom fusion | bytes 6292992 | tf_op jit(solution)/shard_map/gather | solution.py:48
  262.4 5.0 %fusion.1 = (f32[48,8]{1,0:T(8,128)}, bf16[48,32,128]{2,1,0:T(8,128)(2,1)S(1)}) fusion(bf16[48,8,32,128]{3,2,1,0:T(8,128)(2,1)S(1)} %bitcast.64, f32[48,32,128]{2,1,0:T(8,128)} %copy.99, f32[48,8]{1,0:T(8,128)} %copy-done.2), kind=kLoop, calls=%fused_computation.4 | loop fusion | flops 7667328 | bytes 4328448 | tf_op jit(solution)/shard_map/reduce_sum | solution.py:54
  267.4 1.4 copy.106
  269.1 1.0 reshape.136
  (33 shorter events, 2.0 us)
Async XLA Ops:
  7.2 2.7 copy-start.3
  7.2 3.0 %copy-start.4 = (f32[48,8]{0,1:T(8,128)S(1)}, f32[48,8]{0,1:T(8,128)}, u32[]{:S(2)}) copy-start(f32[48,8]{0,1:T(8,128)} %param.6) | copy-start | bytes 4612
  7.2 4.5 %copy-start.1 = (bf16[48,4096]{1,0:T(8,128)(2,1)S(1)}, bf16[48,4096]{1,0:T(8,128)(2,1)}, u32[]{:S(2)}) copy-start(bf16[48,4096]{1,0:T(8,128)(2,1)} %param.9) | copy-start | bytes 1179652
  7.2 74.0 %all-gather.2.cloned.1.call-start = ((), (), s32[]{:S(2)}) async-start(), calls=%async_computation.4 | async-start | bytes 7864320 | tf_op jit(solution)/shard_map/all_gather | solution.py:33
  10.3 9.3 %copy-start.2 = (f32[48,8]{1,0:T(8,128)}, f32[48,8]{1,0:T(8,128)S(1)}, u32[]{:S(2)}) copy-start(f32[48,8]{1,0:T(8,128)S(1)} %copy.89) | copy-start | bytes 4612
  19.6 12.5 %copy-start = (bf16[1,1,64,9,768]{4,2,3,1,0:T(8,128)(2,1)S(1)}, bf16[1,1,64,9,768]{4,2,3,1,0:T(8,128)(2,1)}, u32[]{:S(2)}) copy-start(bf16[1,1,64,9,768]{4,2,3,1,0:T(8,128)(2,1)} %param.7) | copy-start | bytes 2654212
  19.6 119.7 %all-to-all-start.1 = ((bf16[64,9,32,128]{3,2,1,0:T(8,128)(2,1)}), bf16[64,9,32,128]{3,2,1,0:T(8,128)(2,1)}, u32[]{:S(2)}, u32[]{:S(2)}) async-start(bf16[64,9,32,128]{3,2,1,0:T(8,128)(2,1)} %bitcast.63), calls=%async_computation.1 | async-start | bytes 9437184 | tf_op jit(solution)/shard_map/all_to_all | solution.py:67
  31.8 149.7 %reduce-scatter.3.cloned.1.call-start = ((), (), s32[]{:S(2)}) async-start(), calls=%async_computation.5 | async-start | bytes 3932160 | tf_op jit(solution)/shard_map/reduce_scatter | solution.py:86
  145.6 113.2 %all-to-all-start = ((bf16[64,9,32,128]{3,2,1,0:T(8,128)(2,1)}), bf16[64,9,32,128]{3,2,1,0:T(8,128)(2,1)}, u32[]{:S(2)}, u32[]{:S(2)}) async-start(bf16[64,9,32,128]{3,2,1,0:T(8,128)(2,1)} %bitcast.62), calls=%async_computation | async-start | bytes 9437184 | tf_op jit(solution)/shard_map/all_to_all | solution.py:41
  151.3 73.9 %reduce-scatter.5.cloned.1.call-start = ((), (), s32[]{:S(2)}) async-start(), calls=%async_computation.6 | async-start | bytes 3932160 | tf_op jit(solution)/shard_map/reduce_scatter | solution.py:86
Sparse Core Ops, SparseCore 0:
  10.4 70.7 all-gather.1
  145.7 35.7 reduce-scatter.2
  184.7 40.5 reduce-scatter.4

commit v15 on v14

--- a/solution.py
+++ b/solution.py
@@ -63,7 +63,7 @@
         ),
         axis=2,
     )
-    scaled = jnp.dot(dispatch, grad_flat, precision=lax.Precision.HIGH).astype(jnp.bfloat16)
+    scaled = jnp.dot(dispatch, grad_flat, precision=lax.Precision.DEFAULT).astype(jnp.bfloat16)
     arrived = lax.all_to_all(
         scaled.reshape(expert_count, capacity, model_width // lanes, lanes),
         "expert",

time: 277 us -> 276 us (level)
  no operation moved by 1% of the time
where the time goes in v15:
time: 276 us; the launch traced here: 275 us
  waiting for transfers between devices  181 us (66%)
  matrix products  28.2 us (10%)
  local copies, waits for them, and re-layouts  24.9 us (9%)
  starting transfers between devices  18.5 us (7%)
  between operations  14 us (5%)
  other arithmetic  8.1 us (3%)
    reduce_scatter x2, waiting for transfers between devices, shards(): lax.psum_scatter(rounded_partial(partial_value).astype(jnp.bfloat16), 'dp...  57.1 us
    all_gather x1, waiting for transfers between devices, shards(): gathered_weight = lax.all_gather(local_halves, 'dp', axis=2, tiled=False)  48.4 us
    all_to_all x1, waiting for transfers between devices, shards(): lax.all_to_all(scaled.reshape(expert_count, capacity, model_width // lane...  45.9 us
    all_to_all x1, waiting for transfers between devices, shards(): lax.all_to_all(outgoing, 'expert', split_axis=0, concat_axis=0, tiled=True)  29.9 us
    unnamed x19, local copies, waits for them, and re-layouts  15.4 us
    dot_general x2, matrix products, shards(): jnp.einsum('rf,rjl->fjl', hidden_rows, arrived[:, part * half_tiles:(part...  12.5 us
    all_to_all x1, starting transfers between devices, shards(): lax.all_to_all(scaled.reshape(expert_count, capacity, model_width // lane...  12.3 us
    dot_general x1, matrix products, shards(): jnp.einsum('rjl,fjl->rf', arrived, weight_mixed, preferred_element_type=j...  7.42 us
  transfers between devices with their start and end apart: 5, of which 5 were waited for; matrix products, arithmetic and copies ran while one was open for 15% of the time, Pallas kernels for 0%

profile of v15, /device:TPU:18, one launch (start us, length us, event | category | flops | bytes accessed | tf_op | source)
XLA Modules:
  0.0 275.2 jit_solution(3108299823382969103)
XLA Ops:
  7.2 2.6 copy.91
  10.3 0.9 reduce-window.6
  11.7 0.3 reshape.137
  12.3 0.3 reshape_reshape.6
  12.6 0.4 select_reduce_fusion
  13.0 1.4 fusion.9
  14.4 3.7 %copy.112 = bf16[72,8,32,128]{3,2,1,0:T(8,128)(2,1)} copy(bf16[72,8,32,128]{3,1,2,0:T(8,128)(2,1)S(1)} %fusion.9) | data formatting | bytes 9437184
  18.0 12.3 %all-to-all-start.1 = ((bf16[64,9,32,128]{3,2,1,0:T(8,128)(2,1)}), bf16[64,9,32,128]{3,2,1,0:T(8,128)(2,1)}, u32[]{:S(2)}, u32[]{:S(2)}) async-start(bf16[64,9,32,128]{3,2,1,0:T(8,128)(2,1)} %bitcast.63), calls=%async_computation.1 | async-start | bytes 9437184 | tf_op jit(solution)/shard_map/all_to_all | solution.py:67
  30.6 0.5 copy.90
  31.1 0.4 reshape.156
  31.6 1.2 reshape.131
  32.7 48.4 %all-gather.2.cloned.1.call-done = bf16[768,2,4,512]{0,3,2,1:T(8,128)(2,1)} async-done(((bf16[768,2,1,512]{0,3,2,1:T(8,128)(2,1)}), bf16[768,2,4,512]{0,3,2,1:T(8,128)(2,1)}) %all-gather.2.cloned.1.call-update) | async-done | bytes 6291472 | tf_op jit(solution)/shard_map/all_gather | solution.py:33
  81.2 6.9 %fusion.8 = bf16[72,8,32,128]{3,1,2,0:T(8,128)(2,1)S(1)} fusion(bf16[576,768]{1,0:T(8,128)(2,1)} %reshape.131, bf16[768,4096]{0,1:T(8,128)(2,1)} %bitcast.72), kind=kOutput, calls=%fused_computation.15 | convolution fusion | flops 3626237952 | bytes 11894784 | tf_op jit(solution)/shard_map/dot_general | solution.py:37
  88.1 3.7 %copy.111 = bf16[72,8,32,128]{3,2,1,0:T(8,128)(2,1)} copy(bf16[72,8,32,128]{3,1,2,0:T(8,128)(2,1)S(1)} %fusion.8) | data formatting | bytes 9437184
  91.8 45.9 %all-to-all-done.1 = bf16[64,9,32,128]{3,2,1,0:T(8,128)(2,1)} async-done(((bf16[64,9,32,128]{3,2,1,0:T(8,128)(2,1)}), bf16[64,9,32,128]{3,2,1,0:T(8,128)(2,1)}, u32[]{:S(2)}, u32[]{:S(2)}) %all-to-all-start.1) | async-done | bytes 4718624 | tf_op jit(solution)/shard_map/all_to_all | solution.py:67
  137.7 6.4 %convert_bitcast_fusion.1 = bf16[768,16,128]{0,2,1:T(8,128)(2,1)} fusion(bf16[576,768,1]{1,0,2:T(8,128)(2,1)S(1)} %reshape.156, bf16[576,32,128]{2,1,0:T(8,128)(2,1)} %bitcast.10), kind=kOutput, calls=%fused_computation.14 | convolution fusion | flops 1813512192 | bytes 8749056 | tf_op jit(solution)/shard_map/rf,rjl->fjl/dot_general | solution.py:79
  144.1 5.7 %all-to-all-start = ((bf16[64,9,32,128]{3,2,1,0:T(8,128)(2,1)}), bf16[64,9,32,128]{3,2,1,0:T(8,128)(2,1)}, u32[]{:S(2)}, u32[]{:S(2)}) async-start(bf16[64,9,32,128]{3,2,1,0:T(8,128)(2,1)} %bitcast.62), calls=%async_computation | async-start | bytes 9437184 | tf_op jit(solution)/shard_map/all_to_all | solution.py:41
  149.8 0.3 reduce-scatter.5.cloned.1.call-start
  150.1 6.1 %convert_bitcast_fusion = bf16[768,16,128]{0,2,1:T(8,128)(2,1)} fusion(bf16[576,768,1]{1,0,2:T(8,128)(2,1)S(1)} %reshape.156, bf16[576,32,128]{2,1,0:T(8,128)(2,1)} %bitcast.10), kind=kOutput, calls=%fused_computation.13 | convolution fusion | flops 1813512192 | bytes 8749056 | tf_op jit(solution)/shard_map/rf,rjl->fjl/dot_general | solution.py:79
  156.4 1.1 copy.99
  157.6 7.4 %bitcast_convert_fusion = bf16[576,768]{1,0:T(8,128)(2,1)S(1)} fusion(bf16[768,32,128]{0,2,1:T(8,128)(2,1)} %bitcast.73, bf16[576,32,128]{2,1,0:T(8,128)(2,1)} %bitcast.10), kind=kOutput, calls=%fused_computation.17 | convolution fusion | flops 3624321024 | bytes 11894784 | tf_op jit(solution)/shard_map/rjl,fjl->rf/dot_general | solution.py:95
  165.0 0.4 reshape.140
  165.4 1.2 copy.107
  166.6 13.4 %reduce-scatter.3.cloned.1.call-done = bf16[768,4,128]{0,2,1:T(8,128)(2,1)} async-done(((bf16[768,16,128]{0,2,1:T(8,128)(2,1)}), bf16[768,4,128]{0,2,1:T(8,128)(2,1)}) %reduce-scatter.3.cloned.1.call-update) | async-done | bytes 786448 | tf_op jit(solution)/shard_map/reduce_scatter | solution.py:86
  180.0 43.7 %reduce-scatter.5.cloned.1.call-done = bf16[768,4,128]{0,2,1:T(8,128)(2,1)} async-done(((bf16[768,16,128]{0,2,1:T(8,128)(2,1)}), bf16[768,4,128]{0,2,1:T(8,128)(2,1)}) %reduce-scatter.5.cloned.1.call-update) | async-done | bytes 786448 | tf_op jit(solution)/shard_map/reduce_scatter | solution.py:86
  223.7 1.5 pad_maximum_fusion
  225.3 2.1 copy.108
  227.4 29.9 %all-to-all-done = bf16[64,9,32,128]{3,2,1,0:T(8,128)(2,1)} async-done(((bf16[64,9,32,128]{3,2,1,0:T(8,128)(2,1)}), bf16[64,9,32,128]{3,2,1,0:T(8,128)(2,1)}, u32[]{:S(2)}, u32[]{:S(2)}) %all-to-all-start) | async-done | bytes 4718624 | tf_op jit(solution)/shard_map/all_to_all | solution.py:41
  257.3 3.6 %gather_fusion = bf16[384,32,128]{2,1,0:T(8,128)(2,1)S(1)} fusion(bf16[576,32,128]{2,1,0:T(8,128)(2,1)} %bitcast.2, s32[1024]{0:T(1024)S(1)} %pad_clamp_fusion), kind=kCustom, calls=%fused_computation | custom fusion | bytes 6292992 | tf_op jit(solution)/shard_map/gather | solution.py:48
  260.9 5.0 %fusion.1 = (f32[48,8]{1,0:T(8,128)}, bf16[48,32,128]{2,1,0:T(8,128)(2,1)S(1)}) fusion(bf16[48,8,32,128]{3,2,1,0:T(8,128)(2,1)S(1)} %bitcast.64, f32[48,32,128]{2,1,0:T(8,128)} %copy.99, f32[48,8]{1,0:T(8,128)} %copy-done.2), kind=kLoop, calls=%fused_computation.4 | loop fusion | flops 7667328 | bytes 4328448 | tf_op jit(solution)/shard_map/reduce_sum | solution.py:54
  265.9 1.4 copy.106
  267.6 1.0 reshape.136
  (33 shorter events, 2.0 us)
Async XLA Ops:
  7.2 2.7 copy-start.3
  7.2 3.0 %copy-start.4 = (f32[48,8]{0,1:T(8,128)S(1)}, f32[48,8]{0,1:T(8,128)}, u32[]{:S(2)}) copy-start(f32[48,8]{0,1:T(8,128)} %param.6) | copy-start | bytes 4612
  7.2 4.5 %copy-start.1 = (bf16[48,4096]{1,0:T(8,128)(2,1)S(1)}, bf16[48,4096]{1,0:T(8,128)(2,1)}, u32[]{:S(2)}) copy-start(bf16[48,4096]{1,0:T(8,128)(2,1)} %param.9) | copy-start | bytes 1179652
  7.2 74.0 %all-gather.2.cloned.1.call-start = ((), (), s32[]{:S(2)}) async-start(), calls=%async_computation.4 | async-start | bytes 7864320 | tf_op jit(solution)/shard_map/all_gather | solution.py:33
  10.3 7.8 %copy-start.2 = (f32[48,8]{1,0:T(8,128)}, f32[48,8]{1,0:T(8,128)S(1)}, u32[]{:S(2)}) copy-start(f32[48,8]{1,0:T(8,128)S(1)} %copy.89) | copy-start | bytes 4612
  18.0 12.5 %copy-start = (bf16[1,1,64,9,768]{4,2,3,1,0:T(8,128)(2,1)S(1)}, bf16[1,1,64,9,768]{4,2,3,1,0:T(8,128)(2,1)}, u32[]{:S(2)}) copy-start(bf16[1,1,64,9,768]{4,2,3,1,0:T(8,128)(2,1)} %param.7) | copy-start | bytes 2654212
  18.0 119.7 %all-to-all-start.1 = ((bf16[64,9,32,128]{3,2,1,0:T(8,128)(2,1)}), bf16[64,9,32,128]{3,2,1,0:T(8,128)(2,1)}, u32[]{:S(2)}, u32[]{:S(2)}) async-start(bf16[64,9,32,128]{3,2,1,0:T(8,128)(2,1)} %bitcast.63), calls=%async_computation.1 | async-start | bytes 9437184 | tf_op jit(solution)/shard_map/all_to_all | solution.py:67
  30.3 149.7 %reduce-scatter.3.cloned.1.call-start = ((), (), s32[]{:S(2)}) async-start(), calls=%async_computation.5 | async-start | bytes 3932160 | tf_op jit(solution)/shard_map/reduce_scatter | solution.py:86
  144.1 113.2 %all-to-all-start = ((bf16[64,9,32,128]{3,2,1,0:T(8,128)(2,1)}), bf16[64,9,32,128]{3,2,1,0:T(8,128)(2,1)}, u32[]{:S(2)}, u32[]{:S(2)}) async-start(bf16[64,9,32,128]{3,2,1,0:T(8,128)(2,1)} %bitcast.62), calls=%async_computation | async-start | bytes 9437184 | tf_op jit(solution)/shard_map/all_to_all | solution.py:41
  149.8 73.9 %reduce-scatter.5.cloned.1.call-start = ((), (), s32[]{:S(2)}) async-start(), calls=%async_computation.6 | async-start | bytes 3932160 | tf_op jit(solution)/shard_map/reduce_scatter | solution.py:86
Sparse Core Ops, SparseCore 0:
  10.4 70.7 all-gather.1
  144.2 35.7 reduce-scatter.2
  183.2 40.5 reduce-scatter.4
